TPU v7x, 32 devices: a whole 2x2x4 slice. The times are simulated.
32 devices in a mesh: media: 8 (over z, x), keys: 4 (over y, core).
Axes of the slice: x: 2, y: 2, z: 4, core: 2. Of those that a mesh axis runs over, the one named last changes fastest.
Arguments:
- latents: float32 [48, 64, 1024], P('media', 'keys'), may hold values from -6 to 6
- patches: bfloat16 [48, 2048, 1024], P('media', 'keys'), may hold values from -6 to 6
- frame_counts: int32 [48], P('media'), may hold values from 1 to 8
- time_embedding: float32 [8, 1024], replicated, may hold values from -6 to 6
- media_gain: float32 [1024], replicated, may hold values from 0.5 to 1.5
- media_bias: float32 [1024], replicated, may hold values from -3 to 3
- latent_gain: float32 [1024], replicated, may hold values from 0.5 to 1.5
- latent_bias: float32 [1024], replicated, may hold values from -3 to 3
- ff_gain: float32 [1024], replicated, may hold values from 0.5 to 1.5
- ff_bias: float32 [1024], replicated, may hold values from -3 to 3
- query_weight: bfloat16 [1024, 512], replicated, may hold values from -0.1875 to 0.1875
- key_weight: bfloat16 [1024, 512], replicated, may hold values from -0.1875 to 0.1875
- value_weight: bfloat16 [1024, 512], replicated, may hold values from -0.1875 to 0.1875
- out_weight: bfloat16 [512, 1024], replicated, may hold values from -4 to 4
- up_weight: bfloat16 [1024, 4096], replicated, may hold values from -0.1875 to 0.1875
- down_weight: bfloat16 [4096, 1024], replicated, may hold values from -0.09375 to 0.09375
- cotangent: float32 [48, 64, 1024], P('media', 'keys'), may hold values from -6 to 6
Outputs:
- resampled: float32 [48, 64, 1024], P('media', 'keys')
- patches_grad: bfloat16 [48, 2048, 1024], P('media', 'keys')
- latents_grad: float32 [48, 64, 1024], P('media', 'keys')
- time_grad: float32 [8, 1024], replicated
- media_gain_grad: float32 [1024], replicated
- media_bias_grad: float32 [1024], replicated
- latent_gain_grad: float32 [1024], replicated
- latent_bias_grad: float32 [1024], replicated
- ff_gain_grad: float32 [1024], replicated
- ff_bias_grad: float32 [1024], replicated
- query_weight_grad: float32 [1024, 512], P('media', 'keys')
- key_weight_grad: float32 [1024, 512], P('media', 'keys')
- value_weight_grad: float32 [1024, 512], P('media', 'keys')
- out_weight_grad: float32 [512, 1024], P('media', 'keys')
- up_weight_grad: float32 [1024, 4096], P('media', 'keys')
- down_weight_grad: float32 [4096, 1024], P('media', 'keys')
Inputs may be any that keep to these rules, and one draw needn't show every extreme that they name: `frame_counts`: the number of frames of each medium; patch rows of its frame slots at or after this number still hold values, but their keys are invisible to the latents.
All inputs are finite; a program needn't handle non-finite values.
Results may differ from a plain program's by a relative error of at most 0.02.
Values may be sent and summed in bfloat16 or wider, within the bound.
No kernel may reach another device: no remote copies, remote signals or barrier semaphores. Data moves between devices by JAX's collectives and lax.ppermute only.
A program may use at most 192 MiB of HBM per device.

v0:
```python
import jax
import jax.numpy as jnp
from jax import lax
from jax.sharding import PartitionSpec as P

HEAD = 64
PATCH = 256
FRAMES = 8


EPS = 1e-05
NEG = -1e30


def layer_norm(values, gain, bias):
    centre = jnp.mean(values, -1, keepdims=True)
    shifted = values - centre
    spread = jnp.mean(shifted * shifted, -1, keepdims=True)
    return shifted * lax.rsqrt(spread + EPS) * gain + bias


def exact_gelu(values):
    return jax.nn.gelu(values, approximate=False)


def split_heads(values):
    return values.reshape(values.shape[0], values.shape[1], values.shape[2] // HEAD, HEAD)


def join_heads(values):
    return values.reshape(values.shape[0], values.shape[1], values.shape[2] * values.shape[3])


def project(left, right):
    return jnp.dot(left, right, preferred_element_type=jnp.float32)


def project_back(left, right):
    return jnp.einsum("mre,de->mrd", left, right, preferred_element_type=jnp.float32)


def weight_term(left, right):
    return jnp.einsum("mrd,mre->de", left, right, preferred_element_type=jnp.float32)


def shards(
    latents,
    patches,
    frame_counts,
    time_embedding,
    media_gain,
    media_bias,
    latent_gain,
    latent_bias,
    ff_gain,
    ff_bias,
    query_weight,
    key_weight,
    value_weight,
    out_weight,
    up_weight,
    down_weight,
    cotangent,
):
    media_dev, own_rows, features = latents.shape
    key_rows = patches.shape[1]
    key_index = lax.axis_index("keys")
    frames_dev = key_rows // PATCH
    score_scale = HEAD ** (-0.5)
    first_frame = key_index * frames_dev
    own_start = key_index * own_rows
    frame_ids = first_frame + jnp.arange(key_rows, dtype=jnp.int32) // PATCH
    visible = (frame_ids[None, :] < frame_counts[:, None])[:, None, None, :]
    time_rows = lax.dynamic_slice_in_dim(time_embedding, first_frame, frames_dev, 0)
    framed = (
        patches.astype(jnp.float32).reshape(media_dev, frames_dev, PATCH, features)
        + time_rows[None, :, None, :]
    )
    framed = framed.reshape(media_dev, key_rows, features)
    media_low = layer_norm(framed, media_gain, media_bias).astype(jnp.bfloat16)
    lat_low = layer_norm(latents, latent_gain, latent_bias).astype(jnp.bfloat16)
    lat_all = lax.all_gather(lat_low, "keys", axis=1, tiled=True)
    queries = split_heads(project(lat_all, query_weight).astype(jnp.bfloat16))
    patch_keys = split_heads(project(media_low, key_weight).astype(jnp.bfloat16))
    patch_values = split_heads(project(media_low, value_weight).astype(jnp.bfloat16))
    latent_keys = split_heads(project(lat_all, key_weight).astype(jnp.bfloat16))
    latent_values = split_heads(project(lat_all, value_weight).astype(jnp.bfloat16))
    patch_scores = (
        jnp.einsum("mqhd,mkhd->mhqk", queries, patch_keys, preferred_element_type=jnp.float32)
        * score_scale
    )
    patch_scores = jnp.where(visible, patch_scores, NEG)
    local_top = jnp.max(patch_scores, -1)
    local_total = jnp.sum(jnp.where(visible, jnp.exp(patch_scores - local_top[..., None]), 0.0), -1)
    patch_top = lax.pmax(local_top, "keys")
    patch_total = lax.psum(local_total * jnp.exp(local_top - patch_top), "keys")
    lat_scores = (
        jnp.einsum("mqhd,mkhd->mhqk", queries, latent_keys, preferred_element_type=jnp.float32)
        * score_scale
    )
    row_top = jnp.maximum(patch_top, jnp.max(lat_scores, -1))
    row_total = patch_total * jnp.exp(patch_top - row_top) + jnp.sum(
        jnp.exp(lat_scores - row_top[..., None]), -1
    )
    patch_probs = (
        jnp.where(visible, jnp.exp(patch_scores - row_top[..., None]), 0.0) / row_total[..., None]
    )
    lat_probs = jnp.exp(lat_scores - row_top[..., None]) / row_total[..., None]
    patch_probs_low = patch_probs.astype(jnp.bfloat16)
    lat_probs_low = lat_probs.astype(jnp.bfloat16)
    patch_share = join_heads(
        jnp.einsum(
            "mhqk,mkhd->mqhd", patch_probs_low, patch_values, preferred_element_type=jnp.float32
        )
    )
    own_lat_probs = lax.dynamic_slice_in_dim(lat_probs_low, own_start, own_rows, 2)
    lat_share = join_heads(
        jnp.einsum(
            "mhqk,mkhd->mqhd", own_lat_probs, latent_values, preferred_element_type=jnp.float32
        )
    )
    attended = (
        lax.psum_scatter(
            patch_share.astype(jnp.bfloat16), "keys", scatter_dimension=1, tiled=True
        ).astype(jnp.float32)
        + lat_share
    )
    attended_low = attended.astype(jnp.bfloat16)
    middle = latents + project(attended_low, out_weight)
    ff_low = layer_norm(middle, ff_gain, ff_bias).astype(jnp.bfloat16)
    hidden = project(ff_low, up_weight)
    act_low = exact_gelu(hidden).astype(jnp.bfloat16)
    resampled = middle + project(act_low, down_weight)
    out_low = cotangent.astype(jnp.bfloat16)
    down_grad = weight_term(act_low, out_low)
    act_grad = project_back(out_low, down_weight)
    gelu_back = jax.vjp(exact_gelu, hidden)[1]
    hidden_low = gelu_back(act_grad)[0].astype(jnp.bfloat16)
    up_grad = weight_term(ff_low, hidden_low)
    ff_input_grad = project_back(hidden_low, up_weight)
    ff_back = jax.vjp(layer_norm, middle, ff_gain, ff_bias)[1]
    middle_norm_grad, ff_gain_grad, ff_bias_grad = ff_back(ff_input_grad)
    middle_grad = cotangent + middle_norm_grad
    branch_low = middle_grad.astype(jnp.bfloat16)
    out_grad_weight = weight_term(attended_low, branch_low)
    attended_grad = project_back(branch_low, out_weight).astype(jnp.bfloat16)
    grad_all = split_heads(lax.all_gather(attended_grad, "keys", axis=1, tiled=True))
    patch_prob_grad = jnp.einsum(
        "mqhd,mkhd->mhqk", grad_all, patch_values, preferred_element_type=jnp.float32
    )
    lat_prob_grad = jnp.einsum(
        "mqhd,mkhd->mhqk", grad_all, latent_values, preferred_element_type=jnp.float32
    )
    patch_delta = jnp.sum(patch_probs * patch_prob_grad, -1)
    delta = lax.psum(patch_delta, "keys") + jnp.sum(lat_probs * lat_prob_grad, -1)
    patch_score_grad = (patch_probs * (patch_prob_grad - delta[..., None])).astype(jnp.bfloat16)
    lat_score_grad = (lat_probs * (lat_prob_grad - delta[..., None])).astype(jnp.bfloat16)
    query_share = (
        join_heads(
            jnp.einsum(
                "mhqk,mkhd->mqhd", patch_score_grad, patch_keys, preferred_element_type=jnp.float32
            )
        )
        * score_scale
    )
    own_query_rows = lax.dynamic_slice_in_dim(lat_score_grad, own_start, own_rows, 2)
    query_local = (
        join_heads(
            jnp.einsum(
                "mhqk,mkhd->mqhd", own_query_rows, latent_keys, preferred_element_type=jnp.float32
            )
        )
        * score_scale
    )
    query_grad = (
        lax.psum_scatter(
            query_share.astype(jnp.bfloat16), "keys", scatter_dimension=1, tiled=True
        ).astype(jnp.float32)
        + query_local
    ).astype(jnp.bfloat16)
    patch_key_grad = join_heads(
        jnp.einsum("mhqk,mqhd->mkhd", patch_score_grad, queries, preferred_element_type=jnp.float32)
        * score_scale
    ).astype(jnp.bfloat16)
    patch_value_grad = join_heads(
        jnp.einsum("mhqk,mqhd->mkhd", patch_probs_low, grad_all, preferred_element_type=jnp.float32)
    ).astype(jnp.bfloat16)
    own_key_cols = lax.dynamic_slice_in_dim(lat_score_grad, own_start, own_rows, 3)
    own_value_cols = lax.dynamic_slice_in_dim(lat_probs_low, own_start, own_rows, 3)
    lat_key_grad = join_heads(
        jnp.einsum("mhqk,mqhd->mkhd", own_key_cols, queries, preferred_element_type=jnp.float32)
        * score_scale
    ).astype(jnp.bfloat16)
    lat_value_grad = join_heads(
        jnp.einsum("mhqk,mqhd->mkhd", own_value_cols, grad_all, preferred_element_type=jnp.float32)
    ).astype(jnp.bfloat16)
    query_grad_weight = weight_term(lat_low, query_grad)
    key_grad_weight = weight_term(media_low, patch_key_grad) + weight_term(lat_low, lat_key_grad)
    value_grad_weight = weight_term(media_low, patch_value_grad) + weight_term(
        lat_low, lat_value_grad
    )
    media_norm_grad = project_back(patch_key_grad, key_weight) + project_back(
        patch_value_grad, value_weight
    )
    media_back = jax.vjp(layer_norm, framed, media_gain, media_bias)[1]
    framed_grad, media_gain_grad, media_bias_grad = media_back(media_norm_grad)
    patches_grad = framed_grad.astype(jnp.bfloat16)
    time_local = jnp.sum(framed_grad.reshape(media_dev, frames_dev, PATCH, features), axis=(0, 2))
    time_slots = lax.dynamic_update_slice_in_dim(
        jnp.zeros((FRAMES, features), jnp.float32), time_local, first_frame, 0
    )
    lat_norm_grad = (
        project_back(query_grad, query_weight)
        + project_back(lat_key_grad, key_weight)
        + project_back(lat_value_grad, value_weight)
    )
    lat_back = jax.vjp(layer_norm, latents, latent_gain, latent_bias)[1]
    lat_input_grad, latent_gain_grad, latent_bias_grad = lat_back(lat_norm_grad)
    latents_grad = middle_grad + lat_input_grad
    weight_grads = (
        query_grad_weight,
        key_grad_weight,
        value_grad_weight,
        out_grad_weight,
        up_grad,
        down_grad,
    )
    reduced = (
        lax.psum_scatter(
            weight_grads[0].astype(jnp.bfloat16), "media", scatter_dimension=0, tiled=True
        ).astype(jnp.float32),
        lax.psum_scatter(
            weight_grads[1].astype(jnp.bfloat16), "media", scatter_dimension=0, tiled=True
        ).astype(jnp.float32),
        lax.psum_scatter(
            weight_grads[2].astype(jnp.bfloat16), "media", scatter_dimension=0, tiled=True
        ).astype(jnp.float32),
        lax.psum_scatter(
            weight_grads[3].astype(jnp.bfloat16), "media", scatter_dimension=0, tiled=True
        ).astype(jnp.float32),
        lax.psum_scatter(
            weight_grads[4].astype(jnp.bfloat16), "media", scatter_dimension=0, tiled=True
        ).astype(jnp.float32),
        lax.psum_scatter(
            weight_grads[5].astype(jnp.bfloat16), "media", scatter_dimension=0, tiled=True
        ).astype(jnp.float32),
    )
    reduced = (
        lax.psum_scatter(
            reduced[0].astype(jnp.bfloat16), "keys", scatter_dimension=1, tiled=True
        ).astype(jnp.float32),
        lax.psum_scatter(
            reduced[1].astype(jnp.bfloat16), "keys", scatter_dimension=1, tiled=True
        ).astype(jnp.float32),
        lax.psum_scatter(
            reduced[2].astype(jnp.bfloat16), "keys", scatter_dimension=1, tiled=True
        ).astype(jnp.float32),
        lax.psum_scatter(
            reduced[3].astype(jnp.bfloat16), "keys", scatter_dimension=1, tiled=True
        ).astype(jnp.float32),
        lax.psum_scatter(
            reduced[4].astype(jnp.bfloat16), "keys", scatter_dimension=1, tiled=True
        ).astype(jnp.float32),
        lax.psum_scatter(
            reduced[5].astype(jnp.bfloat16), "keys", scatter_dimension=1, tiled=True
        ).astype(jnp.float32),
    )
    smalls = lax.psum(
        (
            time_slots,
            media_gain_grad,
            media_bias_grad,
            latent_gain_grad,
            latent_bias_grad,
            ff_gain_grad,
            ff_bias_grad,
        ),
        ("media", "keys"),
    )
    return (
        resampled,
        patches_grad,
        latents_grad,
        smalls[0],
        smalls[1],
        smalls[2],
        smalls[3],
        smalls[4],
        smalls[5],
        smalls[6],
        reduced[0],
        reduced[1],
        reduced[2],
        reduced[3],
        reduced[4],
        reduced[5],
    )


def solution(mesh):
    in_specs = (
        P("media", "keys", None),
        P("media", "keys", None),
        P("media"),
        P(),
        P(),
        P(),
        P(),
        P(),
        P(),
        P(),
        P(),
        P(),
        P(),
        P(),
        P(),
        P(),
        P("media", "keys", None),
    )
    out_specs = (
        P("media", "keys", None),
        P("media", "keys", None),
        P("media", "keys", None),
        P(),
        P(),
        P(),
        P(),
        P(),
        P(),
        P(),
        P("media", "keys"),
        P("media", "keys"),
        P("media", "keys"),
        P("media", "keys"),
        P("media", "keys"),
        P("media", "keys"),
    )
    return jax.shard_map(shards, mesh=mesh, in_specs=in_specs, out_specs=out_specs, check_vma=False)
```

profile of v0, /device:TPU:0, one launch (start us, length us, event | category | flops | bytes accessed | tf_op | source)
XLA Modules:
  0.0 928.6 jit_solution(17646362462082277765)
XLA Ops:
  21.6 10.1 %all_gather.6 = bf16[6,64,1024]{2,1,0:T(8,128)(2,1)S(1)} all-gather(bf16[6,16,1024]{2,1,0:T(8,128)(2,1)S(1)} %add_convert_fusion.4), channel_id=1, replica_groups=mesh['media'=8,'keys'=4] {'keys'}, dimensions={1}, use_global_device_ids=true | all-gather | bytes 983040 | tf_op jit(solution)/shard_map/all_gather | solution.py:82
  49.8 11.2 %pmax.7 = f32[6,8,64]{2,1,0:T(8,128)S(1)} all-reduce(f32[6,8,64]{2,1,0:T(8,128)S(1)} %get-tuple-element.41), channel_id=1, replica_groups=mesh['media'=8,'keys'=4] {'keys'}, use_global_device_ids=true, to_apply=%region_5.6 | all-reduce | flops 3072 | bytes 24576 | tf_op jit(solution)/shard_map/pmax | solution.py:95
  67.6 11.8 %psum.63 = f32[6,8,64]{2,1,0:T(8,128)} all-reduce(f32[6,8,64]{2,1,0:T(8,128)} %get-tuple-element.39), channel_id=1, replica_groups=mesh['media'=8,'keys'=4] {'keys'}, use_global_device_ids=true, to_apply=%region_8.9 | all-reduce | flops 3072 | bytes 24576 | tf_op jit(solution)/shard_map/psum | solution.py:96
  98.7 16.1 %reduce-scatter.21.cloned.1.call-done = bf16[6,16,512]{2,1,0:T(8,128)(2,1)} async-done(((bf16[6,64,512]{2,1,0:T(8,128)(2,1)}), bf16[6,16,512]{2,1,0:T(8,128)(2,1)}) %reduce-scatter.21.cloned.1.call-update) | async-done | bytes 98320 | tf_op jit(solution)/shard_map/reduce_scatter | solution.py:123
  123.0 8.4 add_convert_fusion.2
  166.6 10.9 %psum.64 = f32[6,8,64]{2,1,0:T(8,128)S(1)} all-reduce(f32[6,8,64]{2,1,0:T(8,128)S(1)} %get-tuple-element.49), channel_id=1, replica_groups=mesh['media'=8,'keys'=4] {'keys'}, use_global_device_ids=true, to_apply=%region_16.17 | all-reduce | flops 3072 | bytes 24576 | tf_op jit(solution)/shard_map/psum | solution.py:155
  197.9 8.3 fusion.91
  223.2 10.2 %bitcast_convert_fusion = bf16[4096,1024]{1,0:T(8,128)(2,1)} fusion(f32[6,16,1024]{2,1,0:T(8,128)} %param.33, f32[6,16,4096]{2,1,0:T(8,128)} %copy-done.100, u8[16,4096]{1,0:T(8,128)(4,1)} %copy-done.102, u8[16,4096]{1,0:T(8,128)(4,1)} %copy-done.101), kind=kOutput, calls=%fused_computation.1 | convolution fusion | flops 837124096 | bytes 10485760 | tf_op jit(solution)/shard_map/mrd,mre->de/dot_general | solution.py:43
  233.5 42.3 %reduce-scatter.29.cloned.1.call-done = bf16[128,512]{1,0:T(8,128)(2,1)} async-done(((bf16[1024,512]{1,0:T(8,128)(2,1)}), bf16[128,512]{1,0:T(8,128)(2,1)}) %reduce-scatter.29.cloned.1.call-update) | async-done | bytes 131088 | tf_op jit(solution)/shard_map/reduce_scatter | solution.py:235
  277.6 64.5 %reduce-scatter.27.cloned.1.call-done = bf16[128,512]{1,0:T(8,128)(2,1)} async-done(((bf16[1024,512]{1,0:T(8,128)(2,1)}), bf16[128,512]{1,0:T(8,128)(2,1)}) %reduce-scatter.27.cloned.1.call-update) | async-done | bytes 131088 | tf_op jit(solution)/shard_map/reduce_scatter | solution.py:232
  343.8 64.0 %reduce-scatter.31.cloned.1.call-done = bf16[64,1024]{1,0:T(8,128)(2,1)} async-done(((bf16[512,1024]{1,0:T(8,128)(2,1)}), bf16[64,1024]{1,0:T(8,128)(2,1)}) %reduce-scatter.31.cloned.1.call-update) | async-done | bytes 131088 | tf_op jit(solution)/shard_map/reduce_scatter | solution.py:238
  407.9 10.2 %fusion.41 = f32[6,512,1024]{2,1,0:T(8,128)} fusion(bf16[6,512,512]{1,2,0:T(8,128)(2,1)} %bitcast.160, bf16[1024,512]{1,0:T(8,128)(2,1)} %param.28), kind=kOutput, calls=%fused_computation.91 | convolution fusion | flops 3221225472 | bytes 16777216 | tf_op jit(solution)/shard_map/mre,de->mrd/dot_general | solution.py:39
  418.1 55.9 %reduce-scatter.25.cloned.1.call-done = bf16[128,512]{1,0:T(8,128)(2,1)} async-done(((bf16[1024,512]{1,0:T(8,128)(2,1)}), bf16[128,512]{1,0:T(8,128)(2,1)}) %reduce-scatter.25.cloned.1.call-update) | async-done | bytes 131088 | tf_op jit(solution)/shard_map/reduce_scatter | solution.py:229
  475.7 15.3 %fusion.92 = (f32[1024]{0:T(1024)}, f32[6,512]{1,0:T(8,128)S(1)}, f32[6,512,1024]{2,1,0:T(8,128)}) fusion(f32[1024]{0:T(1024)} %param.21, f32[6,512]{1,0:T(8,128)S(1)} %broadcast_multiply_fusion, f32[512,1024]{1,0:T(8,128)S(1)} %bitcast.150, bf16[6,512,1024]{2,1,0:T(8,128)(2,1)} %param.18, f32[6,512,1024]{2,1,0:T(8,128)} %fusion.41, ...), kind=kOutput, calls=%fused_computation.177 | convolution fusion | flops 3246387200 | bytes 37781504 | tf_op jit(solution)/shard_map/mre,de->mrd/dot_general | solution.py:39
  491.7 134.0 %reduce-scatter.35.cloned.1.call-done = bf16[128,4096]{1,0:T(8,128)(2,1)} async-done(((bf16[1024,4096]{1,0:T(8,128)(2,1)}), bf16[128,4096]{1,0:T(8,128)(2,1)}) %reduce-scatter.35.cloned.1.call-update) | async-done | bytes 1048592 | tf_op jit(solution)/shard_map/reduce_scatter | solution.py:241
  626.1 10.8 %fusion.89 = f32[6,512]{1,0:T(8,128)S(1)} fusion(f32[6,512]{1,0:T(8,128)} %multiply_multiply_fusion.5, f32[6,512]{1,0:T(8,128)S(1)} %broadcast_multiply_fusion, f32[512,1024]{1,0:T(8,128)S(1)} %bitcast.151, bf16[6,512,1024]{2,1,0:T(8,128)(2,1)} %param.18, f32[6,512]{1,0:T(8,128)} %fusion.77, f32[6,512,1024]{2,1,0:T(8,128)} %get-tuple-element.53, f32[1024]{0:T(1024)} %param.21), kind=kLoop, calls=%fused_computation.174 | loop fusion | flops 28308480 | bytes 21024768 | tf_op jit(solution)/shard_map/transpose(jvp())/reduce_sum | solution.py:17
  636.9 11.5 %multiply_reduce_fusion = (f32[1024]{0:T(1024)}, f32[512,1024]{1,0:T(8,128)}, bf16[6,512,1024]{2,1,0:T(8,128)(2,1)}) fusion(f32[6,512,1024]{2,1,0:T(8,128)S(1)} %copy-done.2, bf16[6,512,1024]{2,1,0:T(8,128)(2,1)} %param.18, f32[6,512]{1,0:T(8,128)S(1)} %copy-done.71, f32[6,512]{1,0:T(8,128)S(1)} %broadcast_multiply_fusion, f32[512,1024]{1,0:T(8,128)S(1)} %bitcast.152, ...), kind=kLoop, calls=%fused_computation.3 | loop fusion | flops 43514880 | bytes 29417472 | tf_op jit(solution)/shard_map/transpose(jvp())/reduce_sum | solution.py:19
  648.4 129.4 %reduce-scatter.39.cloned.1.call-done = bf16[512,1024]{1,0:T(8,128)(2,1)} async-done(((bf16[4096,1024]{1,0:T(8,128)(2,1)}), bf16[512,1024]{1,0:T(8,128)(2,1)}) %reduce-scatter.39.cloned.1.call-update) | async-done | bytes 1048592 | tf_op jit(solution)/shard_map/reduce_scatter | solution.py:244
  777.9 9.3 %fusion.32 = f32[6,16,1024]{2,1,0:T(8,128)} fusion(f32[6,16,1024]{2,1,0:T(8,128)S(1)} %copy-done.21, bf16[4096,1024]{1,0:T(8,128)(2,1)} %param.32, f32[6,16,4096]{2,1,0:T(8,128)} %copy-done.100, u8[16,4096]{1,0:T(8,128)(4,1)} %copy-done.102, u8[16,4096]{1,0:T(8,128)(4,1)} %copy-done.101), kind=kOutput, calls=%fused_computation.82 | convolution fusion | flops 832929792 | bytes 10878976 | tf_op jit(solution)/shard_map/dot_general | solution.py:35
  790.5 40.4 %all-reduce = (f32[8,1024]{1,0:T(8,128)}, f32[1024]{0:T(1024)}, f32[1024]{0:T(1024)}, f32[1024]{0:T(1024)}, f32[1024]{0:T(1024)}, /*index=5*/f32[1024]{0:T(1024)}, f32[1024]{0:T(1024)}) all-reduce(f32[8,1024]{1,0:T(8,128)S(1)} %constant_dynamic-update-slice_fusion, ...), channel_id=1, replica_groups=mesh['media'=8,'keys'=4] {'media','keys'}, use_global_device_ids=true, to_apply=%region_25.26 | all-reduce | flops 14336 | bytes 114688 | tf_op jit(solution)/shard_map/psum | solution.py:268
  835.0 8.0 reduce-scatter.33.cloned.1.call-done
  844.4 20.6 %reduce-scatter.43.cloned.1.call-done = bf16[128,128]{1,0:T(8,128)(2,1)} async-done(((bf16[512,128]{1,0:T(8,128)(2,1)}), bf16[128,128]{1,0:T(8,128)(2,1)}) %reduce-scatter.43.cloned.1.call-update) | async-done | bytes 32784
  866.5 25.9 %reduce-scatter.37.cloned.1.call-done = bf16[128,1024]{1,0:T(8,128)(2,1)} async-done(((bf16[128,4096]{1,0:T(8,128)(2,1)}), bf16[128,1024]{1,0:T(8,128)(2,1)}) %reduce-scatter.37.cloned.1.call-update) | async-done | bytes 262160 | tf_op jit(solution)/shard_map/reduce_scatter | solution.py:261
  894.2 25.7 %reduce-scatter.41.cloned.1.call-done = bf16[512,256]{1,0:T(8,128)(2,1)} async-done(((bf16[512,1024]{1,0:T(8,128)(2,1)}), bf16[512,256]{1,0:T(8,128)(2,1)}) %reduce-scatter.41.cloned.1.call-update) | async-done | bytes 262160 | tf_op jit(solution)/shard_map/reduce_scatter | solution.py:264
  (352 shorter events, 158.0 us)
Async XLA Ops:
  7.2 72.2 %copy-start = (bf16[1024,512]{1,0:T(8,128)(2,1)S(1)}, bf16[1024,512]{1,0:T(8,128)(2,1)}, u32[]{:S(2)}) copy-start(bf16[1024,512]{1,0:T(8,128)(2,1)} %param.29) | copy-start | bytes 3145732
  7.2 107.6 %reduce-scatter.21.cloned.1.call-start = ((), (), s32[]{:S(2)}) async-start(), calls=%async_computation.14 | async-start | bytes 491520 | tf_op jit(solution)/shard_map/reduce_scatter | solution.py:123
  8.8 30.3 %copy-start.3 = (f32[2,256,1024]{2,1,0:T(8,128)}, f32[2,256,1024]{2,1,0:T(8,128)S(1)}, u32[]{:S(2)}) copy-start(f32[2,256,1024]{2,1,0:T(8,128)S(1)} %add.181) | copy-start | bytes 6291460
  67.6 19.7 %slice-start.2 = ((s8[6291456]{0:T(1024)(128)(4,1)}), s8[2097152]{0:T(1024)(128)(4,1)S(1)}, s32[]{:S(2)}) async-start(s8[6291456]{0:T(1024)(128)(4,1)} %bitcast.140), calls=%async_computation.30 | async-start | bytes 4194304
  93.2 120.2 %reduce-scatter.23.cloned.1.call-start = ((), (), s32[]{:S(2)}) async-start(), calls=%async_computation.15 | async-start | bytes 491520 | tf_op jit(solution)/shard_map/reduce_scatter | solution.py:176
  98.7 23.2 %copy-start.43 = (f32[6,16,512]{2,1,0:T(8,128)}, f32[6,16,512]{2,1,0:T(8,128)S(1)}, u32[]{:S(2)}) copy-start(f32[6,16,512]{2,1,0:T(8,128)S(1)} %reshape.218) | copy-start | bytes 589828
  116.1 19.6 %copy-start.20 = (f32[6,16,1024]{2,1,0:T(8,128)}, f32[6,16,1024]{2,1,0:T(8,128)S(1)}, u32[]{:S(2)}) copy-start(f32[6,16,1024]{2,1,0:T(8,128)S(1)} %get-tuple-element.46) | copy-start | bytes 1179652
  116.1 19.6 %copy-start.77 = (f32[6,16]{1,0:T(8,128)}, f32[6,16]{1,0:T(8,128)S(1)}, u32[]{:S(2)}) copy-start(f32[6,16]{1,0:T(8,128)S(1)} %broadcast_multiply_fusion.1) | copy-start | bytes 1156
  116.3 19.4 %copy-start.86 = (f32[6,16]{1,0:T(8,128)}, f32[6,16]{1,0:T(8,128)S(1)}, u32[]{:S(2)}) copy-start(f32[6,16]{1,0:T(8,128)S(1)} %fusion.79) | copy-start | bytes 1156
  187.3 88.6 %reduce-scatter.29.cloned.1.call-start = ((), (), s32[]{:S(2)}) async-start(), calls=%async_computation.18 | async-start | bytes 1179648 | tf_op jit(solution)/shard_map/reduce_scatter | solution.py:235
  194.4 147.7 %reduce-scatter.27.cloned.1.call-start = ((), (), s32[]{:S(2)}) async-start(), calls=%async_computation.17 | async-start | bytes 1179648 | tf_op jit(solution)/shard_map/reduce_scatter | solution.py:232
  207.7 200.1 %reduce-scatter.31.cloned.1.call-start = ((), (), s32[]{:S(2)}) async-start(), calls=%async_computation.19 | async-start | bytes 1179648 | tf_op jit(solution)/shard_map/reduce_scatter | solution.py:238
  210.2 263.8 %reduce-scatter.25.cloned.1.call-start = ((), (), s32[]{:S(2)}) async-start(), calls=%async_computation.16 | async-start | bytes 1179648 | tf_op jit(solution)/shard_map/reduce_scatter | solution.py:229
  216.0 409.7 %reduce-scatter.35.cloned.1.call-start = ((), (), s32[]{:S(2)}) async-start(), calls=%async_computation.21 | async-start | bytes 9437184 | tf_op jit(solution)/shard_map/reduce_scatter | solution.py:241
  223.0 554.9 %reduce-scatter.39.cloned.1.call-start = ((), (), s32[]{:S(2)}) async-start(), calls=%async_computation.23 | async-start | bytes 9437184 | tf_op jit(solution)/shard_map/reduce_scatter | solution.py:244
  233.5 598.5 %reduce-scatter.47.cloned.1.call-start = ((), (), s32[]{:S(2)}) async-start(), calls=%async_computation.27 | async-start | bytes 163840
  277.5 555.9 %reduce-scatter.45.cloned.1.call-start = ((), (), s32[]{:S(2)}) async-start(), calls=%async_computation.26 | async-start | bytes 163840
  343.7 499.2 %reduce-scatter.33.cloned.1.call-start = ((), (), s32[]{:S(2)}) async-start(), calls=%async_computation.20 | async-start | bytes 163840 | tf_op jit(solution)/shard_map/reduce_scatter | solution.py:258
  407.9 457.1 %reduce-scatter.43.cloned.1.call-start = ((), (), s32[]{:S(2)}) async-start(), calls=%async_computation.25 | async-start | bytes 163840
  475.7 416.7 %reduce-scatter.37.cloned.1.call-start = ((), (), s32[]{:S(2)}) async-start(), calls=%async_computation.22 | async-start | bytes 1310720 | tf_op jit(solution)/shard_map/reduce_scatter | solution.py:261
  625.7 294.2 %reduce-scatter.41.cloned.1.call-start = ((), (), s32[]{:S(2)}) async-start(), calls=%async_computation.24 | async-start | bytes 1310720 | tf_op jit(solution)/shard_map/reduce_scatter | solution.py:264
  789.6 41.4 %copy-start.27 = (f32[6,16,1024]{2,1,0:T(8,128)S(1)}, f32[6,16,1024]{2,1,0:T(8,128)}, u32[]{:S(2)}) copy-start(f32[6,16,1024]{2,1,0:T(8,128)} %copy-done.26) | copy-start | bytes 1179652
  789.6 41.4 %copy-start.35 = (f32[6,16,1024]{2,1,0:T(8,128)S(1)}, f32[6,16,1024]{2,1,0:T(8,128)}, u32[]{:S(2)}) copy-start(f32[6,16,1024]{2,1,0:T(8,128)} %param.33) | copy-start | bytes 1179652
  789.6 41.4 %copy-start.79 = (f32[6,16]{1,0:T(8,128)S(1)}, f32[6,16]{1,0:T(8,128)}, u32[]{:S(2)}) copy-start(f32[6,16]{1,0:T(8,128)} %copy-done.78) | copy-start | bytes 1156
  (101 other events, 472.9 us)
Sparse Core Ops, SparseCore 0:
  93.3 21.4 reduce-scatter.20
  187.4 21.4 reduce-scatter.22
  212.3 63.4 reduce-scatter.28
  279.5 62.5 reduce-scatter.26
  345.3 62.4 reduce-scatter.30
  411.5 62.4 reduce-scatter.24
  477.6 148.0 reduce-scatter.34
  629.8 148.0 reduce-scatter.38
  780.3 18.5 reduce-scatter.46
  801.3 19.5 reduce-scatter.44
  823.3 19.5 reduce-scatter.32
  845.4 19.5 reduce-scatter.42
  867.5 24.8 reduce-scatter.36
  895.0 24.8 reduce-scatter.40
where the time goes:
time: 937 us; the launch traced here: 929 us
  waiting for transfers between devices  587 us (63%)
  matrix products  146 us (16%)
  blocking collectives  91 us (10%)
  other arithmetic  56.3 us (6%)
  local copies, waits for them, and re-layouts  31.7 us (3%)
  between operations  15.8 us (2%)
    reduce_scatter x1, waiting for transfers between devices, shards(): lax.psum_scatter(weight_grads[4].astype(jnp.bfloat16), 'media', scatter_d...  134 us
    reduce_scatter x1, waiting for transfers between devices, shards(): lax.psum_scatter(weight_grads[5].astype(jnp.bfloat16), 'media', scatter_d...  129 us
    reduce_scatter x1, waiting for transfers between devices, shards(): lax.psum_scatter(weight_grads[1].astype(jnp.bfloat16), 'media', scatter_d...  64.5 us
    reduce_scatter x1, waiting for transfers between devices, shards(): lax.psum_scatter(weight_grads[3].astype(jnp.bfloat16), 'media', scatter_d...  64 us
    reduce_scatter x1, waiting for transfers between devices, shards(): lax.psum_scatter(weight_grads[0].astype(jnp.bfloat16), 'media', scatter_d...  55.9 us
    reduce_scatter x1, waiting for transfers between devices, shards(): lax.psum_scatter(weight_grads[2].astype(jnp.bfloat16), 'media', scatter_d...  42.3 us
    dot_general x8, matrix products, weight_term(): jnp.einsum('mrd,mre->de', left, right, preferred_element_type=jnp.float32)  40.8 us
    psum x1, blocking collectives, shards(): lax.psum((time_slots, media_gain_grad, media_bias_grad, latent_gain_grad,...  40.4 us
  transfers between devices with their start and end apart: 14, of which 11 were waited for; matrix products, arithmetic and copies ran while one was open for 13% of the time, Pallas kernels for 0%

commit v1 on v0

v1 whole, which is shorter than its diff:
```python
import functools

import jax
import jax.numpy as jnp
from jax import lax
from jax.experimental import pallas as pl
from jax.experimental.pallas import tpu as pltpu
from jax.sharding import PartitionSpec as P

HEAD = 64
PATCH = 256
GROUP = 256
LANES = 128

EPS = 1e-05
NEG = -1e30
PAIR = 2

f32 = jnp.float32
bf16 = jnp.bfloat16


def mul(left, right, contract=((1,), (0,)), precision=None):
    return lax.dot_general(
        left, right, (contract, ((), ())), precision=precision, preferred_element_type=f32
    )


NN = ((1,), (0,))
NT = ((1,), (1,))
TN = ((0,), (0,))


def norm_parts(values):
    centre = jnp.mean(values, -1, keepdims=True)
    shifted = values - centre
    spread = jnp.mean(shifted * shifted, -1, keepdims=True)
    return centre, lax.rsqrt(spread + EPS), shifted


def norm(values, gain, bias):
    _, scale, shifted = norm_parts(values)
    return shifted * scale * gain + bias


def norm_back(values, gain, grad):
    _, scale, shifted = norm_parts(values)
    unit = shifted * scale
    scaled = grad * gain
    first = jnp.mean(scaled, -1, keepdims=True)
    second = jnp.mean(scaled * unit, -1, keepdims=True)
    back = scale * (scaled - first - unit * second)
    return (
        back,
        jnp.sum(grad * unit, 0, keepdims=True),
        jnp.sum(grad, 0, keepdims=True),
    )


def gelu_parts(hidden):
    cdf = 0.5 * (1.0 + lax.erf(hidden * (2.0**-0.5)))
    pdf = jnp.exp(-0.5 * hidden * hidden) * 0.3989422804014327
    return cdf, cdf + hidden * pdf


def head_mask(rows, width, heads):
    row = lax.broadcasted_iota(jnp.int32, (heads * rows, width), 0) // rows
    col = lax.broadcasted_iota(jnp.int32, (heads * rows, width), 1)
    return row, col


def spread_heads(values):
    heads = values.shape[1] // HEAD
    row, col = head_mask(values.shape[0], values.shape[1], heads)
    return jnp.where(row == col // HEAD, jnp.concatenate([values] * heads, 0), jnp.zeros((), values.dtype))


def fold_heads(values):
    heads = values.shape[1] // HEAD
    rows = values.shape[0] // heads
    row, col = head_mask(rows, values.shape[1], heads)
    kept = jnp.where(row == col // HEAD, values, 0.0)
    total = kept[:rows]
    for h in range(1, heads):
        total = total + kept[h * rows : (h + 1) * rows]
    return total


def three_parts(values, lane, start, slots):
    high = values.astype(bf16).astype(f32)
    rest = values - high
    middle = rest.astype(bf16).astype(f32)
    low = rest - middle
    place = lane // slots - start
    return jnp.where(place == 0, high, jnp.where(place == 1, middle, jnp.where(place == 2, low, 0.0)))


def cost(flops, moved, special=0):
    return pl.CostEstimate(flops=int(flops), bytes_accessed=int(moved), transcendentals=int(special))


def params(mib, grid=0):
    return pltpu.CompilerParams(vmem_limit_bytes=mib << 20)


def latent_kernel(lat, gain, bias, cot, wq, wk, wv, low_o, q_o, k_o, v_o, out_o):
    low = norm(lat[...], gain[...], bias[...]).astype(bf16)
    low_o[...] = low
    q_o[...] = mul(low, wq[...]).astype(bf16)
    k_o[...] = mul(low, wk[...]).astype(bf16)
    v_o[...] = mul(low, wv[...]).astype(bf16)
    out_o[...] = cot[...].astype(bf16)


def patch_kernel(frames, patches, time, gain, bias, wk, wv, low_o, k_o, v_o):
    for f in range(frames):
        rows = pl.ds(f * PATCH, PATCH)
        framed = patches[0, rows, :].astype(f32) + time[0, f : f + 1, :]
        low = norm(framed, gain[...], bias[...]).astype(bf16)
        low_o[0, rows, :] = low
        k_o[0, rows, :] = mul(low, wk[...]).astype(bf16)
        v_o[0, rows, :] = mul(low, wv[...]).astype(bf16)


def masked_scores(query, keys, frames, first, count):
    scores = mul(query, keys, NT)
    parts = []
    for f in range(frames):
        part = scores[:, f * PATCH : (f + 1) * PATCH]
        parts.append(jnp.where(first + f < count, part, NEG))
    return jnp.concatenate(parts, 1) if frames > 1 else parts[0]


def attend_kernel(n_keys, frames, scalars, counts, *refs):
    q = refs[:n_keys]
    kp, vp, kl, vl = refs[n_keys : n_keys + 4]
    outs = refs[n_keys + 4 :]
    own = q[0].shape[0]
    inner = q[0].shape[1]
    heads = inner // HEAD
    count = counts[pl.program_id(0)]
    first = scalars[0] * frames
    query = jnp.concatenate([r[...] for r in q], 0)
    rows = query.shape[0]
    stats = jnp.zeros((rows, LANES), f32)
    shares = []
    for g in range(inner // GROUP):
        cols = slice(g * GROUP, (g + 1) * GROUP)
        wide = spread_heads(query[:, cols] * bf16(HEAD**-0.5))
        scores = masked_scores(wide, kp[0, :, cols], frames, first, count)
        lat_scores = mul(wide, kl[:, cols], NT)
        top = jnp.maximum(
            jnp.max(scores, -1, keepdims=True), jnp.max(lat_scores, -1, keepdims=True)
        )
        raw = jnp.exp(scores - top)
        lat_raw = jnp.exp(lat_scores - top)
        total = jnp.sum(raw, -1, keepdims=True) + jnp.sum(lat_raw, -1, keepdims=True)
        share = mul(raw.astype(bf16), vp[0, :, cols]) + mul(lat_raw.astype(bf16), vl[:, cols])
        shares.append(fold_heads(share / total).astype(bf16))
        level = top + jnp.log(total)
        row, lane = head_mask(rows, LANES, GROUP // HEAD)
        kept = jnp.where(lane % heads == row + g * (GROUP // HEAD), level, 0.0)
        for h in range(GROUP // HEAD):
            stats = stats + kept[h * rows : (h + 1) * rows]
    lane = lax.broadcasted_iota(jnp.int32, stats.shape, 1)
    packed = jnp.concatenate(shares + [three_parts(stats, lane, 0, heads).astype(bf16)], 1)
    for s in range(n_keys):
        outs[s][...] = packed[s * own : (s + 1) * own]


def sum_runs(stats, heads, start):
    total = None
    for part in range(3):
        shift = (-(start + part) * heads) % LANES
        term = pltpu.roll(stats, shift, 1) if shift else stats
        total = term if total is None else total + term
    return total


def join_kernel(n_keys, latents, gain, bias, wo, *refs):
    slots = refs[:n_keys]
    att_o, low_o, mid_o, ff_o, lse_o = refs[n_keys:]
    inner = att_o.shape[1]
    heads = inner // HEAD
    levels = [sum_runs(r[:, inner:].astype(f32), heads, 0) for r in slots]
    top = functools.reduce(jnp.maximum, levels)
    weights = [jnp.exp(v - top) for v in levels]
    total = functools.reduce(jnp.add, weights)
    inverse = 1.0 / total
    lane = lax.broadcasted_iota(jnp.int32, (LANES, inner), 0)
    col = lax.broadcasted_iota(jnp.int32, (LANES, inner), 1)
    select = jnp.where(lane == col // HEAD, 1.0, 0.0)
    attended = None
    for s in range(n_keys):
        wide = mul(weights[s] * inverse, select, NN, lax.Precision.HIGHEST)
        term = wide * slots[s][:, :inner].astype(f32)
        attended = term if attended is None else attended + term
    low = attended.astype(bf16)
    middle = latents[...] + mul(low, wo[...])
    att_o[...] = attended
    low_o[...] = low
    mid_o[...] = middle
    ff_o[...] = norm(middle, gain[...], bias[...]).astype(bf16)
    lse_o[...] = top + jnp.log(total)


def forward_kernel(
    n_keys,
    scalars,
    attended,
    att_low,
    middle,
    ff_low,
    lse,
    cot,
    out_low,
    gain,
    wo,
    up,
    down,
    res_o,
    mid_grad_o,
    pack_o,
    gain_o,
    bias_o,
    wo_grad_o,
    res_acc,
    in_acc,
):
    step = pl.program_id(0)

    @pl.when(step == 0)
    def _():
        res_acc[...] = jnp.zeros_like(res_acc)
        in_acc[...] = jnp.zeros_like(in_acc)

    hidden = mul(ff_low[...], up[...])
    act_grad = mul(out_low[...], down[...], NT)
    cdf, slope = gelu_parts(hidden)
    res_acc[...] += mul((hidden * cdf).astype(bf16), down[...])
    in_acc[...] += mul((act_grad * slope).astype(bf16), up[...], NT)

    @pl.when(step == pl.num_programs(0) - 1)
    def _():
        inner = attended.shape[1]
        heads = inner // HEAD
        res_o[...] = middle[...] + res_acc[...]
        back, gain_grad, bias_grad = norm_back(middle[...], gain[...], in_acc[...])
        gain_o[...] = gain_grad
        bias_o[...] = bias_grad
        mid_grad = cot[...] + back
        mid_grad_o[...] = mid_grad
        branch = mid_grad.astype(bf16)
        att_grad = mul(branch, wo[...], NT).astype(bf16)
        col = lax.broadcasted_iota(jnp.int32, (inner, LANES), 0)
        lane = lax.broadcasted_iota(jnp.int32, (inner, LANES), 1)
        select = jnp.where(col // HEAD == lane % heads, 1.0, 0.0)
        delta = mul(attended[...] * att_grad.astype(f32), select, NN, lax.Precision.HIGHEST)
        lane = lax.broadcasted_iota(jnp.int32, delta.shape, 1)
        level = jnp.where(lane < heads, lse[...], 0.0)
        level = level + pltpu.roll(level, heads, 1) + pltpu.roll(level, 2 * heads, 1)
        stats = three_parts(level, lane, 0, heads) + three_parts(delta, lane, 3, heads)
        pack_o[...] = jnp.concatenate([att_grad, stats.astype(bf16)], 1)
        wo_grad_o[...] = mul(att_low[...], branch, TN).astype(bf16)


def ff_grad_kernel(n_slots, *refs):
    ins = refs[:n_slots]
    outs = refs[n_slots : 2 * n_slots]
    up, down, up_o, down_o = refs[2 * n_slots :]
    ff_all = jnp.concatenate([r[...] for r in ins], 0)
    out_all = jnp.concatenate([r[...] for r in outs], 0)
    hidden = mul(ff_all, up[...])
    act_grad = mul(out_all, down[...], NT)
    cdf, slope = gelu_parts(hidden)
    down_o[...] = mul((hidden * cdf).astype(bf16), out_all, TN).astype(bf16)
    up_o[...] = mul((act_grad * slope).astype(bf16), ff_all, TN).astype(bf16)


def attend_back_kernel(n_keys, frames, scalars, counts, *refs):
    q = refs[:n_keys]
    packs = refs[n_keys : 2 * n_keys]
    kp, vp, kl, vl = refs[2 * n_keys : 2 * n_keys + 4]
    kv_t_o, kl_o, vl_o = refs[2 * n_keys + 4 : 2 * n_keys + 7]
    q_o = refs[2 * n_keys + 7 :]
    own = q[0].shape[0]
    inner = q[0].shape[1]
    heads = inner // HEAD
    count = counts[pl.program_id(0)]
    first = scalars[0] * frames
    query = jnp.concatenate([r[...] for r in q], 0)
    grad = jnp.concatenate([r[:, :inner] for r in packs], 0)
    stats = jnp.concatenate([r[:, inner:] for r in packs], 0).astype(f32)
    rows = query.shape[0]
    for g in range(inner // GROUP):
        cols = slice(g * GROUP, (g + 1) * GROUP)
        row, lane = head_mask(rows, LANES, GROUP // HEAD)
        tiled = jnp.concatenate([stats] * (GROUP // HEAD), 0)
        mine = lane % heads == row + g * (GROUP // HEAD)
        level = jnp.sum(jnp.where(mine & (lane < 3 * heads), tiled, 0.0), -1, keepdims=True)
        delta = jnp.sum(
            jnp.where(mine & (lane >= 3 * heads) & (lane < 6 * heads), tiled, 0.0),
            -1,
            keepdims=True,
        )
        wide = spread_heads(query[:, cols] * bf16(HEAD**-0.5))
        wide_grad = spread_heads(grad[:, cols])
        probs = jnp.exp(masked_scores(wide, kp[0, :, cols], frames, first, count) - level)
        prob_grad = mul(wide_grad, vp[0, :, cols], NT)
        score_grad = (probs * (prob_grad - delta)).astype(bf16)
        kv_t_o[pl.ds(g * GROUP, GROUP), :] = mul(wide, score_grad, TN).astype(bf16)
        kv_t_o[pl.ds(inner + g * GROUP, GROUP), :] = mul(
            wide_grad, probs.astype(bf16), TN
        ).astype(bf16)
        lat_probs = jnp.exp(mul(wide, kl[:, cols], NT) - level)
        lat_prob_grad = mul(wide_grad, vl[:, cols], NT)
        lat_score_grad = (lat_probs * (lat_prob_grad - delta)).astype(bf16)
        kl_o[:, cols] = mul(lat_score_grad, wide, TN).astype(bf16)
        vl_o[:, cols] = mul(lat_probs.astype(bf16), wide_grad, TN).astype(bf16)
        query_grad = mul(score_grad, kp[0, :, cols]) + mul(lat_score_grad, kl[:, cols])
        query_grad = (fold_heads(query_grad) * HEAD**-0.5).astype(bf16)
        for s in range(n_keys):
            q_o[s][:, cols] = query_grad[s * own : (s + 1) * own]


def weight_kernel(n_keys, scalars, k_t, v_t, low, kl_t, lat_low, *refs):
    q_grads = refs[:n_keys]
    lats = refs[n_keys : 2 * n_keys]
    out = refs[-1]
    vl_t = refs[-2]
    width = k_t.shape[0]
    kv = jnp.concatenate([k_t[...], v_t[...]], 0)
    kv_lat = jnp.concatenate([kl_t[...], vl_t[...]], 1)
    total = mul(kv, low[...]) + mul(kv_lat, lat_low[...], TN)
    query = jnp.concatenate([r[...] for r in q_grads], 0)
    lat_all = jnp.concatenate([r[...] for r in lats], 0)
    out[0, :width, :] = mul(query, lat_all, TN).astype(bf16)
    out[0, width:, :] = total.astype(bf16)


def patch_back_kernel(frames, n_frames, scalars, kv_t, patches, time, gain, wk, wv, grad_o, small_o):
    inner = wk.shape[1]

    @pl.when(pl.program_id(0) == 0)
    def _():
        small_o[...] = jnp.zeros_like(small_o)

    for f in range(frames):
        rows = pl.ds(f * PATCH, PATCH)
        span = slice(f * PATCH, (f + 1) * PATCH)
        grad = mul(kv_t[:inner, span], wk[...], ((0,), (1,)))
        grad = grad + mul(kv_t[inner:, span], wv[...], ((0,), (1,)))
        framed = patches[0, rows, :].astype(f32) + time[0, f : f + 1, :]
        back, gain_grad, bias_grad = norm_back(framed, gain[...], grad)
        grad_o[0, rows, :] = back.astype(bf16)
        slot = pl.ds(scalars[0] * frames + f, 1)
        small_o[slot, :] += jnp.sum(back, 0, keepdims=True)
        small_o[n_frames : n_frames + 1, :] += gain_grad
        small_o[n_frames + 1 : n_frames + 2, :] += bias_grad


def latent_back_kernel(n_keys, latents, gain, mid_grad, kl_g, vl_g, wq, wk, wv, *refs):
    slots = refs[:n_keys]
    lat_o, gain_o, bias_o = refs[n_keys:]
    query = functools.reduce(jnp.add, [r[...].astype(f32) for r in slots]).astype(bf16)
    grad = mul(query, wq[...], NT) + mul(kl_g[...], wk[...], NT) + mul(vl_g[...], wv[...], NT)
    back, gain_grad, bias_grad = norm_back(latents[...], gain[...], grad)
    lat_o[...] = mid_grad[...] + back
    gain_o[...] = gain_grad
    bias_o[...] = bias_grad


def whole(shape):
    return pl.BlockSpec(shape, lambda *_: (0,) * len(shape))


def struct(shape, dtype):
    return jax.ShapeDtypeStruct(shape, dtype)


def tree_sum(parts):
    while len(parts) > 1:
        parts = [parts[i] + parts[i + 1] for i in range(0, len(parts), 2)]
    return parts[0]


def shards(
    n_media,
    n_keys,
    latents,
    patches,
    frame_counts,
    time_embedding,
    media_gain,
    media_bias,
    latent_gain,
    latent_bias,
    ff_gain,
    ff_bias,
    query_weight,
    key_weight,
    value_weight,
    out_weight,
    up_weight,
    down_weight,
    cotangent,
):
    media, own, dim = latents.shape
    key_rows = patches.shape[1]
    inner = query_weight.shape[1]
    hidden = up_weight.shape[1]
    frames = key_rows // PATCH
    n_frames = time_embedding.shape[0]
    rows = media * own
    n_far = n_media // PAIR
    width = inner // n_keys
    m_index = lax.axis_index("media")
    k_index = lax.axis_index("keys")
    near = m_index % PAIR
    far = m_index // PAIR
    scalars = k_index.astype(jnp.int32).reshape(1)

    def over_keys(value, shift):
        return lax.ppermute(value, "keys", [(i, i ^ shift) for i in range(n_keys)])

    def over_media(value, shift):
        return lax.ppermute(value, "media", [(i, i ^ shift) for i in range(n_media)])

    def gather_keys(value):
        slots = [None] * n_keys
        for s in range(0, n_keys, 2):
            slots[s] = value if s == 0 else over_keys(value, s)
        for s in range(0, n_keys, 2):
            slots[s + 1] = over_keys(slots[s], 1)
        return slots

    def gather_near(value):
        return gather_keys(value) + gather_keys(over_media(value, 1))

    def scatter_keys(slots):
        kept = [
            (slots[s].astype(f32) + over_keys(slots[s + 1], 1).astype(f32))
            for s in range(0, n_keys, 2)
        ]
        total = kept[0]
        for s in range(2, n_keys, 2):
            total = total + over_keys(kept[s // 2].astype(bf16), s).astype(f32)
        return total.astype(bf16)

    def scatter_far(parts):
        total = lax.dynamic_index_in_dim(parts, far, 0, False).astype(f32)
        for s in range(1, n_far):
            part = lax.dynamic_index_in_dim(parts, far ^ s, 0, False)
            total = total + over_media(part, PAIR * s).astype(f32)
        return total

    def scatter_media(value, axis):
        shape = value.shape
        each = shape[axis] // n_media
        parts = value.reshape(shape[:axis] + (n_far, PAIR, each) + shape[axis + 1 :])
        keep = lax.dynamic_index_in_dim(parts, near, axis + 1, False)
        send = lax.dynamic_index_in_dim(parts, 1 - near, axis + 1, False)
        half = (keep.astype(f32) + over_media(send, 1).astype(f32)).astype(bf16)
        return scatter_far(jnp.moveaxis(half, axis, 0))

    def everywhere(value):
        total = tree_sum([value] + [over_media(value, s) for s in range(1, n_media)])
        return tree_sum([total] + [over_keys(total, s) for s in range(1, n_keys)])

    lat = latents.reshape(rows, dim)
    cot = cotangent.reshape(rows, dim)
    row = lambda v: v.reshape(1, dim)
    time_blocks = time_embedding.reshape(n_keys, frames, dim)

    lat_low, q_own, kl, vl, out_low = pl.pallas_call(
        latent_kernel,
        name="latent_project",
        out_shape=(
            struct((rows, dim), bf16),
            struct((rows, inner), bf16),
            struct((rows, inner), bf16),
            struct((rows, inner), bf16),
            struct((rows, dim), bf16),
        ),
        compiler_params=params(24),
        cost_estimate=cost(6 * rows * dim * inner, 6 * dim * inner + 14 * rows * dim),
    )(lat, row(latent_gain), row(latent_bias), cot, query_weight, key_weight, value_weight)
    q_all = gather_keys(q_own)
    lat_all = gather_keys(lat_low)
    out_all = gather_near(out_low)

    patch_block = pl.BlockSpec((1, key_rows, dim), lambda i, *_: (i, 0, 0))
    inner_block = pl.BlockSpec((1, key_rows, inner), lambda i, *_: (i, 0, 0))
    time_block = pl.BlockSpec((1, frames, dim), lambda i, s, *_: (s[0], 0, 0))
    patch_flops = 4 * media * key_rows * dim * inner
    media_low, kp, vp = pl.pallas_call(
        lambda scalars, *refs: patch_kernel(frames, *refs),
        name="patch_project",
        grid_spec=pltpu.PrefetchScalarGridSpec(
            num_scalar_prefetch=1,
            grid=(media,),
            in_specs=[
                patch_block,
                time_block,
                whole((1, dim)),
                whole((1, dim)),
                whole((dim, inner)),
                whole((dim, inner)),
            ],
            out_specs=[patch_block, inner_block, inner_block],
        ),
        out_shape=(
            struct(patches.shape, bf16),
            struct((media, key_rows, inner), bf16),
            struct((media, key_rows, inner), bf16),
        ),
        compiler_params=params(40),
        cost_estimate=cost(patch_flops, 12 * media * key_rows * dim),
    )(scalars, patches, time_blocks, row(media_gain), row(media_bias), key_weight, value_weight)

    own_block = lambda w: pl.BlockSpec((own, w), lambda i, *_: (i, 0))
    packed = inner + LANES
    att_flops = 4 * media * n_keys * own * (key_rows + own) * inner * (GROUP // HEAD)
    shares = pl.pallas_call(
        functools.partial(attend_kernel, n_keys, frames),
        name="attend",
        grid_spec=pltpu.PrefetchScalarGridSpec(
            num_scalar_prefetch=2,
            grid=(media,),
            in_specs=[own_block(inner)] * n_keys
            + [inner_block, inner_block, own_block(inner), own_block(inner)],
            out_specs=[own_block(packed)] * n_keys,
        ),
        out_shape=[struct((rows, packed), bf16)] * n_keys,
        compiler_params=params(24),
        cost_estimate=cost(att_flops, 4 * media * key_rows * inner),
    )(scalars, frame_counts, *q_all, kp, vp, kl, vl)
    joined = [shares[0]] + [over_keys(shares[s], s) for s in range(1, n_keys)]

    attended, att_low, middle, ff_low, lse = pl.pallas_call(
        functools.partial(join_kernel, n_keys),
        name="join",
        out_shape=(
            struct((rows, inner), f32),
            struct((rows, inner), bf16),
            struct((rows, dim), f32),
            struct((rows, dim), bf16),
            struct((rows, LANES), f32),
        ),
        compiler_params=params(16),
        cost_estimate=cost(2 * rows * inner * dim, 2 * inner * dim + 16 * rows * dim),
    )(lat, row(ff_gain), row(ff_bias), out_weight, *joined)
    ff_all = gather_near(ff_low)

    chunk = min(512, hidden)
    steps = hidden // chunk
    resampled, mid_grad, pack, ff_gain_grad, ff_bias_grad, out_partial = pl.pallas_call(
        functools.partial(forward_kernel, n_keys),
        name="feed_forward",
        grid_spec=pltpu.PrefetchScalarGridSpec(
            num_scalar_prefetch=1,
            grid=(steps,),
            in_specs=[
                whole((rows, inner)),
                whole((rows, inner)),
                whole((rows, dim)),
                whole((rows, dim)),
                whole((rows, LANES)),
                whole((rows, dim)),
                whole((rows, dim)),
                whole((1, dim)),
                whole((inner, dim)),
                pl.BlockSpec((dim, chunk), lambda i, *_: (0, i)),
                pl.BlockSpec((chunk, dim), lambda i, *_: (i, 0)),
            ],
            out_specs=[
                whole((rows, dim)),
                whole((rows, dim)),
                whole((rows, packed)),
                whole((1, dim)),
                whole((1, dim)),
                whole((inner, dim)),
            ],
            scratch_shapes=[pltpu.VMEM((rows, dim), f32), pltpu.VMEM((rows, dim), f32)],
        ),
        out_shape=(
            struct((rows, dim), f32),
            struct((rows, dim), f32),
            struct((rows, packed), bf16),
            struct((1, dim), f32),
            struct((1, dim), f32),
            struct((inner, dim), bf16),
        ),
        compiler_params=params(32),
        cost_estimate=cost(8 * rows * dim * hidden, 4 * dim * hidden + 24 * rows * dim),
    )(
        scalars,
        attended,
        att_low,
        middle,
        ff_low,
        lse,
        cot,
        out_low,
        row(ff_gain),
        out_weight,
        up_weight,
        down_weight,
    )
    packs = gather_keys(pack)

    units = hidden // (n_keys * PAIR)
    slice_index = (k_index * PAIR + near).astype(jnp.int32).reshape(1)
    n_slots = PAIR * n_keys
    up_partial, down_partial = pl.pallas_call(
        lambda s, *refs: ff_grad_kernel(n_slots, *refs),
        name="feed_forward_weights",
        grid_spec=pltpu.PrefetchScalarGridSpec(
            num_scalar_prefetch=1,
            grid=(1,),
            in_specs=[whole((rows, dim))] * (2 * n_slots)
            + [
                pl.BlockSpec((dim, units), lambda i, s: (0, s[0])),
                pl.BlockSpec((units, dim), lambda i, s: (s[0], 0)),
            ],
            out_specs=[whole((units, dim)), whole((units, dim))],
        ),
        out_shape=(struct((units, dim), bf16), struct((units, dim), bf16)),
        compiler_params=params(40),
        cost_estimate=cost(
            8 * n_slots * rows * dim * units, 8 * dim * units + 4 * n_slots * rows * dim
        ),
    )(slice_index, *ff_all, *out_all, up_weight, down_weight)
    each = dim // n_media
    up_parts = jnp.moveaxis(up_partial.reshape(units, n_far, PAIR * each), 1, 0)
    up_sum = scatter_far(up_parts).astype(bf16).reshape(units, PAIR, each)
    up_keep = lax.dynamic_index_in_dim(up_sum, near, 1, False)
    up_send = lax.dynamic_index_in_dim(up_sum, 1 - near, 1, False)
    up_got = over_media(up_send, 1)
    up_grad = jnp.where(
        near == 0,
        jnp.concatenate([up_keep, up_got], 0),
        jnp.concatenate([up_got, up_keep], 0),
    ).T.astype(f32)
    blocks = n_far // n_keys
    down_parts = down_partial.reshape(blocks, units // blocks, n_keys, dim // n_keys)
    down_parts = down_parts.transpose(0, 2, 1, 3).reshape(
        n_far, units // blocks, dim // n_keys
    )
    down_sum = scatter_far(down_parts).astype(bf16)
    route = []
    for m in range(n_media):
        for k in range(n_keys):
            block, owner = divmod(m // PAIR, n_keys)
            target = (k * PAIR + m % PAIR) * blocks + block
            route.append((m * n_keys + k, target * n_keys + owner))
    down_grad = lax.ppermute(down_sum, ("media", "keys"), route).astype(f32)

    back = pl.pallas_call(
        functools.partial(attend_back_kernel, n_keys, frames),
        name="attend_back",
        grid_spec=pltpu.PrefetchScalarGridSpec(
            num_scalar_prefetch=2,
            grid=(media,),
            in_specs=[own_block(inner)] * n_keys
            + [own_block(packed)] * n_keys
            + [inner_block, inner_block, own_block(inner), own_block(inner)],
            out_specs=[
                pl.BlockSpec((2 * inner, key_rows), lambda i, *_: (0, i)),
                own_block(inner),
                own_block(inner),
            ]
            + [own_block(inner)] * n_keys,
        ),
        out_shape=[
            struct((2 * inner, media * key_rows), bf16),
            struct((rows, inner), bf16),
            struct((rows, inner), bf16),
        ]
        + [struct((rows, inner), bf16)] * n_keys,
        compiler_params=params(40),
        cost_estimate=cost(5 * att_flops // 2, 8 * media * key_rows * inner),
    )(scalars, frame_counts, *q_all, *packs, kp, vp, kl, vl)
    kv_t, kl_grad, vl_grad = back[:3]
    q_partial = back[3:]
    q_slots = [q_partial[0]] + [over_keys(q_partial[s], s) for s in range(1, n_keys)]

    all_rows = media * key_rows
    slot_rows = lambda base: pl.BlockSpec(
        (width, all_rows), lambda i, s, base=base: (base + (s[0] ^ i), 0)
    )
    slot_cols = pl.BlockSpec((rows, width), lambda i, s: (0, s[0] ^ i))
    if width % LANES == 0:
        kl_cols, vl_cols, q_cols, cols_spec = kl_grad, vl_grad, q_partial, slot_cols
    else:
        cut = lambda v: v.reshape(rows, n_keys, width).transpose(1, 0, 2)
        kl_cols, vl_cols, q_cols = cut(kl_grad), cut(vl_grad), [cut(v) for v in q_partial]
        cols_spec = pl.BlockSpec((None, rows, width), lambda i, s: (s[0] ^ i, 0, 0))
    w_slots = pl.pallas_call(
        functools.partial(weight_kernel, n_keys),
        name="projection_weights",
        grid_spec=pltpu.PrefetchScalarGridSpec(
            num_scalar_prefetch=1,
            grid=(n_keys,),
            in_specs=[
                slot_rows(0),
                slot_rows(n_keys),
                whole((all_rows, dim)),
                cols_spec,
                whole((rows, dim)),
            ]
            + [cols_spec] * n_keys
            + [whole((rows, dim))] * n_keys
            + [cols_spec],
            out_specs=pl.BlockSpec((1, 3 * width, dim), lambda i, s: (i, 0, 0)),
        ),
        out_shape=struct((n_keys, 3 * width, dim), bf16),
        compiler_params=params(48),
        cost_estimate=cost(patch_flops, 4 * media * key_rows * dim),
    )(
        scalars,
        kv_t,
        kv_t,
        media_low.reshape(all_rows, dim),
        kl_cols,
        lat_low,
        *q_cols,
        *lat_all,
        vl_cols,
    )
    w_sum = scatter_keys([w_slots[s] for s in range(n_keys)])
    w_grads = scatter_media(w_sum, 1).reshape(3, width, each).transpose(0, 2, 1)

    out_slots = out_partial.reshape(inner, n_keys, dim // n_keys)
    out_slots = [
        lax.dynamic_index_in_dim(out_slots, k_index ^ s, 1, False) for s in range(n_keys)
    ]
    out_grad = scatter_media(scatter_keys(out_slots), 0)

    small_rows = -(-(n_frames + 2) // 8) * 8
    patches_grad, small = pl.pallas_call(
        functools.partial(patch_back_kernel, frames, n_frames),
        name="patch_back",
        grid_spec=pltpu.PrefetchScalarGridSpec(
            num_scalar_prefetch=1,
            grid=(media,),
            in_specs=[
                pl.BlockSpec((2 * inner, key_rows), lambda i, *_: (0, i)),
                patch_block,
                time_block,
                whole((1, dim)),
                whole((dim, inner)),
                whole((dim, inner)),
            ],
            out_specs=[patch_block, whole((small_rows, dim))],
        ),
        out_shape=(struct(patches.shape, bf16), struct((small_rows, dim), f32)),
        compiler_params=params(40),
        cost_estimate=cost(patch_flops, 8 * media * key_rows * dim),
    )(scalars, kv_t, patches, time_blocks, row(media_gain), key_weight, value_weight)

    latents_grad, lat_gain_grad, lat_bias_grad = pl.pallas_call(
        functools.partial(latent_back_kernel, n_keys),
        name="latent_back",
        out_shape=(struct((rows, dim), f32), struct((1, dim), f32), struct((1, dim), f32)),
        compiler_params=params(24),
        cost_estimate=cost(6 * rows * dim * inner, 6 * dim * inner + 20 * rows * dim),
    )(
        lat,
        row(latent_gain),
        mid_grad,
        kl_grad,
        vl_grad,
        query_weight,
        key_weight,
        value_weight,
        *q_slots,
    )

    early = everywhere(
        jnp.concatenate([ff_gain_grad, ff_bias_grad, lat_gain_grad, lat_bias_grad], 0)
    )
    late = everywhere(small[: n_frames + 2])
    return (
        resampled.reshape(latents.shape),
        patches_grad,
        latents_grad.reshape(latents.shape),
        late[:n_frames],
        late[n_frames],
        late[n_frames + 1],
        early[2],
        early[3],
        early[0],
        early[1],
        w_grads[0],
        w_grads[1],
        w_grads[2],
        out_grad,
        up_grad,
        down_grad,
    )


def solution(mesh):
    split = P("media", "keys", None)
    return jax.shard_map(
        functools.partial(shards, mesh.shape["media"], mesh.shape["keys"]),
        mesh=mesh,
        in_specs=(split, split, P("media")) + (P(),) * 13 + (split,),
        out_specs=(split,) * 3 + (P(),) * 7 + (P("media", "keys"),) * 6,
        check_vma=False,
    )
```

time: 937 us -> 306 us (0.33)
  waiting for transfers between devices: 587 us -> 61.9 us
  matrix products: 146 us -> 0 us
  blocking collectives: 91 us -> 0 us
  Pallas kernels: 0 us -> 83.5 us
  starting transfers between devices: 1.21 us -> 76 us
  other arithmetic: 56.3 us -> 13 us
  local copies, waits for them, and re-layouts: 31.7 us -> 64 us
  between operations: 15.8 us -> 1.71 us
    reduce_scatter x11 -> x0, waiting for transfers between devices: 566 us -> none  [the longest x1 134 us: shards(): lax.psum_scatter(weight_grads[4].astype(jnp.bfloat16), 'media', scatter_d...]
    dot_general x36 -> x0, matrix products: 146 us -> none  [the longest x8 40.8 us: weight_term(): jnp.einsum('mrd,mre->de', left, right, preferred_element_type=jnp.float32)]
    pallas_call x0 -> x10, Pallas kernels: none -> 83.5 us  [the longest x1 17.2 us: shards(): pl.pallas_call(functools.partial(patch_back_kernel, frames, n_frames), na...]
    ppermute x0 -> x71, starting transfers between devices: none -> 76 us  [the longest x31 53.7 us: over_media(): lax.ppermute(value, 'media', [(i, i ^ shift) for i in range(n_media)])]
    psum x3 -> x0, blocking collectives: 63.1 us -> none  [the longest x1 40.4 us: shards(): lax.psum((time_slots, media_gain_grad, media_bias_grad, latent_gain_grad,...]
    ppermute x0 -> x71, waiting for transfers between devices: none -> 61.9 us  [the longest x31 36.9 us: over_media(): lax.ppermute(value, 'media', [(i, i ^ shift) for i in range(n_media)])]
    reduce_sum x12 -> x0, other arithmetic: 35.5 us -> none  [the longest x2 11.8 us: layer_norm(): return shifted * lax.rsqrt(spread + EPS) * gain + bias]
    unnamed x17 -> x0, waiting for transfers between devices: 20.8 us -> none
  transfers between devices with their start and end apart: 14 -> 71, of which waited for: 11 -> 18; matrix products, arithmetic and copies ran while one was open for 13% -> 19% of each run, Pallas kernels for 0% -> 25%
where the time goes in v1:
time: 306 us; the launch traced here: 300 us
  Pallas kernels  83.5 us (27%)
  starting transfers between devices  76 us (25%)
  local copies, waits for them, and re-layouts  64 us (21%)
  waiting for transfers between devices  61.9 us (20%)
  other arithmetic  13 us (4%)
    ppermute x31, starting transfers between devices, over_media(): lax.ppermute(value, 'media', [(i, i ^ shift) for i in range(n_media)])  53.7 us
    ppermute x31, waiting for transfers between devices, over_media(): lax.ppermute(value, 'media', [(i, i ^ shift) for i in range(n_media)])  36.9 us
    unnamed x138, local copies, waits for them, and re-layouts  25.2 us
    ppermute x39, waiting for transfers between devices, over_keys(): return lax.ppermute(value, 'keys', [(i, i ^ shift) for i in range(n_keys)])  25.1 us
    ppermute x39, starting transfers between devices, over_keys(): return lax.ppermute(value, 'keys', [(i, i ^ shift) for i in range(n_keys)])  20.7 us
    pallas_call x1, Pallas kernels, shards(): pl.pallas_call(functools.partial(patch_back_kernel, frames, n_frames), na...  17.2 us
    pallas_call x1, Pallas kernels, shards(): pl.pallas_call(functools.partial(attend_back_kernel, n_keys, frames), nam...  13.3 us
    pallas_call x1, Pallas kernels, shards(): pl.pallas_call(functools.partial(weight_kernel, n_keys), name='projection...  12.6 us
  transfers between devices with their start and end apart: 71, of which 18 were waited for; matrix products, arithmetic and copies ran while one was open for 19% of the time, Pallas kernels for 25%

profile of v1, /device:TPU:0, one launch (start us, length us, event | category | flops | bytes accessed | tf_op | source)
XLA Modules:
  0.0 300.2 jit_solution(10859970885392922394)
XLA Ops:
  15.4 11.5 %patch_project.1 = (bf16[6,512,1024]{2,1,0:T(8,128)(2,1)}, bf16[6,512,512]{2,1,0:T(8,128)(2,1)S(1)}, bf16[6,512,512]{2,1,0:T(8,128)(2,1)S(1)}) custom-call(s32[1]{0:T(128)} %bitcast.scalars, bf16[6,512,1024]{2,1,0:T(8,128)(2,1)} %patches.1, f32[4,2,1024]{2,1,0:T(2,128)S(1)} %reshape.158.refs_1_.time, f32[1,1024]{1,0:T(1,128)S(1)} %bitcast.146, ...), custom_call_target="tpu_custom_call" | custom-call | flops 6442450944 | bytes 37748736 | tf_op jit(solution)/shard_map/patch_project/pallas_call | solution.py:496
  27.0 7.4 %attend.1 = (bf16[96,640]{1,0:T(8,128)(2,1)S(1)}, bf16[96,640]{1,0:T(8,128)(2,1)S(1)}, bf16[96,640]{1,0:T(8,128)(2,1)S(1)}, bf16[96,640]{1,0:T(8,128)(2,1)S(1)}) custom-call(s32[1]{0:T(128)} %bitcast.scalars, s32[6]{0:T(128)S(1)} %copy-done.46, bf16[96,512]{1,0:T(8,128)(2,1)S(1)} %get-tuple-element.53.refs_0_, ...), custom_call_target="tpu_custom_call" | custom-call | flops 1660944384 | bytes 6291456 | tf_op jit(solution)/shard_map/attend/pallas_call | solution.py:524
  44.6 3.4 %copy-done = bf16[4096,1024]{1,0:T(8,128)(2,1)S(1)} copy-done((bf16[4096,1024]{1,0:T(8,128)(2,1)S(1)}, bf16[4096,1024]{1,0:T(8,128)(2,1)}, u32[]{:S(2)}) %copy-start) | copy-done | bytes 8388632
  48.0 12.0 %feed_forward.1 = (f32[96,1024]{1,0:T(8,128)}, f32[96,1024]{1,0:T(8,128)S(1)}, bf16[96,640]{1,0:T(8,128)(2,1)}, f32[1,1024]{1,0:T(1,128)S(1)}, f32[1,1024]{1,0:T(1,128)S(1)}, /*index=5*/bf16[512,1024]{1,0:T(8,128)(2,1)S(1)}) custom-call(s32[1]{0:T(128)} %bitcast.scalars, f32[96,512]{1,0:T(8,128)S(1)} %get-tuple-element.62.attended, ...), custom_call_target="tpu_custom_call" | custom-call | flops 3221225472 | bytes 19136512 | tf_op jit(solution)/shard_map/feed_forward/pallas_call | solution.py:557
  66.8 4.7 %constant_dynamic-slice_fusion.13 = (bf16[512,1,256]{2,1,0:T(2,128)(2,1)S(1)}, bf16[512,1,256]{2,1,0:T(2,128)(2,1)S(1)}, bf16[512,1,256]{2,1,0:T(2,128)(2,1)S(1)}, bf16[512,1,256]{2,1,0:T(2,128)(2,1)S(1)}) fusion(bf16[512,4,256]{2,1,0:T(4,128)(2,1)} %reshape.166, s32[]{:T(128)S(6)} %select_n.80, s32[]{:T(128)S(6)} %select_n.82, s32[]{:T(128)S(6)} %select_n.81, ...), kind=kLoop, calls=%fused_computation.76 | loop fusion | bytes 2097168 | tf_op jit(solution)/shard_map/jit(dynamic_index_in_dim)/dynamic_slice | solution.py:736
  75.0 13.3 %attend_back.1 = (bf16[1024,3072]{1,0:T(8,128)(2,1)S(1)}, bf16[96,512]{1,0:T(8,128)(2,1)S(1)}, bf16[96,512]{1,0:T(8,128)(2,1)S(1)}, bf16[96,512]{1,0:T(8,128)(2,...) custom-call(s32[1]{0:T(128)} %bitcast.scalars, s32[6]{0:T(128)S(1)} %copy-done.46, ...), custom_call_target="tpu_custom_call" | custom-call | flops 4152360960 | bytes 12582912 | tf_op jit(solution)/shard_map/attend_back/pallas_call | solution.py:659
  88.4 17.2 %patch_back.1 = (bf16[6,512,1024]{2,1,0:T(8,128)(2,1)}, f32[16,1024]{1,0:T(8,128)S(1)}) custom-call(s32[1]{0:T(128)} %bitcast.scalars, bf16[1024,3072]{1,0:T(8,128)(2,1)S(1)} %get-tuple-element.70.kv_t.k_t.v_t, bf16[6,512,1024]{2,1,0:T(8,128)(2,1)} %patches.1, f32[4,2,1024]{2,1,0:T(2,128)S(1)} %copy-done.40, f32[1,1024]{1,0:T(1,128)S(1)} %bitcast.147, ...), custom_call_target="tpu_custom_call" | custom-call | flops 6442450944 | bytes 25165824 | tf_op jit(solution)/shard_map/patch_back/pallas_call | solution.py:741
  113.0 12.6 %projection_weights.1 = bf16[4,384,1024]{2,1,0:T(8,128)(2,1)S(1)} custom-call(s32[1]{0:T(128)} %bitcast.scalars, bf16[1024,3072]{1,0:T(8,128)(2,1)} %copy-done.49, bf16[1024,3072]{1,0:T(8,128)(2,1)} %copy-done.49, bf16[3072,1024]{1,0:T(8,128)(2,1)} %bitcast.165, bf16[96,512]{1,0:T(8,128)(2,1)S(1)} %get-tuple-element.73.kl_g.kl_t, ...), custom_call_target="tpu_custom_call" | custom-call | flops 6442450944 | bytes 12582912 | tf_op jit(solution)/shard_map/projection_weights/pallas_call | solution.py:699
  127.4 3.7 %collective-permute-start.17 = (f32[10,1024]{1,0:T(8,128)S(1)}, f32[10,1024]{1,0:T(8,128)S(1)}, u32[]{:S(2)}, u32[]{:S(2)}) collective-permute-start(f32[10,1024]{1,0:T(8,128)S(1)} %bitcast.137), channel_id=1, source_target_pairs={{0,24},{4,28},{8,16},{12,20},{16,8},{20,12},{24,0},{28,4},{1,25},{... | collective-permute-start | bytes 122888 | tf_op jit(solution)/shard_map/ppermute | solution.py:427
  146.6 3.2 %collective-permute-start.24 = (f32[4,1024]{1,0:T(4,128)S(1)}, f32[4,1024]{1,0:T(4,128)S(1)}, u32[]{:S(2)}, u32[]{:S(2)}) collective-permute-start(f32[4,1024]{1,0:T(4,128)S(1)} %pad_maximum_fusion), channel_id=1, source_target_pairs={{0,12},{4,8},{8,4},{12,0},{16,28},{20,24},{24,20},{28,16},{1,13},{... | collective-permute-start | bytes 49160 | tf_op jit(solution)/shard_map/ppermute | solution.py:427
  152.5 3.7 %collective-permute-start.27 = (f32[4,1024]{1,0:T(4,128)S(1)}, f32[4,1024]{1,0:T(4,128)S(1)}, u32[]{:S(2)}, u32[]{:S(2)}) collective-permute-start(f32[4,1024]{1,0:T(4,128)S(1)} %pad_maximum_fusion), channel_id=1, source_target_pairs={{0,24},{4,28},{8,16},{12,20},{16,8},{20,12},{24,0},{28,4},{1,25},{... | collective-permute-start | bytes 49160 | tf_op jit(solution)/shard_map/ppermute | solution.py:427
  171.0 4.2 %collective-permute-done.52.refs_4_ = bf16[96,1024]{1,0:T(8,128)(2,1)S(1)} collective-permute-done((bf16[96,1024]{1,0:T(8,128)(2,1)S(1)}, bf16[96,1024]{1,0:T(8,128)(2,1)S(1)}, u32[]{:S(2)}, u32[]{:S(2)}) %collective-permute-start.52) | collective-permute-done | bytes 196640 | tf_op jit(solution)/shard_map/ppermute | solution.py:427
  177.6 7.5 %collective-permute-done.54.refs_6_ = bf16[96,1024]{1,0:T(8,128)(2,1)S(1)} collective-permute-done((bf16[96,1024]{1,0:T(8,128)(2,1)S(1)}, bf16[96,1024]{1,0:T(8,128)(2,1)S(1)}, u32[]{:S(2)}, u32[]{:S(2)}) %collective-permute-start.54) | collective-permute-done | bytes 196640 | tf_op jit(solution)/shard_map/ppermute | solution.py:424
  188.3 5.0 %feed_forward_weights.1 = (bf16[512,1024]{1,0:T(8,128)(2,1)S(1)}, bf16[512,1024]{1,0:T(8,128)(2,1)S(1)}) custom-call(s32[1]{0:T(128)} %bitcast.45.s, bf16[96,1024]{1,0:T(8,128)(2,1)S(1)} %copy-done.24, bf16[96,1024]{1,0:T(8,128)(2,1)S(1)} %collective-permute-done.49.refs_1_, bf16[96,1024]{1,0:T(8,128)(2,1)S(1)} %collective-permute-done.50.refs_2_, ...), custom_call_target="tpu_custom_call" | custom-call | flops 3221225472 | bytes 7340032 | tf_op jit(solution)/shard_map/feed_forward_weights/pallas_call | solution.py:615
  195.4 11.3 %reshape.171 = bf16[1,512,4,256]{3,2,1,0:T(4,128)(2,1)} reshape(bf16[512,1024]{1,0:T(8,128)(2,1)} %copy-done.19) | data formatting | bytes 2097152 | tf_op jit(solution)/shard_map/reshape | solution.py:646
  209.6 3.3 %constant_dynamic-slice_fusion.3 = (bf16[1,512,1,256]{3,2,1,0:T(2,128)(2,1)}, bf16[1,512,1,256]{3,2,1,0:T(2,128)(2,1)}, bf16[1,512,1,256]{3,2,1,0:T(2,128)(2,1)}, bf16[1,512,1,256]{3,2,1,0:T(2,128)(2,1)}) fusion(bf16[1,512,4,256]{3,2,1,0:T(4,128)(2,1)S(1)} %copy-done.50, s32[]{:T(128)S(6)} %select_n.76, s32[]{:T(128)S(6)} %select_n.78, s32[]{:T(128)S(6)} %select_n.77, ...), kind=kLoop, calls=%fused_computation.66 | loop fusion | bytes 2097168 | tf_op jit(solution)/shard_map/dynamic-slice.12
  216.7 4.2 %collective-permute-start.47 = (bf16[64,256]{1,0:T(8,128)(2,1)S(1)}, bf16[64,256]{1,0:T(8,128)(2,1)S(1)}, u32[]{:S(2)}, u32[]{:S(2)}) collective-permute-start(bf16[64,256]{1,0:T(8,128)(2,1)S(1)} %get-tuple-element.132), channel_id=1, source_target_pairs={{0,16},{4,20},{8,24},{12,28},{16,0},{20,4},{24,8},{28,12},{1,17},{... | collective-permute-start | bytes 98312 | tf_op jit(solution)/shard_map/ppermute | solution.py:427
  221.1 5.5 %constant_dynamic-slice_fusion.9 = (bf16[512,1,256]{2,1,0:T(2,128)(2,1)}, bf16[512,1,256]{2,1,0:T(2,128)(2,1)S(1)}, bf16[512,1,256]{2,1,0:T(2,128)(2,1)S(1)}, bf16[512,1,256]{2,1,0:T(2,128)(2,1)S(1)}) fusion(bf16[512,4,256]{2,1,0:T(4,128)(2,1)} %reshape.169, s32[]{:T(128)S(6)} %select_n.76, s32[]{:T(128)S(6)} %select_n.78, s32[]{:T(128)S(6)} %select_n.77, ...), kind=kLoop, calls=%fused_computation.72 | loop fusion | bytes 2097168 | tf_op jit(solution)/shard_map/dynamic-slice.4
  230.8 3.8 %collective-permute-start.68 = (bf16[512,256]{1,0:T(8,128)(2,1)}, bf16[512,256]{1,0:T(8,128)(2,1)}, u32[]{:S(2)}, u32[]{:S(2)}) collective-permute-start(bf16[512,256]{1,0:T(8,128)(2,1)} %bitcast.115), channel_id=1, source_target_pairs={{0,16},{4,20},{8,24},{12,28},{16,0},{20,4},{24,8},{28,12},{1,17},{... | collective-permute-start | bytes 786440 | tf_op jit(solution)/shard_map/ppermute | solution.py:427
  235.9 3.8 %collective-permute-start.64 = (bf16[512,256]{1,0:T(8,128)(2,1)}, bf16[512,256]{1,0:T(8,128)(2,1)}, u32[]{:S(2)}, u32[]{:S(2)}) collective-permute-start(bf16[512,256]{1,0:T(8,128)(2,1)} %bitcast.118), channel_id=1, source_target_pairs={{0,16},{4,20},{8,24},{12,28},{16,0},{20,4},{24,8},{28,12},{1,17},{... | collective-permute-start | bytes 786440 | tf_op jit(solution)/shard_map/ppermute | solution.py:427
  245.4 4.9 %collective-permute-start.65 = (bf16[512,256]{1,0:T(8,128)(2,1)S(1)}, bf16[512,256]{1,0:T(8,128)(2,1)S(1)}, u32[]{:S(2)}, u32[]{:S(2)}) collective-permute-start(bf16[512,256]{1,0:T(8,128)(2,1)S(1)} %bitcast.155), channel_id=1, source_target_pairs={{0,24},{4,28},{8,16},{12,20},{16,8},{20,12},{24,0},{28,4},{1,25},{... | collective-permute-start | bytes 786440 | tf_op jit(solution)/shard_map/ppermute | solution.py:427
  257.5 24.0 %collective-permute-done.64 = bf16[512,256]{1,0:T(8,128)(2,1)} collective-permute-done((bf16[512,256]{1,0:T(8,128)(2,1)}, bf16[512,256]{1,0:T(8,128)(2,1)}, u32[]{:S(2)}, u32[]{:S(2)}) %collective-permute-start.64) | collective-permute-done | bytes 262176 | tf_op jit(solution)/shard_map/ppermute | solution.py:427
  284.3 6.1 %collective-permute-start.39 = (bf16[384,128]{1,0:T(8,128)(2,1)S(1)}, bf16[384,128]{1,0:T(8,128)(2,1)S(1)}, u32[]{:S(2)}, u32[]{:S(2)}) collective-permute-start(bf16[384,128]{1,0:T(8,128)(2,1)S(1)} %get-tuple-element.122), channel_id=1, source_target_pairs={{0,8},{4,12},{8,0},{12,4},{16,24},{20,28},{24,16},{28,20},{1,9},{5... | collective-permute-start | bytes 294920 | tf_op jit(solution)/shard_map/ppermute | solution.py:427
  294.6 3.1 %collective-permute-done.40 = bf16[384,128]{1,0:T(8,128)(2,1)S(1)} collective-permute-done((bf16[384,128]{1,0:T(8,128)(2,1)S(1)}, bf16[384,128]{1,0:T(8,128)(2,1)S(1)}, u32[]{:S(2)}, u32[]{:S(2)}) %collective-permute-start.40) | collective-permute-done | bytes 98336 | tf_op jit(solution)/shard_map/ppermute | solution.py:427
  (306 shorter events, 119.3 us)
Async XLA Ops:
  12.5 14.3 %collective-permute-start = (bf16[96,512]{1,0:T(8,128)(2,1)S(1)}, bf16[96,512]{1,0:T(8,128)(2,1)S(1)}, u32[]{:S(2)}, u32[]{:S(2)}) collective-permute-start(bf16[96,512]{1,0:T(8,128)(2,1)S(1)} %get-tuple-element.53.refs_0_), channel_id=1, source_target_pairs={{0,1},{1,0},{2,3},{3,2},{4,5},{5,4},{6,7},{7,6},{8,9},{9,8},{10,11... | collective-permute-start | bytes 294920 | tf_op jit(solution)/shard_map/ppermute | solution.py:424
  36.8 25.9 %collective-permute-start.33 = (bf16[96,1024]{1,0:T(8,128)(2,1)}, bf16[96,1024]{1,0:T(8,128)(2,1)}, u32[]{:S(2)}, u32[]{:S(2)}) collective-permute-start(bf16[96,1024]{1,0:T(8,128)(2,1)} %get-tuple-element.86.lat_low.refs_4_), channel_id=1, source_target_pairs={{0,2},{1,3},{2,0},{3,1},{4,6},{5,7},{6,4},{7,5},{8,10},{9,11},{10,... | collective-permute-start | bytes 589832 | tf_op jit(solution)/shard_map/ppermute | solution.py:424
  61.5 47.5 %collective-permute-start.32 = (bf16[96,1024]{1,0:T(8,128)(2,1)}, bf16[96,1024]{1,0:T(8,128)(2,1)}, u32[]{:S(2)}, u32[]{:S(2)}) collective-permute-start(bf16[96,1024]{1,0:T(8,128)(2,1)} %get-tuple-element.86.lat_low.refs_4_), channel_id=1, source_target_pairs={{0,1},{1,0},{2,3},{3,2},{4,5},{5,4},{6,7},{7,6},{8,9},{9,8},{10,11... | collective-permute-start | bytes 589832 | tf_op jit(solution)/shard_map/ppermute | solution.py:424
  62.8 49.0 %collective-permute-start.34 = (bf16[96,1024]{1,0:T(8,128)(2,1)}, bf16[96,1024]{1,0:T(8,128)(2,1)}, u32[]{:S(2)}, u32[]{:S(2)}) collective-permute-start(bf16[96,1024]{1,0:T(8,128)(2,1)} %collective-permute-done.33.refs_6_), channel_id=1, source_target_pairs={{0,1},{1,0},{2,3},{3,2},{4,5},{5,4},{6,7},{7,6},{8,9},{9,8},{10,11... | collective-permute-start | bytes 589832 | tf_op jit(solution)/shard_map/ppermute | solution.py:424
  105.5 21.9 %collective-permute-start.12 = (f32[10,1024]{1,0:T(8,128)S(1)}, f32[10,1024]{1,0:T(8,128)S(1)}, u32[]{:S(2)}, u32[]{:S(2)}) collective-permute-start(f32[10,1024]{1,0:T(8,128)S(1)} %bitcast.132), channel_id=1, source_target_pairs={{0,4},{4,0},{8,12},{12,8},{16,20},{20,16},{24,28},{28,24},{1,5},{5... | collective-permute-start | bytes 122888 | tf_op jit(solution)/shard_map/ppermute | solution.py:427
  107.2 23.9 %collective-permute-start.13 = (f32[10,1024]{1,0:T(8,128)S(1)}, f32[10,1024]{1,0:T(8,128)S(1)}, u32[]{:S(2)}, u32[]{:S(2)}) collective-permute-start(f32[10,1024]{1,0:T(8,128)S(1)} %bitcast.133), channel_id=1, source_target_pairs={{0,8},{4,12},{8,0},{12,4},{16,24},{20,28},{24,16},{28,20},{1,9},{5... | collective-permute-start | bytes 122888 | tf_op jit(solution)/shard_map/ppermute | solution.py:427
  108.7 25.1 %collective-permute-start.14 = (f32[10,1024]{1,0:T(8,128)S(1)}, f32[10,1024]{1,0:T(8,128)}, u32[]{:S(2)}, u32[]{:S(2)}) collective-permute-start(f32[10,1024]{1,0:T(8,128)S(1)} %bitcast.134), channel_id=1, source_target_pairs={{0,12},{4,8},{8,4},{12,0},{16,28},{20,24},{24,20},{28,16},{1,13},{... | collective-permute-start | bytes 122888 | tf_op jit(solution)/shard_map/ppermute | solution.py:427
  109.0 26.5 %collective-permute-start.15 = (f32[10,1024]{1,0:T(8,128)S(1)}, f32[10,1024]{1,0:T(8,128)}, u32[]{:S(2)}, u32[]{:S(2)}) collective-permute-start(f32[10,1024]{1,0:T(8,128)S(1)} %bitcast.135), channel_id=1, source_target_pairs={{0,16},{4,20},{8,24},{12,28},{16,0},{20,4},{24,8},{28,12},{1,17},{... | collective-permute-start | bytes 122888 | tf_op jit(solution)/shard_map/ppermute | solution.py:427
  111.8 23.7 %collective-permute-start.16 = (f32[10,1024]{1,0:T(8,128)S(1)}, f32[10,1024]{1,0:T(8,128)}, u32[]{:S(2)}, u32[]{:S(2)}) collective-permute-start(f32[10,1024]{1,0:T(8,128)S(1)} %bitcast.136), channel_id=1, source_target_pairs={{0,20},{4,16},{8,28},{12,24},{16,4},{20,0},{24,12},{28,8},{1,21},{... | collective-permute-start | bytes 122888 | tf_op jit(solution)/shard_map/ppermute | solution.py:427
  169.4 15.8 %collective-permute-start.44 = (bf16[512,256]{1,0:T(8,128)(2,1)S(1)}, bf16[512,256]{1,0:T(8,128)(2,1)S(1)}, u32[]{:S(2)}, u32[]{:S(2)}) collective-permute-start(bf16[512,256]{1,0:T(8,128)(2,1)S(1)} %fusion.10), channel_id=1, source_target_pairs={{0,2},{1,3},{2,0},{3,1},{4,6},{5,7},{6,4},{7,5},{8,10},{9,11},{10,... | collective-permute-start | bytes 786440 | tf_op jit(solution)/shard_map/ppermute | solution.py:424
  176.4 30.3 %collective-permute-start.36 = (bf16[384,1024]{1,0:T(8,128)(2,1)}, bf16[384,1024]{1,0:T(8,128)(2,1)}, u32[]{:S(2)}, u32[]{:S(2)}) collective-permute-start(bf16[384,1024]{1,0:T(8,128)(2,1)} %get-tuple-element.107), channel_id=1, source_target_pairs={{0,1},{1,0},{2,3},{3,2},{4,5},{5,4},{6,7},{7,6},{8,9},{9,8},{10,11... | collective-permute-start | bytes 2359304 | tf_op jit(solution)/shard_map/ppermute | solution.py:424
  185.8 49.7 %collective-permute-start.35 = (bf16[384,1024]{1,0:T(8,128)(2,1)}, bf16[384,1024]{1,0:T(8,128)(2,1)}, u32[]{:S(2)}, u32[]{:S(2)}) collective-permute-start(bf16[384,1024]{1,0:T(8,128)(2,1)} %get-tuple-element.106), channel_id=1, source_target_pairs={{0,1},{1,0},{2,3},{3,2},{4,5},{5,4},{6,7},{7,6},{8,9},{9,8},{10,11... | collective-permute-start | bytes 2359304 | tf_op jit(solution)/shard_map/ppermute | solution.py:424
  186.6 29.0 %collective-permute-start.45 = (bf16[4,64,256]{2,1,0:T(8,128)(2,1)S(1)}, bf16[4,64,256]{2,1,0:T(8,128)(2,1)}, u32[]{:S(2)}, u32[]{:S(2)}) collective-permute-start(bf16[4,64,256]{2,1,0:T(8,128)(2,1)S(1)} %dynamic-slice_bitcast_fusion), channel_id=1, source_target_pairs={{0,4},{4,0},{8,12},{12,8},{16,20},{20,16},{24,28},{28,24},{1,5},{5... | collective-permute-start | bytes 393224 | tf_op jit(solution)/shard_map/ppermute | solution.py:427
  209.2 26.7 %collective-permute-start.37 = (bf16[384,1024]{1,0:T(8,128)(2,1)}, bf16[384,1024]{1,0:T(8,128)(2,1)}, u32[]{:S(2)}, u32[]{:S(2)}) collective-permute-start(bf16[384,1024]{1,0:T(8,128)(2,1)} %fusion), channel_id=1, source_target_pairs={{0,2},{1,3},{2,0},{3,1},{4,6},{5,7},{6,4},{7,5},{8,10},{9,11},{10,... | collective-permute-start | bytes 2359304 | tf_op jit(solution)/shard_map/ppermute | solution.py:424
  216.7 14.0 %collective-permute-start.47 = (bf16[64,256]{1,0:T(8,128)(2,1)S(1)}, bf16[64,256]{1,0:T(8,128)(2,1)S(1)}, u32[]{:S(2)}, u32[]{:S(2)}) collective-permute-start(bf16[64,256]{1,0:T(8,128)(2,1)S(1)} %get-tuple-element.132), channel_id=1, source_target_pairs={{0,16},{4,20},{8,24},{12,28},{16,0},{20,4},{24,8},{28,12},{1,17},{... | collective-permute-start | bytes 98312 | tf_op jit(solution)/shard_map/ppermute | solution.py:427
  220.9 13.7 %collective-permute-start.48 = (bf16[64,256]{1,0:T(8,128)(2,1)S(1)}, bf16[64,256]{1,0:T(8,128)(2,1)S(1)}, u32[]{:S(2)}, u32[]{:S(2)}) collective-permute-start(bf16[64,256]{1,0:T(8,128)(2,1)S(1)} %get-tuple-element.131), channel_id=1, source_target_pairs={{0,24},{4,28},{8,16},{12,20},{16,8},{20,12},{24,0},{28,4},{1,25},{... | collective-permute-start | bytes 98312 | tf_op jit(solution)/shard_map/ppermute | solution.py:427
  230.4 15.1 %collective-permute-start.67 = (bf16[512,256]{1,0:T(8,128)(2,1)}, bf16[512,256]{1,0:T(8,128)(2,1)}, u32[]{:S(2)}, u32[]{:S(2)}) collective-permute-start(bf16[512,256]{1,0:T(8,128)(2,1)} %bitcast.116), channel_id=1, source_target_pairs={{0,8},{4,12},{8,0},{12,4},{16,24},{20,28},{24,16},{28,20},{1,9},{5... | collective-permute-start | bytes 786440 | tf_op jit(solution)/shard_map/ppermute | solution.py:427
  230.8 22.6 %collective-permute-start.68 = (bf16[512,256]{1,0:T(8,128)(2,1)}, bf16[512,256]{1,0:T(8,128)(2,1)}, u32[]{:S(2)}, u32[]{:S(2)}) collective-permute-start(bf16[512,256]{1,0:T(8,128)(2,1)} %bitcast.115), channel_id=1, source_target_pairs={{0,16},{4,20},{8,24},{12,28},{16,0},{20,4},{24,8},{28,12},{1,17},{... | collective-permute-start | bytes 786440 | tf_op jit(solution)/shard_map/ppermute | solution.py:427
  234.6 19.3 %collective-permute-start.69 = (bf16[512,256]{1,0:T(8,128)(2,1)}, bf16[512,256]{1,0:T(8,128)(2,1)}, u32[]{:S(2)}, u32[]{:S(2)}) collective-permute-start(bf16[512,256]{1,0:T(8,128)(2,1)} %bitcast.114), channel_id=1, source_target_pairs={{0,24},{4,28},{8,16},{12,20},{16,8},{20,12},{24,0},{28,4},{1,25},{... | collective-permute-start | bytes 786440 | tf_op jit(solution)/shard_map/ppermute | solution.py:427
  235.5 22.0 %collective-permute-start.63 = (bf16[512,256]{1,0:T(8,128)(2,1)}, bf16[512,256]{1,0:T(8,128)(2,1)}, u32[]{:S(2)}, u32[]{:S(2)}) collective-permute-start(bf16[512,256]{1,0:T(8,128)(2,1)} %bitcast.119), channel_id=1, source_target_pairs={{0,8},{4,12},{8,0},{12,4},{16,24},{20,28},{24,16},{28,20},{1,9},{5... | collective-permute-start | bytes 786440 | tf_op jit(solution)/shard_map/ppermute | solution.py:427
  235.9 45.6 %collective-permute-start.64 = (bf16[512,256]{1,0:T(8,128)(2,1)}, bf16[512,256]{1,0:T(8,128)(2,1)}, u32[]{:S(2)}, u32[]{:S(2)}) collective-permute-start(bf16[512,256]{1,0:T(8,128)(2,1)} %bitcast.118), channel_id=1, source_target_pairs={{0,16},{4,20},{8,24},{12,28},{16,0},{20,4},{24,8},{28,12},{1,17},{... | collective-permute-start | bytes 786440 | tf_op jit(solution)/shard_map/ppermute | solution.py:427
  245.4 36.1 %collective-permute-start.65 = (bf16[512,256]{1,0:T(8,128)(2,1)S(1)}, bf16[512,256]{1,0:T(8,128)(2,1)S(1)}, u32[]{:S(2)}, u32[]{:S(2)}) collective-permute-start(bf16[512,256]{1,0:T(8,128)(2,1)S(1)} %bitcast.155), channel_id=1, source_target_pairs={{0,24},{4,28},{8,16},{12,20},{16,8},{20,12},{24,0},{28,4},{1,25},{... | collective-permute-start | bytes 786440 | tf_op jit(solution)/shard_map/ppermute | solution.py:427
  253.4 30.8 %collective-permute-start.38 = (bf16[384,4,128]{2,0,1:T(8,128)(2,1)S(1)}, bf16[384,4,128]{2,0,1:T(8,128)(2,1)S(1)}, u32[]{:S(2)}, u32[]{:S(2)}) collective-permute-start(bf16[384,4,128]{2,0,1:T(8,128)(2,1)S(1)} %bitcast.152), channel_id=1, source_target_pairs={{0,4},{4,0},{8,12},{12,8},{16,20},{20,16},{24,28},{28,24},{1,5},{5... | collective-permute-start | bytes 1179656 | tf_op jit(solution)/shard_map/ppermute | solution.py:427
  255.9 37.9 %collective-permute-start.70 = (bf16[512,256]{1,0:T(8,128)(2,1)}, bf16[512,256]{1,0:T(8,128)(2,1)S(1)}, u32[]{:S(2)}, u32[]{:S(2)}) collective-permute-start(bf16[512,256]{1,0:T(8,128)(2,1)} %fusion.6), channel_id=1, source_target_pairs={{0,0},{1,8},{2,16},{3,24},{4,4},{5,12},{6,20},{7,28},{8,1},{9,9},{... | collective-permute-start | bytes 786440 | tf_op jit(solution)/shard_map/ppermute | solution.py:657
  (110 other events, 1173.3 us)

commit v2 on v1

v2 whole, which is shorter than its diff:
```python
import functools

import jax
import jax.numpy as jnp
from jax import lax
from jax.experimental import pallas as pl
from jax.experimental.pallas import tpu as pltpu
from jax.sharding import Mesh, PartitionSpec as P

HEAD = 64
PATCH = 256
GROUP = 256
LANES = 128

VMEM_LIMIT = 60 << 20

EPS = 1e-05
NEG = -1e30
PAIR = 2

f32 = jnp.float32
bf16 = jnp.bfloat16


def mul(left, right, contract=((1,), (0,)), precision=None):
    return lax.dot_general(
        left, right, (contract, ((), ())), precision=precision, preferred_element_type=f32
    )


NN = ((1,), (0,))
NT = ((1,), (1,))
TN = ((0,), (0,))


def norm_parts(values):
    centre = jnp.mean(values, -1, keepdims=True)
    shifted = values - centre
    spread = jnp.mean(shifted * shifted, -1, keepdims=True)
    return centre, lax.rsqrt(spread + EPS), shifted


def norm(values, gain, bias):
    _, scale, shifted = norm_parts(values)
    return shifted * scale * gain + bias


def norm_back(values, gain, grad):
    _, scale, shifted = norm_parts(values)
    unit = shifted * scale
    scaled = grad * gain
    first = jnp.mean(scaled, -1, keepdims=True)
    second = jnp.mean(scaled * unit, -1, keepdims=True)
    back = scale * (scaled - first - unit * second)
    return (
        back,
        jnp.sum(grad * unit, 0, keepdims=True),
        jnp.sum(grad, 0, keepdims=True),
    )


def gelu_parts(hidden):
    cdf = 0.5 * (1.0 + lax.erf(hidden * (2.0**-0.5)))
    pdf = jnp.exp(-0.5 * hidden * hidden) * 0.3989422804014327
    return cdf, cdf + hidden * pdf


def head_mask(rows, width, heads):
    row = lax.broadcasted_iota(jnp.int32, (heads * rows, width), 0) // rows
    col = lax.broadcasted_iota(jnp.int32, (heads * rows, width), 1)
    return row, col


def spread_heads(values):
    heads = values.shape[1] // HEAD
    row, col = head_mask(values.shape[0], values.shape[1], heads)
    return jnp.where(row == col // HEAD, jnp.concatenate([values] * heads, 0), jnp.zeros((), values.dtype))


def fold_heads(values):
    heads = values.shape[1] // HEAD
    rows = values.shape[0] // heads
    row, col = head_mask(rows, values.shape[1], heads)
    kept = jnp.where(row == col // HEAD, values, 0.0)
    total = kept[:rows]
    for h in range(1, heads):
        total = total + kept[h * rows : (h + 1) * rows]
    return total


def three_parts(values, lane, start, slots):
    high = values.astype(bf16).astype(f32)
    rest = values - high
    middle = rest.astype(bf16).astype(f32)
    low = rest - middle
    place = lane // slots - start
    return jnp.where(place == 0, high, jnp.where(place == 1, middle, jnp.where(place == 2, low, 0.0)))


def cost(flops, moved, special=0):
    return pl.CostEstimate(flops=int(flops), bytes_accessed=int(moved), transcendentals=int(special))


def params():
    return pltpu.CompilerParams(vmem_limit_bytes=VMEM_LIMIT)


def tie(*values):
    return lax.optimization_barrier(values)


def latent_kernel(_, lat, gain, bias, cot, wq, rows_o, q_o):
    dim = lat.shape[1]
    low = norm(lat[...], gain[...], bias[...]).astype(bf16)
    rows_o[:, :dim] = low
    rows_o[:, dim:] = cot[...].astype(bf16)
    q_o[...] = mul(low, wq[...]).astype(bf16)


def two_parts(values):
    high = values.astype(bf16)
    return high, (values - high.astype(f32)).astype(bf16)


def patch_kernel(
    frames, scalars, patches, time, gain, bias, wk, wv, lat_low, low_o, k_o, v_o, kl_o, vl_o, stat_o, once_o, vec_o
):
    for f in range(frames):
        rows = pl.ds(f * PATCH, PATCH)
        framed = patches[0, rows, :].astype(f32) + time[0, f : f + 1, :]
        centre, scale, shifted = norm_parts(framed)
        low = (shifted * scale * gain[...] + bias[...]).astype(bf16)
        low_o[0, rows, :] = low
        k_o[0, rows, :] = mul(low, wk[...]).astype(bf16)
        v_o[0, rows, :] = mul(low, wv[...]).astype(bf16)
        lane = lax.broadcasted_iota(jnp.int32, (PATCH, LANES), 1)
        stat = jnp.where(lane == 0, centre, jnp.where(lane == 1, scale, 0.0))
        stat_o[:, f * PATCH : (f + 1) * PATCH] = stat.T[:8]
        high = scale.astype(bf16).astype(f32)
        once = jnp.where(lane == 0, 1.0, jnp.where(lane == 1 + f, high, 0.0))
        once_o[0, rows, :] = jnp.where(lane == 1 + frames + f, scale - high, once).astype(bf16)

    @pl.when(pl.program_id(0) == pl.num_programs(0) - 1)
    def _():
        kl_o[...] = mul(lat_low[...], wk[...]).astype(bf16)
        vl_o[...] = mul(lat_low[...], wv[...]).astype(bf16)
        row = lax.broadcasted_iota(jnp.int32, (16, gain.shape[1]), 0)
        both = jnp.where(row % 2 == 0, gain[...], bias[...])
        high, low = two_parts(both)
        both = jnp.where(row < 2, high.astype(f32), jnp.where(row < 4, low.astype(f32), 0.0)).astype(bf16)
        for i, w in enumerate((wk, wv)):
            term = mul(both, w[...])
            vec_o[:, i * w.shape[1] : (i + 1) * w.shape[1]] = term[:8] + pltpu.roll(term, 14, 0)[:8]


def masked_scores(query, keys, frames, first, count):
    scores = mul(query, keys, NT)
    parts = []
    for f in range(frames):
        part = scores[:, f * PATCH : (f + 1) * PATCH]
        parts.append(jnp.where(first + f < count, part, NEG))
    return jnp.concatenate(parts, 1) if frames > 1 else parts[0]


def attend_kernel(n_keys, frames, scalars, counts, *refs):
    q = refs[:n_keys]
    kp, vp, kl, vl = refs[n_keys : n_keys + 4]
    outs = refs[n_keys + 4 :]
    own = q[0].shape[0]
    inner = q[0].shape[1]
    heads = inner // HEAD
    count = counts[pl.program_id(0)]
    first = scalars[0] * frames
    query = jnp.concatenate([r[...] for r in q], 0)
    rows = query.shape[0]
    stats = jnp.zeros((rows, LANES), f32)
    shares = []
    for g in range(inner // GROUP):
        cols = slice(g * GROUP, (g + 1) * GROUP)
        wide = spread_heads(query[:, cols] * bf16(HEAD**-0.5))
        scores = masked_scores(wide, kp[0, :, cols], frames, first, count)
        lat_scores = mul(wide, kl[:, cols], NT)
        top = jnp.maximum(
            jnp.max(scores, -1, keepdims=True), jnp.max(lat_scores, -1, keepdims=True)
        )
        raw = jnp.exp(scores - top)
        lat_raw = jnp.exp(lat_scores - top)
        total = jnp.sum(raw, -1, keepdims=True) + jnp.sum(lat_raw, -1, keepdims=True)
        share = mul(raw.astype(bf16), vp[0, :, cols]) + mul(lat_raw.astype(bf16), vl[:, cols])
        shares.append(fold_heads(share / total).astype(bf16))
        level = top + jnp.log(total)
        row, lane = head_mask(rows, LANES, GROUP // HEAD)
        kept = jnp.where(lane % heads == row + g * (GROUP // HEAD), level, 0.0)
        for h in range(GROUP // HEAD):
            stats = stats + kept[h * rows : (h + 1) * rows]
    lane = lax.broadcasted_iota(jnp.int32, stats.shape, 1)
    packed = jnp.concatenate(shares + [three_parts(stats, lane, 0, heads).astype(bf16)], 1)
    for s in range(n_keys):
        outs[s][...] = packed[s * own : (s + 1) * own]


def sum_runs(stats, heads, start):
    total = None
    for part in range(3):
        shift = (-(start + part) * heads) % LANES
        term = pltpu.roll(stats, shift, 1) if shift else stats
        total = term if total is None else total + term
    return total


def join_kernel(n_keys, _, latents, gain, bias, wo, *refs):
    slots = refs[:n_keys]
    att_o, low_o, mid_o, ff_o, lse_o = refs[n_keys:]
    inner = att_o.shape[1]
    heads = inner // HEAD
    levels = [sum_runs(r[:, inner:].astype(f32), heads, 0) for r in slots]
    top = functools.reduce(jnp.maximum, levels)
    weights = [jnp.exp(v - top) for v in levels]
    total = functools.reduce(jnp.add, weights)
    inverse = 1.0 / total
    lane = lax.broadcasted_iota(jnp.int32, (LANES, inner), 0)
    col = lax.broadcasted_iota(jnp.int32, (LANES, inner), 1)
    select = jnp.where(lane == col // HEAD, 1.0, 0.0)
    attended = None
    for s in range(n_keys):
        wide = mul(weights[s] * inverse, select, NN, lax.Precision.HIGHEST)
        term = wide * slots[s][:, :inner].astype(f32)
        attended = term if attended is None else attended + term
    low = attended.astype(bf16)
    middle = latents[...] + mul(low, wo[...])
    att_o[...] = attended
    low_o[...] = low
    mid_o[...] = middle
    ff_o[...] = norm(middle, gain[...], bias[...]).astype(bf16)
    lse_o[...] = top + jnp.log(total)


def forward_kernel(
    n_keys,
    aligned,
    scalars,
    attended,
    att_low,
    middle,
    ff_low,
    lse,
    cot,
    out_low,
    gain,
    wo,
    up,
    down,
    res_o,
    mid_grad_o,
    pack_o,
    small_o,
    wo_grad_o,
    res_acc,
    in_acc,
    wo_acc,
):
    step = pl.program_id(0)

    @pl.when(step == 0)
    def _():
        res_acc[...] = jnp.zeros_like(res_acc)
        in_acc[...] = jnp.zeros_like(in_acc)

    hidden = mul(ff_low[...], up[...])
    act_grad = mul(out_low[...], down[...], NT)
    cdf, slope = gelu_parts(hidden)
    res_acc[...] += mul((hidden * cdf).astype(bf16), down[...])
    in_acc[...] += mul((act_grad * slope).astype(bf16), up[...], NT)

    @pl.when(step == pl.num_programs(0) - 1)
    def _():
        inner = attended.shape[1]
        heads = inner // HEAD
        res_o[...] = middle[...] + res_acc[...]
        back, gain_grad, bias_grad = norm_back(middle[...], gain[...], in_acc[...])
        small_o[0:1, :] = gain_grad
        small_o[1:2, :] = bias_grad
        mid_grad = cot[...] + back
        mid_grad_o[...] = mid_grad
        branch = mid_grad.astype(bf16)
        att_grad = mul(branch, wo[...], NT).astype(bf16)
        col = lax.broadcasted_iota(jnp.int32, (inner, LANES), 0)
        lane = lax.broadcasted_iota(jnp.int32, (inner, LANES), 1)
        select = jnp.where(col // HEAD == lane % heads, 1.0, 0.0)
        delta = mul(attended[...] * att_grad.astype(f32), select, NN, lax.Precision.HIGHEST)
        lane = lax.broadcasted_iota(jnp.int32, delta.shape, 1)
        level = jnp.where(lane < heads, lse[...], 0.0)
        level = level + pltpu.roll(level, heads, 1) + pltpu.roll(level, 2 * heads, 1)
        stats = three_parts(level, lane, 0, heads) + three_parts(delta, lane, 3, heads)
        pack_o[...] = jnp.concatenate([att_grad, stats.astype(bf16)], 1)
        wo_grad = mul(att_low[...], branch, TN)
        if aligned:
            wo_acc[...] = wo_grad
            slot_rows(scalars, wo_acc, wo_grad_o, n_keys)
        else:
            wo_grad_o[...] = wo_grad.astype(bf16)


def slot_rows(scalars, full, out, n_keys):
    lanes = LANES
    n_media = out.shape[2] // lanes
    r = full.shape[0] // n_media
    c = full.shape[1] // n_keys
    for s in range(n_keys):
        owner = (scalars[0] ^ s) * c
        for m in range(n_media):
            place = (scalars[2] ^ (m // PAIR)) * PAIR + m % PAIR
            place = pl.ds(pl.multiple_of(place * lanes, lanes), lanes)
            for h in range(c // lanes):
                start = pl.multiple_of(owner + h * lanes, lanes)
                out[s, h * r : (h + 1) * r, place] = full[
                    m * r : (m + 1) * r, pl.ds(start, lanes)
                ].astype(bf16)


def ff_grad_kernel(aligned, scalars, ff_all, out_all, up, down, grad_o):
    units, dim = down.shape
    hidden = mul(ff_all[...], up[...])
    act_grad = mul(out_all[...], down[...], NT)
    cdf, slope = gelu_parts(hidden)
    grad_o[units:, :] = mul((hidden * cdf).astype(bf16), out_all[...], TN).astype(bf16)
    up_grad = mul((act_grad * slope).astype(bf16), ff_all[...], TN).astype(bf16)
    if aligned:
        for j in range(dim // LANES):
            place = ((j // PAIR) * PAIR + (scalars[1] ^ (j % PAIR))) * LANES
            grad_o[:units, pl.ds(pl.multiple_of(place, LANES), LANES)] = up_grad[
                :, j * LANES : (j + 1) * LANES
            ]
    else:
        grad_o[:units, :] = up_grad


def attend_back_kernel(n_keys, frames, turn, heads, scalars, counts, *refs):
    q = refs[:n_keys]
    grads = refs[n_keys : 2 * n_keys]
    stat = refs[2 * n_keys : 3 * n_keys]
    kp, vp, kl, vl, k_vec, v_vec = refs[3 * n_keys : 3 * n_keys + 6]
    n_out = 4 + n_keys
    kv_t_o, stat_o, kl_o, vl_o = refs[-n_out : -n_keys]
    q_o = refs[-n_keys:]
    q_before = refs[3 * n_keys + 6 : -n_out]
    own = q[0].shape[0]
    per = GROUP // HEAD
    count = counts[pl.program_id(0)]
    first = scalars[0] * frames
    group = scalars[5] ^ (1 - turn)
    query = jnp.concatenate([r[...] for r in q], 0)
    grad = jnp.concatenate([r[...] for r in grads], 0)
    stats = jnp.concatenate([r[...] for r in stat], 0).astype(f32)
    rows = query.shape[0]
    row, lane = head_mask(rows, LANES, per)
    tiled = jnp.concatenate([stats] * per, 0)
    mine = lane % heads == row + group * per
    level = jnp.sum(jnp.where(mine & (lane < 3 * heads), tiled, 0.0), -1, keepdims=True)
    delta = jnp.sum(
        jnp.where(mine & (lane >= 3 * heads) & (lane < 6 * heads), tiled, 0.0), -1, keepdims=True
    )
    wide = spread_heads(query * bf16(HEAD**-0.5))
    wide_grad = spread_heads(grad)
    scores = masked_scores(wide, kp[0], frames, first, count)
    probs = jnp.exp(scores - level)
    prob_grad = mul(wide_grad, vp[0], NT)
    score_grad = probs * (prob_grad - delta)
    along = jnp.sum(score_grad * scores + probs * prob_grad, 0, keepdims=True)
    score_grad = score_grad.astype(bf16)
    key_side = jnp.concatenate([wide, mul(wide, k_vec[...].astype(bf16), NT).astype(bf16)], 1)
    value_side = jnp.concatenate(
        [wide_grad, mul(wide_grad, v_vec[...].astype(bf16), NT).astype(bf16)], 1
    )
    key_t = mul(key_side, score_grad, TN)
    value_t = mul(value_side, probs.astype(bf16), TN)
    kv_t_o[0] = key_t[:GROUP].astype(bf16)
    kv_t_o[1] = value_t[:GROUP].astype(bf16)
    ends = key_t[GROUP:] + value_t[GROUP:]
    line = lax.broadcasted_iota(jnp.int32, ends.shape, 0)
    stat_o[...] = jnp.where(line == 1, along - ends, ends)
    lat_probs = jnp.exp(mul(wide, kl[...], NT) - level)
    lat_prob_grad = mul(wide_grad, vl[...], NT)
    lat_score_grad = (lat_probs * (lat_prob_grad - delta)).astype(bf16)
    kl_o[...] = mul(lat_score_grad, wide, TN).astype(bf16)
    vl_o[...] = mul(lat_probs.astype(bf16), wide_grad, TN).astype(bf16)
    query_grad = mul(score_grad, kp[0]) + mul(lat_score_grad, kl[...])
    query_grad = (fold_heads(query_grad) * HEAD**-0.5).astype(bf16)
    if turn == 0:
        for s in range(n_keys):
            q_o[s][...] = query_grad[s * own : (s + 1) * own]
    else:
        here = pl.ds(pl.multiple_of(group * GROUP, GROUP), GROUP)
        there = pl.ds(pl.multiple_of((1 - group) * GROUP, GROUP), GROUP)
        for s in range(n_keys):
            q_o[s][:, here] = query_grad[s * own : (s + 1) * own]
            q_o[s][:, there] = q_before[s][...]


def weight_kernel(
    n_keys,
    turn,
    width,
    frames,
    aligned,
    scalars,
    kv_t,
    low,
    kl_g,
    vl_g,
    lat_own,
    rows_all,
    wo_g,
    once,
    norm_stat,
    grad_stat,
    wk,
    wv,
    gain,
    bias,
    *refs,
):
    q_grads = refs[:n_keys]
    before = refs[n_keys:-5]
    given, kept, small, total, sums = refs[-5:]
    rows = q_grads[0].shape[0]
    per = GROUP // width
    kv = jnp.concatenate([kv_t[0], kv_t[1]], 0)
    keys = kv.shape[1]

    @pl.when(pl.program_id(0) == 0)
    def _():
        sums[...] = mul(kv, once[...])

    inverse = 1.0 / (scalars[6].astype(f32))
    scale = norm_stat[1:2, :] * inverse
    first = grad_stat[0:1, :] * scale
    second = grad_stat[1:2, :] * scale
    frame = (lax.broadcasted_iota(jnp.int32, (16, keys), 1) // PATCH) % frames
    row = lax.broadcasted_iota(jnp.int32, (16, keys), 0)
    high = second.astype(bf16).astype(f32)
    mine = frame == row % frames
    ends = jnp.where(mine & (row < frames), high, 0.0)
    ends = jnp.where(mine & (row >= frames) & (row < 2 * frames), second - high, ends)
    out = mul(jnp.concatenate([kv, ends.astype(bf16)], 0), low[...])
    main = out[: 2 * GROUP]
    ends = out[2 * GROUP :]
    behind = None
    for part in two_parts(sums[...]):
        for i, w in enumerate((wk, wv)):
            term = mul(part[i * GROUP : (i + 1) * GROUP], w[...], ((0,), (1,)))
            behind = term if behind is None else behind + term
    bias_grad = behind[0:1]
    turned = jnp.concatenate([wk[...].astype(f32).T, wv[...].astype(f32).T], 0)
    over = 1.0 / gain[...]
    gain_grad = (jnp.sum(main * turned, 0, keepdims=True) - bias[...] * bias_grad) * over
    lines = []
    for f in range(frames):
        here = frame[0:1] == f
        first_sum = jnp.sum(jnp.where(here, first, 0.0), -1, keepdims=True)
        second_sum = jnp.sum(jnp.where(here, second, 0.0), -1, keepdims=True)
        along = ends[f : f + 1] + ends[frames + f : frames + f + 1]
        scaled = behind[1 + f : 2 + f] + behind[1 + frames + f : 2 + frames + f]
        lines.append(gain[...] * scaled - first_sum - (along - bias[...] * second_sum) * over)
    for i, line in enumerate(lines + [gain_grad, bias_grad]):
        small[i : i + 1, :] = line + before[0][i : i + 1, :] if turn else line

    kv_lat = jnp.concatenate([kl_g[...], vl_g[...]], 1)
    total[GROUP:, :] = main + mul(kv_lat, lat_own[...], TN)
    base = scalars[1] * n_keys
    query = None
    for s in range(n_keys):
        slot = pl.ds(pl.multiple_of((base + (scalars[0] ^ s)) * rows, 8), rows)
        term = mul(q_grads[s][...], rows_all[slot, :], TN)
        query = term if query is None else query + term
    total[:GROUP, :] = query
    near = scalars[1] if aligned else 0
    lanes = total.shape[1] // PAIR
    for j in range(per):
        out = (given, kept)[j % 2]
        slot = per * (1 - turn) + 2 * (j // 2) + 1 - j % 2
        start = ((scalars[0] ^ slot) % per) * width
        for part in range(3):
            piece = total[pl.ds(pl.multiple_of(part * GROUP + start, width), width), :].astype(bf16)
            for n in range(PAIR):
                out[j // 2, near ^ n, part * width : (part + 1) * width, :] = piece[
                    :, n * lanes : (n + 1) * lanes
                ]
        piece = wo_g[slot]
        for n in range(PAIR):
            out[j // 2, near ^ n, 3 * width :, :] = piece[:, n * lanes : (n + 1) * lanes]


def patch_back_kernel(
    frames, scalars, kv_a, kv_b, stat_a, stat_b, norm_stat, patches, time, gain, wk_a, wv_a, wk_b, wv_b, _, grad_o
):
    turned = ((0,), (1,))
    inverse = 1.0 / gain.shape[1]
    for f in range(frames):
        rows = pl.ds(f * PATCH, PATCH)
        span = slice(f * PATCH, (f + 1) * PATCH)
        scale = norm_stat[1:2, span]
        first = (stat_a[0:1, span] + stat_b[0:1, span]) * inverse
        second = (stat_a[1:2, span] + stat_b[1:2, span]) * inverse
        slope = scale * scale * second
        level = scale * first - norm_stat[0:1, span] * slope
        line = lax.broadcasted_iota(jnp.int32, (8, PATCH), 0)
        columns = jnp.where(line == 0, scale, jnp.where(line == 1, level, slope)).T
        grad = mul(kv_a[0, :, span], wk_a[...], turned)
        grad = grad + mul(kv_a[1, :, span], wv_a[...], turned)
        grad = grad + mul(kv_b[0, :, span], wk_b[...], turned)
        grad = grad + mul(kv_b[1, :, span], wv_b[...], turned)
        framed = patches[0, rows, :].astype(f32) + time[0, f : f + 1, :]
        back = grad * gain[...] * columns[:, 0:1] - columns[:, 1:2] - framed * columns[:, 2:3]
        grad_o[0, rows, :] = back.astype(bf16)


def latent_back_kernel(n_keys, frames, n_frames, scalars, latents, gain, mid_grad, media_small, ff_small, *refs):
    keys = refs[:8]
    wq = refs[8]
    slots = refs[9 : 9 + n_keys]
    lat_o, small_o = refs[9 + n_keys :]
    query = functools.reduce(jnp.add, [r[...].astype(f32) for r in slots]).astype(bf16)
    grad = mul(query, wq[...], NT)
    for i in range(4):
        grad = grad + mul(keys[2 * i][...], keys[2 * i + 1][...], NT)
    back, gain_grad, bias_grad = norm_back(latents[...], gain[...], grad)
    lat_o[...] = mid_grad[...] + back
    small_o[...] = jnp.zeros_like(small_o)
    for f in range(frames):
        small_o[pl.ds(scalars[0] * frames + f, 1), :] = media_small[f : f + 1, :]
    for i, line in enumerate(
        (media_small[frames : frames + 1, :], media_small[frames + 1 : frames + 2, :], gain_grad, bias_grad)
    ):
        small_o[n_frames + i : n_frames + i + 1, :] = line
    small_o[n_frames + 4 : n_frames + 6, :] = ff_small[...]


def finish_kernel(width, scalars, *refs):
    parts = refs[:-4]
    q_o, k_o, v_o, out_o = refs[-4:]
    total = functools.reduce(jnp.add, [r[...].astype(f32) for r in parts])
    for i, ref in enumerate((q_o, k_o, v_o)):
        ref[...] = total[i * width : (i + 1) * width].T
    r = out_o.shape[0]
    for h in range(out_o.shape[1] // LANES):
        out_o[:, h * LANES : (h + 1) * LANES] = total[3 * width + h * r : 3 * width + (h + 1) * r]


def finish_up_kernel(scalars, keep, got, out):
    units = keep.shape[0]
    near = scalars[1]
    own = pl.ds(pl.multiple_of(near * units, LANES), units)
    other = pl.ds(pl.multiple_of((1 - near) * units, LANES), units)
    out[:, own] = keep[...].astype(f32).T
    out[:, other] = got[...].astype(f32).T


def whole(shape):
    return pl.BlockSpec(shape, lambda *_: (0,) * len(shape))


def struct(shape, dtype):
    return jax.ShapeDtypeStruct(shape, dtype)


def shards(
    n_far,
    n_keys,
    latents,
    patches,
    frame_counts,
    time_embedding,
    media_gain,
    media_bias,
    latent_gain,
    latent_bias,
    ff_gain,
    ff_bias,
    query_weight,
    key_weight,
    value_weight,
    out_weight,
    up_weight,
    down_weight,
    cotangent,
):
    media, own, dim = latents.shape
    key_rows = patches.shape[1]
    inner = query_weight.shape[1]
    hidden = up_weight.shape[1]
    frames = key_rows // PATCH
    n_frames = time_embedding.shape[0]
    n_media = n_far * PAIR
    rows = media * own
    all_rows = media * key_rows
    width = inner // n_keys
    each = dim // n_media
    aligned = each == LANES and width % LANES == 0 and n_far == n_keys
    far = lax.axis_index("far")
    near = lax.axis_index("near")
    key = lax.axis_index("keys")
    own_group = key // (n_keys // 2)
    scalars = jnp.stack([key, near, far, far, key * PAIR + near, own_group, jnp.full_like(far, dim)])
    scalars = scalars.astype(jnp.int32)

    def over_keys(value, shift):
        return lax.ppermute(value, "keys", [(i, i ^ shift) for i in range(n_keys)])

    def over_near(value):
        return lax.ppermute(value, "near", [(0, 1), (1, 0)])

    def over_far(value, shift):
        return lax.ppermute(value, "far", [(i, i ^ shift) for i in range(n_far)])

    def exchange_keys(slots):
        return [slots[0]] + [over_keys(slots[s], s) for s in range(1, n_keys)]

    def gather_keys(value):
        slots = [None] * n_keys
        for s in range(0, n_keys, 2):
            slots[s] = value if s == 0 else over_keys(value, s)
        for s in range(0, n_keys, 2):
            slots[s + 1] = over_keys(slots[s], 1)
        return slots

    def add(left, right):
        return (left.astype(f32) + right.astype(f32)).astype(bf16)

    lat = latents.reshape(rows, dim)
    cot = cotangent.reshape(rows, dim)
    row = lambda v: v.reshape(1, dim)
    time_blocks = time_embedding.reshape(n_keys, frames, dim)
    packed = inner + LANES
    own_block = lambda w: pl.BlockSpec((own, w), lambda i, *_: (i, 0))
    patch_block = pl.BlockSpec((1, key_rows, dim), lambda i, *_: (i, 0, 0))
    inner_block = pl.BlockSpec((1, key_rows, inner), lambda i, *_: (i, 0, 0))
    time_block = pl.BlockSpec((1, frames, dim), lambda i, s, *_: (s[0], 0, 0))
    stat_block = pl.BlockSpec((8, key_rows), lambda i, *_: (0, i))
    patch_flops = 4 * all_rows * dim * inner
    att_flops = 4 * media * n_keys * own * (key_rows + own) * inner * (GROUP // HEAD)

    def call(kernel, name, grid, in_specs, out_specs, out_shape, price, prefetch=1, **more):
        run = pl.pallas_call(
            kernel,
            name=name,
            grid_spec=pltpu.PrefetchScalarGridSpec(
                num_scalar_prefetch=prefetch,
                grid=grid,
                in_specs=in_specs,
                out_specs=out_specs,
                scratch_shapes=more.pop("scratch_shapes", ()),
            ),
            out_shape=out_shape,
            compiler_params=params(),
            cost_estimate=price,
            **more,
        )

        def pinned(*args):
            args = list(args)
            for i in range(prefetch, len(args)):
                if in_specs[i - prefetch].memory_space is None:
                    args[i] = pltpu.with_memory_space_constraint(args[i], pltpu.HBM)
            return run(*args)

        return pinned

    own_rows, q_own = call(
        latent_kernel,
        "latent_project",
        (1,),
        [whole((rows, dim)), whole((1, dim)), whole((1, dim)), whole((rows, dim)), whole((dim, inner))],
        [whole((rows, 2 * dim)), whole((rows, inner))],
        (struct((rows, 2 * dim), bf16), struct((rows, inner), bf16)),
        cost(2 * rows * dim * inner, 2 * dim * inner + 14 * rows * dim),
    )(scalars, lat, row(latent_gain), row(latent_bias), cot, query_weight)
    q_all = exchange_keys([q_own] * n_keys)
    rows_all = lax.all_gather(own_rows, ("near", "keys"), axis=0, tiled=True)

    media_low, kp, vp, kl, vl, norm_stat, once, norm_vec = call(
        functools.partial(patch_kernel, frames),
        "patch_project",
        (media,),
        [
            patch_block,
            time_block,
            whole((1, dim)),
            whole((1, dim)),
            whole((dim, inner)),
            whole((dim, inner)),
            whole((rows, dim)),
        ],
        [
            patch_block,
            inner_block,
            inner_block,
            whole((rows, inner)),
            whole((rows, inner)),
            stat_block,
            pl.BlockSpec((1, key_rows, LANES), lambda i, *_: (i, 0, 0)),
            whole((8, 2 * inner)),
        ],
        (
            struct(patches.shape, bf16),
            struct((media, key_rows, inner), bf16),
            struct((media, key_rows, inner), bf16),
            struct((rows, inner), bf16),
            struct((rows, inner), bf16),
            struct((8, all_rows), f32),
            struct((media, key_rows, LANES), bf16),
            struct((8, 2 * inner), f32),
        ),
        cost(patch_flops, 12 * all_rows * dim),
    )(
        scalars,
        patches,
        time_blocks,
        row(media_gain),
        row(media_bias),
        key_weight,
        value_weight,
        own_rows,
    )

    shares = call(
        functools.partial(attend_kernel, n_keys, frames),
        "attend",
        (media,),
        [own_block(inner)] * n_keys
        + [inner_block, inner_block, own_block(inner), own_block(inner)],
        [own_block(packed)] * n_keys,
        [struct((rows, packed), bf16)] * n_keys,
        cost(att_flops, 4 * all_rows * inner),
        prefetch=2,
    )(scalars, frame_counts, *q_all, kp, vp, kl, vl)
    joined = exchange_keys(shares)

    attended, att_low, middle, ff_low, lse = call(
        functools.partial(join_kernel, n_keys),
        "join",
        (1,),
        [whole((rows, dim)), whole((1, dim)), whole((1, dim)), whole((inner, dim))]
        + [whole((rows, packed))] * n_keys,
        [
            whole((rows, inner)),
            whole((rows, inner)),
            whole((rows, dim)),
            whole((rows, dim)),
            whole((rows, LANES)),
        ],
        (
            struct((rows, inner), f32),
            struct((rows, inner), bf16),
            struct((rows, dim), f32),
            struct((rows, dim), bf16),
            struct((rows, LANES), f32),
        ),
        cost(2 * rows * inner * dim, 2 * inner * dim + 16 * rows * dim),
    )(scalars, lat, row(ff_gain), row(ff_bias), out_weight, *joined)
    ff_all = lax.all_gather(ff_low, ("near", "keys"), axis=0, tiled=True)

    chunk = min(512, hidden)
    wo_rows = inner * dim // n_keys // dim
    wo_shape = (n_keys, wo_rows, dim) if aligned else (inner, dim)
    resampled, mid_grad, pack, ff_small, out_slots = call(
        functools.partial(forward_kernel, n_keys, aligned),
        "feed_forward",
        (hidden // chunk,),
        [
            whole((rows, inner)),
            whole((rows, inner)),
            whole((rows, dim)),
            whole((rows, dim)),
            whole((rows, LANES)),
            whole((rows, dim)),
            pl.BlockSpec((rows, dim), lambda i, *_: (0, 1)),
            whole((1, dim)),
            whole((inner, dim)),
            pl.BlockSpec((dim, chunk), lambda i, *_: (0, i)),
            pl.BlockSpec((chunk, dim), lambda i, *_: (i, 0)),
        ],
        [
            whole((rows, dim)),
            whole((rows, dim)),
            whole((rows, packed)),
            whole((2, dim)),
            whole(wo_shape),
        ],
        (
            struct((rows, dim), f32),
            struct((rows, dim), f32),
            struct((rows, packed), bf16),
            struct((2, dim), f32),
            struct(wo_shape, bf16),
        ),
        cost(8 * rows * dim * hidden, 4 * dim * hidden + 24 * rows * dim),
        scratch_shapes=[
            pltpu.VMEM((rows, dim), f32),
            pltpu.VMEM((rows, dim), f32),
            pltpu.VMEM((inner, dim) if aligned else (8, LANES), f32),
        ],
    )(
        scalars,
        attended,
        att_low,
        middle,
        ff_low,
        lse,
        cot,
        own_rows,
        row(ff_gain),
        out_weight,
        up_weight,
        down_weight,
    )
    if not aligned:
        c = dim // n_keys
        out_slots = out_slots.reshape(n_media, inner // n_media, n_keys, c // each, each)
        out_slots = out_slots.transpose(2, 3, 1, 0, 4).reshape(n_keys, wo_rows, dim)
        out_slots = jnp.stack(
            [lax.dynamic_index_in_dim(out_slots, key ^ s, 0, False) for s in range(n_keys)]
        )
    packs = gather_keys(pack)

    half_keys = n_keys // 2
    pick = lambda turn: (lambda s: s[5] ^ (1 - turn))
    high = 3 * width + wo_rows

    def attend_back(turn, packs, before):
        g = pick(turn)
        own_cols = pl.BlockSpec((own, GROUP), lambda i, s, *_: (i, g(s)))
        stat_cols = pl.BlockSpec((own, LANES), lambda i, *_: (i, inner // LANES))
        key_cols = pl.BlockSpec((1, key_rows, GROUP), lambda i, s, *_: (i, 0, g(s)))
        q_width = GROUP if turn == 0 else inner
        out = call(
            functools.partial(attend_back_kernel, n_keys, frames, turn, inner // HEAD),
            "attend_back",
            (media,),
            [own_cols] * (2 * n_keys)
            + [stat_cols] * n_keys
            + [key_cols, key_cols, own_cols, own_cols]
            + [
                pl.BlockSpec((8, GROUP), lambda i, s, *_: (0, g(s))),
                pl.BlockSpec((8, GROUP), lambda i, s, *_: (0, inner // GROUP + g(s))),
            ]
            + [own_block(GROUP)] * len(before),
            [
                pl.BlockSpec((2, GROUP, key_rows), lambda i, *_: (0, 0, i)),
                stat_block,
                own_block(GROUP),
                own_block(GROUP),
            ]
            + [own_block(q_width)] * n_keys,
            [
                struct((2, GROUP, all_rows), bf16),
                struct((8, all_rows), f32),
                struct((rows, GROUP), bf16),
                struct((rows, GROUP), bf16),
            ]
            + [struct((rows, q_width), bf16)] * n_keys,
            cost(5 * att_flops // 4, 4 * all_rows * inner),
            prefetch=2,
        )(
            scalars,
            frame_counts,
            *q_all,
            *packs,
            *packs,
            kp,
            vp,
            kl,
            vl,
            norm_vec,
            norm_vec,
            *before,
        )
        return out[:4], out[4:]

    def regroup(value):
        value = jnp.moveaxis(value, 1, 2).reshape(-1, high, n_far, PAIR, each)
        value = value.transpose(0, 3, 1, 2, 4).reshape(-1, PAIR, high, n_far * each)
        return jnp.where(near == 0, value, value[:, ::-1])

    def weights(turn, kv_t, stat, kl_g, vl_g, q_grads, before):
        g = pick(turn)
        lanes = dim // n_far
        cols = pl.BlockSpec((rows, GROUP), lambda i, s: (0, g(s) if turn else 0))
        place = (lambda i, s: (0, 0, 0, i ^ s[2])) if aligned else (lambda i, s: (0, 0, 0, i))
        if aligned:
            grid, run = (n_far,), lanes
            out = [pl.BlockSpec((n_keys // 4, PAIR, high, run // PAIR), place)] * 2
        else:
            grid, run = (1,), dim
            out = [whole((n_keys // 4, PAIR, high, dim // PAIR))] * 2
        small_run = pl.BlockSpec((8, run), lambda i, s: (0, i))
        wo_run = pl.BlockSpec((n_keys, wo_rows, run), (lambda i, s: (0, 0, i ^ s[2])) if aligned else (lambda i, s: (0, 0, 0)))
        grads = call(
            functools.partial(weight_kernel, n_keys, turn, width, frames, aligned),
            "projection_weights",
            grid,
            [
                whole((2, GROUP, all_rows)),
                pl.BlockSpec((all_rows, run), lambda i, s: (0, i)),
                whole((rows, GROUP)),
                whole((rows, GROUP)),
                pl.BlockSpec((rows, run), lambda i, s: (0, i)),
                pl.BlockSpec((group_rows, run), lambda i, s: (0, i)),
                wo_run,
                whole((all_rows, LANES)),
                whole((8, all_rows)),
                whole((8, all_rows)),
                pl.BlockSpec((run, GROUP), lambda i, s: (i, g(s))),
                pl.BlockSpec((run, GROUP), lambda i, s: (i, g(s))),
                pl.BlockSpec((1, run), lambda i, s: (0, i)),
                pl.BlockSpec((1, run), lambda i, s: (0, i)),
            ]
            + [cols] * n_keys
            + [small_run] * len(before),
            out + [small_run],
            [struct((n_keys // 4, PAIR, high, dim // PAIR), bf16)] * 2 + [struct((8, dim), f32)],
            cost(patch_flops // 2, 4 * all_rows * dim),
            scratch_shapes=[pltpu.VMEM((3 * GROUP, run), f32), pltpu.VMEM((2 * GROUP, LANES), f32)],
        )(
            scalars,
            kv_t,
            media_low.reshape(all_rows, dim),
            kl_g,
            vl_g,
            own_rows,
            rows_all,
            out_slots,
            once.reshape(all_rows, LANES),
            norm_stat,
            stat,
            key_weight,
            value_weight,
            row(media_gain),
            row(media_bias),
            *q_grads,
            *before,
        )
        return grads if aligned else [regroup(v) for v in grads[:2]] + [grads[2]]

    group_rows = PAIR * n_keys * rows
    (kv_a, stat_a, kl_a, vl_a), q_a = attend_back(0, packs, [])
    given_a, kept_a, media_small = weights(0, kv_a, stat_a, kl_a, vl_a, q_a, [])
    far_core = over_keys(given_a, 1)
    ff_all, kept_a = tie(ff_all, kept_a)

    units = hidden // (n_keys * PAIR)
    ff_partial = call(
        functools.partial(ff_grad_kernel, aligned),
        "feed_forward_weights",
        (1,),
        [
            whole((group_rows, dim)),
            pl.BlockSpec((group_rows, dim), lambda i, s: (0, 1)),
            pl.BlockSpec((dim, units), lambda i, s: (0, s[4])),
            pl.BlockSpec((units, dim), lambda i, s: (s[4], 0)),
        ],
        whole((2 * units, dim)),
        struct((2 * units, dim), bf16),
        cost(8 * group_rows * dim * units, 8 * dim * units + 4 * group_rows * dim),
    )(scalars, ff_all, rows_all, up_weight, down_weight)
    blocks = n_far // n_keys
    if not aligned:
        pieces = ff_partial[units:].reshape(blocks, units // blocks, n_keys, dim // n_keys)
        pieces = pieces.transpose(0, 2, 1, 3).reshape(n_far, units, dim // n_far)
        pieces = pieces.transpose(1, 0, 2).reshape(units, dim)
        ups = ff_partial[:units].reshape(units, n_far, PAIR, each)
        ups = jnp.where(near == 0, ups, ups[:, :, ::-1]).reshape(units, dim)
        ff_partial = jnp.concatenate([ups, pieces], 0)
    far_core, ff_partial = tie(far_core, ff_partial)
    ff_sum = lax.psum_scatter(ff_partial, "far", scatter_dimension=1, tiled=True)
    far_sum = add(kept_a, far_core)
    far_sum, packs[0] = tie(far_sum, packs[0])
    far_near = over_near(far_sum[:, 1])
    (kv_b, stat_b, kl_b, vl_b), q_b = attend_back(1, packs, q_a)
    q_slots = exchange_keys(q_b)
    far_near, kv_b = tie(far_near, kv_b)
    far_half = add(far_sum[:, 0], far_near)
    far_half, kv_b = tie(far_half, kv_b)
    far_got = [over_keys(far_half[j], half_keys + 2 * j) for j in range(n_keys // 4)]
    given_b, kept_b, media_small = weights(1, kv_b, stat_b, kl_b, vl_b, q_b, [media_small])
    near_core = over_keys(given_b, 1)
    kept_b, lat = tie(kept_b, lat)

    col = lambda turn: pl.BlockSpec((dim, GROUP), lambda i, s: (0, s[5] ^ (1 - turn)))
    both = lambda value: [value, value]
    small_rows = -(-(n_frames + 6) // 8) * 8
    latents_grad, small = call(
        functools.partial(latent_back_kernel, n_keys, frames, n_frames),
        "latent_back",
        (1,),
        [whole((rows, dim)), whole((1, dim)), whole((rows, dim)), whole((8, dim)), whole((2, dim))]
        + [whole((rows, GROUP)), col(0), whole((rows, GROUP)), col(0)]
        + [whole((rows, GROUP)), col(1), whole((rows, GROUP)), col(1)]
        + [whole((dim, inner))]
        + [whole((rows, inner))] * n_keys,
        [whole((rows, dim)), whole((small_rows, dim))],
        (struct((rows, dim), f32), struct((small_rows, dim), f32)),
        cost(6 * rows * dim * inner, 6 * dim * inner + 20 * rows * dim),
    )(
        scalars,
        lat,
        row(latent_gain),
        mid_grad,
        media_small,
        ff_small,
        kl_a,
        key_weight,
        vl_a,
        value_weight,
        kl_b,
        key_weight,
        vl_b,
        value_weight,
        query_weight,
        *q_slots,
    )

    pieces = 3
    each_piece = media // pieces

    def patch_back(piece, gain, patches_grad):
        at = piece * each_piece
        block = pl.BlockSpec((1, key_rows, dim), lambda i, *_: (i + at, 0, 0))
        keys = pl.BlockSpec((2, GROUP, key_rows), lambda i, *_: (0, 0, i + at))
        stat = pl.BlockSpec((8, key_rows), lambda i, *_: (0, i + at))
        return call(
            functools.partial(patch_back_kernel, frames),
            "patch_back",
            (each_piece,),
            [
                keys,
                keys,
                stat,
                stat,
                stat,
                block,
                time_block,
                whole((1, dim)),
                col(0),
                col(0),
                col(1),
                col(1),
                pl.BlockSpec(memory_space=pl.ANY),
            ],
            block,
            struct(patches.shape, bf16),
            cost(patch_flops // pieces, 8 * all_rows * dim // pieces),
            **({} if piece == 0 else {"input_output_aliases": {13: 0}}),
        )(
            scalars,
            kv_a,
            kv_b,
            stat_a,
            stat_b,
            norm_stat,
            patches,
            time_blocks,
            gain,
            key_weight,
            value_weight,
            key_weight,
            value_weight,
            gain if piece == 0 else patches_grad,
        )

    def butterfly(value, step):
        axis, shift = step
        size = {"keys": n_keys, "near": PAIR, "far": n_far}[axis]
        return lax.ppermute(value, axis, [(i, i ^ shift) for i in range(size)])

    steps = [
        (axis, 1 << i)
        for axis, size in (("keys", n_keys), ("near", PAIR), ("far", n_far))
        for i in range(size.bit_length() - 1)
    ]
    gain = row(media_gain)
    small = small + butterfly(small, steps[0])
    near_core, latents_grad = tie(near_core, latents_grad)
    near_sum = add(kept_b, near_core)
    total = near_sum[0]
    for j in range(1, n_keys // 4):
        total = add(total, over_keys(near_sum[j], 2 * j))
    total, small, gain = tie(total, small, gain)
    near_got = over_near(total[1])
    small_got = butterfly(small, steps[1])
    patches_grad = patch_back(0, gain, None)
    patches_grad, small_got, *far_got = tie(patches_grad, small_got, *far_got)
    total = total[0]
    for value in far_got:
        total = add(total, value)
    small = small + small_got
    total, small, gain, ff_sum = tie(total, small, gain, ff_sum)
    small_got = butterfly(small, steps[2])
    up_keep = ff_sum[:units, :each]
    up_got = over_near(ff_sum[:units, each:])
    patches_grad = patch_back(1, gain, patches_grad)
    patches_grad, small_got, near_got, up_got = tie(patches_grad, small_got, near_got, up_got)
    total = add(total, near_got)
    small = small + small_got
    if not aligned:
        total = total.reshape(-1, n_far, each)
        total = jnp.concatenate(
            [lax.dynamic_index_in_dim(total, far ^ s, 1, False) for s in range(n_far)], 1
        )
    total, small, gain = tie(total, small, gain)
    parts = [over_far(total[:, s * each : (s + 1) * each], s) for s in range(1, n_far)]
    small_got = butterfly(small, steps[3])
    route = []
    for m in range(n_media):
        for k in range(n_keys):
            block, owner = divmod(m // PAIR, n_keys)
            target = (k * PAIR + m % PAIR) * blocks + block
            route.append((m * n_keys + k, target * n_keys + owner))
    down_grad = lax.ppermute(ff_sum[units:], ("far", "near", "keys"), route)
    patches_grad = patch_back(2, gain, patches_grad)
    patches_grad, small_got, down_grad, *parts = tie(patches_grad, small_got, down_grad, *parts)
    parts = [total[:, :each]] + parts
    small = small + small_got
    for step in steps[4:]:
        small = small + butterfly(small, step)
    if aligned:
        up_grad = call(
            finish_up_kernel,
            "finish_up",
            (1,),
            [whole((units, each))] * 2,
            whole((each, PAIR * units)),
            struct((each, PAIR * units), f32),
            cost(0, 8 * units * each),
        )(scalars, up_keep, up_got)
    else:
        up_grad = jnp.where(
            near == 0,
            jnp.concatenate([up_keep, up_got], 0),
            jnp.concatenate([up_got, up_keep], 0),
        ).T.astype(f32)
    down_grad = down_grad.reshape(units // blocks, dim // n_keys).astype(f32)

    if aligned:
        q_grad, k_grad, v_grad, out_grad = call(
            functools.partial(finish_kernel, width),
            "finish_projections",
            (1,),
            [whole(p.shape) for p in parts],
            [whole((each, width))] * 3 + [whole((inner // n_media, dim // n_keys))],
            [struct((each, width), f32)] * 3
            + [struct((inner // n_media, dim // n_keys), f32)],
            cost(0, 16 * width * each),
        )(scalars, *parts)
    else:
        total = functools.reduce(jnp.add, [p.astype(f32) for p in parts])
        q_grad, k_grad, v_grad = (total[i * width : (i + 1) * width].T for i in range(3))
        out_grad = total[3 * width :].reshape(-1, inner // n_media, each)
        out_grad = out_grad.transpose(1, 0, 2).reshape(inner // n_media, dim // n_keys)

    return (
        resampled.reshape(latents.shape),
        patches_grad,
        latents_grad.reshape(latents.shape),
        small[:n_frames],
        small[n_frames],
        small[n_frames + 1],
        small[n_frames + 2],
        small[n_frames + 3],
        small[n_frames + 4],
        small[n_frames + 5],
        q_grad,
        k_grad,
        v_grad,
        out_grad,
        up_grad,
        down_grad,
    )


def solution(mesh):
    n_media, n_keys = mesh.shape["media"], mesh.shape["keys"]
    n_far = n_media // PAIR
    fine = Mesh(mesh.devices.reshape(n_far, PAIR, n_keys), ("far", "near", "keys"))
    split = P(("far", "near"), "keys", None)
    return jax.shard_map(
        functools.partial(shards, n_far, n_keys),
        mesh=fine,
        in_specs=(split, split, P(("far", "near"))) + (P(),) * 13 + (split,),
        out_specs=(split,) * 3 + (P(),) * 7 + (P(("far", "near"), "keys"),) * 6,
        check_vma=False,
    )
```

time: 306 us -> 222 us (0.73); the launches traced: 300 us -> 221 us
  Pallas kernels: 83.5 us -> 139 us
  local copies, waits for them, and re-layouts: 64 us -> 9.35 us
  starting transfers between devices: 76 us -> 27 us
  waiting for transfers between devices: 61.9 us -> 27.9 us
  between operations: 1.71 us -> 14.1 us
  other arithmetic: 13 us -> 3.74 us
    pallas_call x10 -> x16, Pallas kernels: 83.5 us -> 139 us  [pinned(): return run(*args)]
    ppermute x32 -> x12, starting transfers between devices: 55.3 us -> 14.6 us  [the longest x5 5.95 us: butterfly(): return lax.ppermute(value, axis, [(i, i ^ shift) for i in range(size)])]
    ppermute x32 -> x12, waiting for transfers between devices: 36.9 us -> 7.5 us  [the longest x3 5.41 us: over_far(): return lax.ppermute(value, 'far', [(i, i ^ shift) for i in range(n_far)])]
    unnamed x138 -> x42, local copies, waits for them, and re-layouts: 25.2 us -> 2.69 us
    reshape x5 -> x0, local copies, waits for them, and re-layouts: 18.3 us -> none  [the longest x1 11.3 us: shards(): down_partial.reshape(blocks, units // blocks, n_keys, dim // n_keys)]
    convert_element_type x10 -> x5, other arithmetic: 11.3 us -> 2.56 us  [the longest x4 1.73 us: add(): return (left.astype(f32) + right.astype(f32)).astype(bf16)]
    ppermute x39 -> x15, starting transfers between devices: 20.7 us -> 12.1 us  [over_keys(): return lax.ppermute(value, 'keys', [(i, i ^ shift) for i in range(n_keys)])]
    another operation x2 -> x1, local copies, waits for them, and re-layouts: 8.78 us -> 0.6 us  [shards(): jnp.stack([key, near, far, far, key * PAIR + near, own_group, jnp.full_li...]
  transfers between devices with their start and end apart: 71 -> 30, of which waited for: 18 -> 10; matrix products, arithmetic and copies ran while one was open for 19% -> 4% of each run, Pallas kernels for 25% -> 61%
where the time goes in v2:
time: 222 us; the launch traced here: 221 us
  Pallas kernels  139 us (63%)
  waiting for transfers between devices  27.9 us (13%)
  starting transfers between devices  27 us (12%)
  between operations  14.1 us (6%)
  local copies, waits for them, and re-layouts  9.35 us (4%)
  other arithmetic  3.74 us (2%)
    pallas_call x16, Pallas kernels, pinned(): return run(*args)  139 us
    ppermute x15, waiting for transfers between devices, over_keys(): return lax.ppermute(value, 'keys', [(i, i ^ shift) for i in range(n_keys)])  20.3 us
    ppermute x15, starting transfers between devices, over_keys(): return lax.ppermute(value, 'keys', [(i, i ^ shift) for i in range(n_keys)])  12.1 us
    ppermute x5, starting transfers between devices, butterfly(): return lax.ppermute(value, axis, [(i, i ^ shift) for i in range(size)])  5.95 us
    ppermute x3, waiting for transfers between devices, over_far(): return lax.ppermute(value, 'far', [(i, i ^ shift) for i in range(n_far)])  5.41 us
  transfers between devices with their start and end apart: 30, of which 10 were waited for; matrix products, arithmetic and copies ran while one was open for 4% of the time, Pallas kernels for 61%

profile of v2, /device:TPU:0, one launch (start us, length us, event | category | flops | bytes accessed | tf_op | source)
XLA Modules:
  0.0 220.9 jit_solution(9944924909089097978)
XLA Ops:
  7.8 3.3 %latent_project.1 = (bf16[96,2048]{1,0:T(8,128)(2,1)}, bf16[96,512]{1,0:T(8,128)(2,1)}) custom-call(s32[7]{0:T(128)} %stack.24._.scalars, f32[96,1024]{1,0:T(8,128)} %bitcast.38, f32[1,1024]{1,0:T(1,128)} %bitcast.56, f32[1,1024]{1,0:T(1,128)} %bitcast.60, f32[96,1024]{1,0:T(8,128)} %bitcast.43, bf16[1024,512]{1,0:T(8,128)(2,1)} %refs_8_.1), custom_call_target="tpu_custom_call" | custom-call | flops 100663296 | bytes 2424832 | tf_op jit(solution)/shard_map/latent_project/pallas_call | solution.py:665
  11.2 2.5 %collective-permute-start.2 = (bf16[96,512]{1,0:T(8,128)(2,1)}, bf16[96,512]{1,0:T(8,128)(2,1)S(1)}, u32[]{:S(2)}, u32[]{:S(2)}) collective-permute-start(bf16[96,512]{1,0:T(8,128)(2,1)} %get-tuple-element.105.refs_0_), channel_id=1, source_target_pairs={{0,3},{1,2},{2,1},{3,0},{4,7},{5,6},{6,5},{7,4},{8,11},{9,10},{10,... | collective-permute-start | bytes 294920 | tf_op jit(solution)/shard_map/ppermute | solution.py:608
  15.8 15.9 %patch_project.1 = (bf16[6,512,1024]{2,1,0:T(8,128)(2,1)}, bf16[6,512,512]{2,1,0:T(8,128)(2,1)}, bf16[6,512,512]{2,1,0:T(8,128)(2,1)}, bf16[96,512]{1,0:T(8,128)...) custom-call(s32[7]{0:T(128)} %stack.24._.scalars, ...), custom_call_target="tpu_custom_call" | custom-call | flops 6442450944 | bytes 37748736 | tf_op jit(solution)/shard_map/patch_project/pallas_call | solution.py:665
  32.4 9.9 %attend.1 = (bf16[96,640]{1,0:T(8,128)(2,1)}, bf16[96,640]{1,0:T(8,128)(2,1)}, bf16[96,640]{1,0:T(8,128)(2,1)}, bf16[96,640]{1,0:T(8,128)(2,1)}) custom-call(s32[7]{0:T(128)} %stack.24._.scalars, s32[6]{0:T(128)} %counts.5, bf16[96,512]{1,0:T(8,128)(2,1)} %get-tuple-element.105.refs_0_, bf16[96,512]{1,0:T(8,128)(2,1)} %copy-done.7, ...), custom_call_target="tpu_custom_call" | custom-call | flops 1660944384 | bytes 6291456 | tf_op jit(solution)/shard_map/attend/pallas_call | solution.py:665
  44.4 5.0 %collective-permute-done.4.refs_2_ = bf16[96,640]{1,0:T(8,128)(2,1)S(1)} collective-permute-done((bf16[96,640]{1,0:T(8,128)(2,1)}, bf16[96,640]{1,0:T(8,128)(2,1)S(1)}, u32[]{:S(2)}, u32[]{:S(2)}) %collective-permute-start.4) | collective-permute-done | bytes 122912 | tf_op jit(solution)/shard_map/ppermute | solution.py:608
  50.9 4.2 %join.1 = (f32[96,512]{1,0:T(8,128)}, bf16[96,512]{1,0:T(8,128)(2,1)}, f32[96,1024]{1,0:T(8,128)}, bf16[96,1024]{1,0:T(8,128)(2,1)}, f32[96,128]{1,0:T(8,128)}) custom-call(s32[7]{0:T(128)} %stack.24._.scalars, f32[96,1024]{1,0:T(8,128)} %bitcast.39, f32[1,1024]{1,0:T(1,128)} %bitcast.58, f32[1,1024]{1,0:T(1,128)} %bitcast.61, bf16[512,1024]{1,0:T(8,128)(2,1)} %wo.3, ...), custom_call_target="tpu_custom_call" | custom-call | flops 100663296 | bytes 2621440 | tf_op jit(solution)/shard_map/join/pallas_call | solution.py:665
  55.3 16.7 %feed_forward.1 = (f32[96,1024]{1,0:T(8,128)}, f32[96,1024]{1,0:T(8,128)}, bf16[96,640]{1,0:T(8,128)(2,1)}, f32[2,1024]{1,0:T(2,128)}, bf16[4,128,1024]{2,1,0:T(8,128)(2,1)}) custom-call(s32[7]{0:T(128)} %stack.24._.scalars, f32[96,512]{1,0:T(8,128)} %get-tuple-element.115.attended, bf16[96,512]{1,0:T(8,128)(2,1)} %get-tuple-element.116.att_low, ...), custom_call_target="tpu_custom_call" | custom-call | flops 3221225472 | bytes 19136512 | tf_op jit(solution)/shard_map/feed_forward/pallas_call | solution.py:665
  73.9 6.0 %collective-permute-done.7.refs_6_.refs_10_ = bf16[96,640]{1,0:T(8,128)(2,1)S(1)} collective-permute-done((bf16[96,640]{1,0:T(8,128)(2,1)}, bf16[96,640]{1,0:T(8,128)(2,1)S(1)}, u32[]{:S(2)}, u32[]{:S(2)}) %collective-permute-start.7) | collective-permute-done | bytes 122912 | tf_op jit(solution)/shard_map/ppermute | solution.py:608
  81.9 11.2 %attend_back.2 = (bf16[2,256,3072]{2,1,0:T(8,128)(2,1)}, f32[8,3072]{1,0:T(8,128)}, bf16[96,256]{1,0:T(8,128)(2,1)}, bf16[96,256]{1,0:T(8,128)(2,1)}, bf16[96,25...) custom-call(s32[7]{0:T(128)} %stack.24._.scalars, s32[6]{0:T(128)} %counts.5, ...), custom_call_target="tpu_custom_call" | custom-call | flops 2076180480 | bytes 6291456 | tf_op jit(solution)/shard_map/attend_back/pallas_call | solution.py:665
  93.1 12.9 %projection_weights.2 = (bf16[1,2,512,512]{3,2,1,0:T(8,128)(2,1)}, bf16[1,2,512,512]{3,2,1,0:T(8,128)(2,1)}, f32[8,1024]{1,0:T(8,128)}) custom-call(s32[7]{0:T(128)} %stack.24._.scalars, bf16[2,256,3072]{2,1,0:T(8,128)(2,1)} %get-tuple-element.123.kv_t.kv_a, bf16[3072,1024]{1,0:T(8,128)(2,1)} %bitcast.36, bf16[96,256]{1,0:T(8,128)(2,1)} %get-tuple-element.125.kl_g.refs_0_, ...), custom_call_target="tpu_custom_call" | custom-call | flops 3221225472 | bytes 12582912 | tf_op jit(solution)/shard_map/projection_weights/pallas_call | solution.py:665
  106.3 8.4 %feed_forward_weights.1 = bf16[1024,1024]{1,0:T(8,128)(2,1)} custom-call(s32[7]{0:T(128)} %stack.24._.scalars, bf16[768,1024]{1,0:T(8,128)(2,1)} %all-gather.3.cloned.1.call-done.ff_all, bf16[768,2048]{1,0:T(8,128)(2,1)} %all-gather.5.cloned.1.call-done.rows_all.out_all, bf16[1024,4096]{1,0:T(8,128)(2,1)} %up.3, bf16[4096,1024]{1,0:T(8,128)(2,1)} %down.3), custom_call_target="tpu_custom_call" | custom-call | flops 3221225472 | bytes 7340032 | tf_op jit(solution)/shard_map/feed_forward_weights/pallas_call | solution.py:665
  116.6 11.3 %attend_back.3 = (bf16[2,256,3072]{2,1,0:T(8,128)(2,1)}, f32[8,3072]{1,0:T(8,128)}, bf16[96,256]{1,0:T(8,128)(2,1)}, bf16[96,256]{1,0:T(8,128)(2,1)}, bf16[96,51...) custom-call(s32[7]{0:T(128)} %stack.24._.scalars, s32[6]{0:T(128)} %counts.5, ...), custom_call_target="tpu_custom_call" | custom-call | flops 2076180480 | bytes 6291456 | tf_op jit(solution)/shard_map/attend_back/pallas_call | solution.py:665
  129.4 13.5 %projection_weights.3 = (bf16[1,2,512,512]{3,2,1,0:T(8,128)(2,1)}, bf16[1,2,512,512]{3,2,1,0:T(8,128)(2,1)}, f32[8,1024]{1,0:T(8,128)}) custom-call(s32[7]{0:T(128)} %stack.24._.scalars, bf16[2,256,3072]{2,1,0:T(8,128)(2,1)} %get-tuple-element.145.kv_t.kv_b, bf16[3072,1024]{1,0:T(8,128)(2,1)} %bitcast.37, bf16[96,256]{1,0:T(8,128)(2,1)} %get-tuple-element.147.kl_g.refs_4_, ...), custom_call_target="tpu_custom_call" | custom-call | flops 3221225472 | bytes 12582912 | tf_op jit(solution)/shard_map/projection_weights/pallas_call | solution.py:665
  143.5 2.4 %collective-permute-start.13 = (bf16[96,512]{1,0:T(8,128)(2,1)S(1)}, bf16[96,512]{1,0:T(8,128)(2,1)S(1)}, u32[]{:S(2)}, u32[]{:S(2)}) collective-permute-start(bf16[96,512]{1,0:T(8,128)(2,1)S(1)} %copy-done.16), channel_id=1, source_target_pairs={{0,2},{1,3},{2,0},{3,1},{4,6},{5,7},{6,4},{7,5},{8,10},{9,11},{10,... | collective-permute-start | bytes 294920 | tf_op jit(solution)/shard_map/ppermute | solution.py:608
  145.9 3.1 %collective-permute-done.13.refs_11_ = bf16[96,512]{1,0:T(8,128)(2,1)S(1)} collective-permute-done((bf16[96,512]{1,0:T(8,128)(2,1)S(1)}, bf16[96,512]{1,0:T(8,128)(2,1)S(1)}, u32[]{:S(2)}, u32[]{:S(2)}) %collective-permute-start.13) | collective-permute-done | bytes 98336 | tf_op jit(solution)/shard_map/ppermute | solution.py:608
  151.6 5.1 %latent_back.1 = (f32[96,1024]{1,0:T(8,128)}, f32[16,1024]{1,0:T(8,128)}) custom-call(s32[7]{0:T(128)} %stack.24._.scalars, f32[96,1024]{1,0:T(8,128)} %bitcast.40, f32[1,1024]{1,0:T(1,128)} %bitcast.57, f32[96,1024]{1,0:T(8,128)} %get-tuple-element.158.mid_grad, f32[8,1024]{1,0:T(8,128)} %get-tuple-element.159.media_small, ...), custom_call_target="tpu_custom_call" | custom-call | flops 301989888 | bytes 5111808 | tf_op jit(solution)/shard_map/latent_back/pallas_call | solution.py:665
  162.6 7.1 %patch_back.3._ = bf16[6,512,1024]{2,1,0:T(8,128)(2,1)} custom-call(s32[7]{0:T(128)} %stack.24._.scalars, bf16[2,256,3072]{2,1,0:T(8,128)(2,1)} %get-tuple-element.123.kv_t.kv_a, bf16[2,256,3072]{2,1,0:T(8,128)(2,1)} %get-tuple-element.145.kv_t.kv_b, f32[8,3072]{1,0:T(8,128)} %get-tuple-element.130.grad_stat.stat_a, ...), custom_call_target="tpu_custom_call" | custom-call | flops 2147483648 | bytes 8388608 | tf_op jit(solution)/shard_map/patch_back/pallas_call | solution.py:665
  179.1 7.1 %patch_back.4._ = bf16[6,512,1024]{2,1,0:T(8,128)(2,1)} custom-call(s32[7]{0:T(128)} %stack.24._.scalars, bf16[2,256,3072]{2,1,0:T(8,128)(2,1)} %get-tuple-element.123.kv_t.kv_a, bf16[2,256,3072]{2,1,0:T(8,128)(2,1)} %get-tuple-element.145.kv_t.kv_b, f32[8,3072]{1,0:T(8,128)} %get-tuple-element.130.grad_stat.stat_a, ...), custom_call_target="tpu_custom_call", output_to_operand_aliasing={{}: (13, {})} | custom-call | flops 2147483648 | bytes 8388608 | tf_op jit(solution)/shard_map/patch_back/pallas_call | solution.py:665
  186.4 3.0 %collective-permute-start.21 = (f32[16,1024]{1,0:T(8,128)S(1)}, f32[16,1024]{1,0:T(8,128)S(1)}, u32[]{:S(2)}, u32[]{:S(2)}) collective-permute-start(f32[16,1024]{1,0:T(8,128)S(1)} %add.44), channel_id=1, source_target_pairs={{0,8},{8,0},{16,24},{24,16},{1,9},{9,1},{17,25},{25,17},{2,10},{10... | collective-permute-start | bytes 196616 | tf_op jit(solution)/shard_map/ppermute | solution.py:1074
  190.1 3.7 %collective-permute-start.25 = (bf16[512,128]{1,0:T(8,128)(2,1)S(1)}, bf16[512,128]{1,0:T(8,128)(2,1)S(1)}, u32[]{:S(2)}, u32[]{:S(2)}) collective-permute-start(bf16[512,128]{1,0:T(8,128)(2,1)S(1)} %get-tuple-element.197), channel_id=1, source_target_pairs={{0,24},{8,16},{16,8},{24,0},{1,25},{9,17},{17,9},{25,1},{2,26},{10... | collective-permute-start | bytes 393224 | tf_op jit(solution)/shard_map/ppermute | solution.py:614
  194.5 7.1 %patch_back.5 = bf16[6,512,1024]{2,1,0:T(8,128)(2,1)} custom-call(s32[7]{0:T(128)} %stack.24._.scalars, bf16[2,256,3072]{2,1,0:T(8,128)(2,1)} %get-tuple-element.123.kv_t.kv_a, bf16[2,256,3072]{2,1,0:T(8,128)(2,1)} %get-tuple-element.145.kv_t.kv_b, f32[8,3072]{1,0:T(8,128)} %get-tuple-element.130.grad_stat.stat_a, ...), custom_call_target="tpu_custom_call", output_to_operand_aliasing={{}: (13, {})} | custom-call | flops 2147483648 | bytes 8388608 | tf_op jit(solution)/shard_map/patch_back/pallas_call | solution.py:665
  201.7 5.4 %collective-permute-done.24.refs_2_ = bf16[512,128]{1,0:T(8,128)(2,1)S(1)} collective-permute-done((bf16[512,128]{1,0:T(8,128)(2,1)S(1)}, bf16[512,128]{1,0:T(8,128)(2,1)S(1)}, u32[]{:S(2)}, u32[]{:S(2)}) %collective-permute-start.24) | collective-permute-done | bytes 131104 | tf_op jit(solution)/shard_map/ppermute | solution.py:614
  207.2 2.6 %finish_up.1 = f32[128,1024]{1,0:T(8,128)} custom-call(s32[7]{0:T(128)} %stack.24._.scalars, bf16[512,128]{1,0:T(8,128)(2,1)} %get-tuple-element.194.keep, bf16[512,128]{1,0:T(8,128)(2,1)} %copy-done.11), custom_call_target="tpu_custom_call" | custom-call | bytes 524288 | tf_op jit(solution)/shard_map/finish_up/pallas_call | solution.py:665
  210.6 2.5 %finish_projections.1 = (f32[128,128]{1,0:T(8,128)}, f32[128,128]{1,0:T(8,128)}, f32[128,128]{1,0:T(8,128)}, f32[64,256]{1,0:T(8,128)}) custom-call(s32[7]{0:T(128)} %stack.24._.scalars, bf16[512,128]{1,0:T(8,128)(2,1)} %get-tuple-element.196.refs_0_, bf16[512,128]{1,0:T(8,128)(2,1)} %copy-done.10, bf16[512,128]{1,0:T(8,128)(2,1)} %copy-done.9, ...), custom_call_target="tpu_custom_call" | custom-call | bytes 262144 | tf_op jit(solution)/shard_map/finish_projections/pallas_call | solution.py:665
  (117 shorter events, 37.1 us)
Async XLA Ops:
  7.2 85.9 %all-gather.5.cloned.1.call-start = ((), (), s32[]{:S(2)}) async-start(), calls=%async_computation.2 | async-start | bytes 3538944 | tf_op jit(solution)/shard_map/all_gather | solution.py:679
  11.2 95.1 %all-gather.3.cloned.1.call-start = ((), (), s32[]{:S(2)}) async-start(), calls=%async_computation.1 | async-start | bytes 1769472 | tf_op jit(solution)/shard_map/all_gather | solution.py:761
  11.2 20.4 %collective-permute-start.2 = (bf16[96,512]{1,0:T(8,128)(2,1)}, bf16[96,512]{1,0:T(8,128)(2,1)S(1)}, u32[]{:S(2)}, u32[]{:S(2)}) collective-permute-start(bf16[96,512]{1,0:T(8,128)(2,1)} %get-tuple-element.105.refs_0_), channel_id=1, source_target_pairs={{0,3},{1,2},{2,1},{3,0},{4,7},{5,6},{6,5},{7,4},{8,11},{9,10},{10,... | collective-permute-start | bytes 294920 | tf_op jit(solution)/shard_map/ppermute | solution.py:608
  13.7 18.0 %collective-permute-start.1 = (bf16[96,512]{1,0:T(8,128)(2,1)}, bf16[96,512]{1,0:T(8,128)(2,1)S(1)}, u32[]{:S(2)}, u32[]{:S(2)}) collective-permute-start(bf16[96,512]{1,0:T(8,128)(2,1)} %get-tuple-element.105.refs_0_), channel_id=1, source_target_pairs={{0,2},{1,3},{2,0},{3,1},{4,6},{5,7},{6,4},{7,5},{8,10},{9,11},{10,... | collective-permute-start | bytes 294920 | tf_op jit(solution)/shard_map/ppermute | solution.py:608
  14.3 17.3 %collective-permute-start = (bf16[96,512]{1,0:T(8,128)(2,1)}, bf16[96,512]{1,0:T(8,128)(2,1)S(1)}, u32[]{:S(2)}, u32[]{:S(2)}) collective-permute-start(bf16[96,512]{1,0:T(8,128)(2,1)} %get-tuple-element.105.refs_0_), channel_id=1, source_target_pairs={{0,1},{1,0},{2,3},{3,2},{4,5},{5,4},{6,7},{7,6},{8,9},{9,8},{10,11... | collective-permute-start | bytes 294920 | tf_op jit(solution)/shard_map/ppermute | solution.py:608
  42.9 6.4 %collective-permute-start.4 = (bf16[96,640]{1,0:T(8,128)(2,1)}, bf16[96,640]{1,0:T(8,128)(2,1)S(1)}, u32[]{:S(2)}, u32[]{:S(2)}) collective-permute-start(bf16[96,640]{1,0:T(8,128)(2,1)} %get-tuple-element.113), channel_id=1, source_target_pairs={{0,2},{1,3},{2,0},{3,1},{4,6},{5,7},{6,4},{7,5},{8,10},{9,11},{10,... | collective-permute-start | bytes 368648 | tf_op jit(solution)/shard_map/ppermute | solution.py:608
  44.2 6.1 %collective-permute-start.5 = (bf16[96,640]{1,0:T(8,128)(2,1)}, bf16[96,640]{1,0:T(8,128)(2,1)S(1)}, u32[]{:S(2)}, u32[]{:S(2)}) collective-permute-start(bf16[96,640]{1,0:T(8,128)(2,1)} %get-tuple-element.114), channel_id=1, source_target_pairs={{0,3},{1,2},{2,1},{3,0},{4,7},{5,6},{6,5},{7,4},{8,11},{9,10},{10,... | collective-permute-start | bytes 368648 | tf_op jit(solution)/shard_map/ppermute | solution.py:608
  55.1 118.7 %reduce-scatter.2.cloned.1.call-start = ((), (), s32[]{:S(2)}) async-start(), calls=%async_computation.3 | async-start | bytes 2621440 | tf_op jit(solution)/shard_map/reduce_scatter | solution.py:975
  72.0 7.9 %collective-permute-start.7 = (bf16[96,640]{1,0:T(8,128)(2,1)}, bf16[96,640]{1,0:T(8,128)(2,1)S(1)}, u32[]{:S(2)}, u32[]{:S(2)}) collective-permute-start(bf16[96,640]{1,0:T(8,128)(2,1)} %get-tuple-element.141.refs_4_.refs_8_), channel_id=1, source_target_pairs={{0,2},{1,3},{2,0},{3,1},{4,6},{5,7},{6,4},{7,5},{8,10},{9,11},{10,... | collective-permute-start | bytes 368648 | tf_op jit(solution)/shard_map/ppermute | solution.py:608
  73.8 6.1 %collective-permute-start.6 = (bf16[96,640]{1,0:T(8,128)(2,1)}, bf16[96,640]{1,0:T(8,128)(2,1)S(1)}, u32[]{:S(2)}, u32[]{:S(2)}) collective-permute-start(bf16[96,640]{1,0:T(8,128)(2,1)} %get-tuple-element.141.refs_4_.refs_8_), channel_id=1, source_target_pairs={{0,1},{1,0},{2,3},{3,2},{4,5},{5,4},{6,7},{7,6},{8,9},{9,8},{10,11... | collective-permute-start | bytes 368648 | tf_op jit(solution)/shard_map/ppermute | solution.py:608
  106.0 8.6 %collective-permute-start.9 = (bf16[1,2,512,512]{3,2,1,0:T(8,128)(2,1)}, bf16[1,2,512,512]{3,2,1,0:T(8,128)(2,1)S(1)}, u32[]{:S(2)}, u32[]{:S(2)}) collective-permute-start(bf16[1,2,512,512]{3,2,1,0:T(8,128)(2,1)} %get-tuple-element.137), channel_id=1, source_target_pairs={{0,1},{1,0},{2,3},{3,2},{4,5},{5,4},{6,7},{7,6},{8,9},{9,8},{10,11... | collective-permute-start | bytes 3145736 | tf_op jit(solution)/shard_map/ppermute | solution.py:608
  115.0 14.3 %collective-permute-start.10 = (bf16[1,512,512]{2,1,0:T(8,128)(2,1)S(1)}, bf16[1,512,512]{2,1,0:T(8,128)(2,1)S(1)}, u32[]{:S(2)}, u32[]{:S(2)}) collective-permute-start(bf16[1,512,512]{2,1,0:T(8,128)(2,1)S(1)} %slice_bitcast_fusion.1), channel_id=1, source_target_pairs={{0,4},{4,0},{1,5},{5,1},{2,6},{6,2},{3,7},{7,3},{8,12},{12,8},{9,1... | collective-permute-start | bytes 1572872 | tf_op jit(solution)/shard_map/ppermute | solution.py:611
  142.9 16.7 %collective-permute-start.11 = (bf16[1,2,512,512]{3,2,1,0:T(8,128)(2,1)}, bf16[1,2,512,512]{3,2,1,0:T(8,128)(2,1)S(1)}, u32[]{:S(2)}, u32[]{:S(2)}) collective-permute-start(bf16[1,2,512,512]{3,2,1,0:T(8,128)(2,1)} %get-tuple-element.156), channel_id=1, source_target_pairs={{0,1},{1,0},{2,3},{3,2},{4,5},{5,4},{6,7},{7,6},{8,9},{9,8},{10,11... | collective-permute-start | bytes 3145736 | tf_op jit(solution)/shard_map/ppermute | solution.py:608
  156.9 14.9 %collective-permute-start.17 = (bf16[512,512]{1,0:T(8,128)(2,1)S(1)}, bf16[512,512]{1,0:T(8,128)(2,1)}, u32[]{:S(2)}, u32[]{:S(2)}) collective-permute-start(bf16[512,512]{1,0:T(8,128)(2,1)S(1)} %bitcast.45), channel_id=1, source_target_pairs={{0,2},{1,3},{2,0},{3,1},{4,6},{5,7},{6,4},{7,5},{8,10},{9,11},{10,... | collective-permute-start | bytes 1572872 | tf_op jit(solution)/shard_map/ppermute | solution.py:608
  159.9 12.6 %collective-permute-start.16 = (f32[16,1024]{1,0:T(8,128)S(1)}, f32[16,1024]{1,0:T(8,128)S(1)}, u32[]{:S(2)}, u32[]{:S(2)}) collective-permute-start(f32[16,1024]{1,0:T(8,128)S(1)} %add.40), channel_id=1, source_target_pairs={{0,2},{1,3},{2,0},{3,1},{4,6},{5,7},{6,4},{7,5},{8,10},{9,11},{10,... | collective-permute-start | bytes 196616 | tf_op jit(solution)/shard_map/ppermute | solution.py:1074
  161.1 25.1 %collective-permute-start.19 = (bf16[512,512]{1,0:T(8,128)(2,1)S(1)}, bf16[512,512]{1,0:T(8,128)(2,1)S(1)}, u32[]{:S(2)}, u32[]{:S(2)}) collective-permute-start(bf16[512,512]{1,0:T(8,128)(2,1)S(1)} %slice_bitcast_fusion), channel_id=1, source_target_pairs={{0,4},{4,0},{1,5},{5,1},{2,6},{6,2},{3,7},{7,3},{8,12},{12,8},{9,1... | collective-permute-start | bytes 1572872 | tf_op jit(solution)/shard_map/ppermute | solution.py:611
  173.7 12.5 %collective-permute-start.18 = (f32[16,1024]{1,0:T(8,128)S(1)}, f32[16,1024]{1,0:T(8,128)S(1)}, u32[]{:S(2)}, u32[]{:S(2)}) collective-permute-start(f32[16,1024]{1,0:T(8,128)S(1)} %add.42), channel_id=1, source_target_pairs={{0,4},{4,0},{1,5},{5,1},{2,6},{6,2},{3,7},{7,3},{8,12},{12,8},{9,1... | collective-permute-start | bytes 196616 | tf_op jit(solution)/shard_map/ppermute | solution.py:1074
  177.9 8.4 %collective-permute-start.20 = (bf16[512,128]{1,0:T(8,128)(2,1)S(1)}, bf16[512,128]{1,0:T(8,128)(2,1)S(1)}, u32[]{:S(2)}, u32[]{:S(2)}) collective-permute-start(bf16[512,128]{1,0:T(8,128)(2,1)S(1)} %get-tuple-element.195), channel_id=1, source_target_pairs={{0,4},{4,0},{1,5},{5,1},{2,6},{6,2},{3,7},{7,3},{8,12},{12,8},{9,1... | collective-permute-start | bytes 393224 | tf_op jit(solution)/shard_map/ppermute | solution.py:611
  178.4 23.2 %collective-permute-start.22 = (bf16[512,256]{1,0:T(8,128)(2,1)S(1)}, bf16[512,256]{1,0:T(8,128)(2,1)S(1)}, u32[]{:S(2)}, u32[]{:S(2)}) collective-permute-start(bf16[512,256]{1,0:T(8,128)(2,1)S(1)} %slice.59), channel_id=1, source_target_pairs={{0,0},{1,8},{2,16},{3,24},{4,4},{5,12},{6,20},{7,28},{8,1},{9,9},{... | collective-permute-start | bytes 786440 | tf_op jit(solution)/shard_map/ppermute | solution.py:1119
  186.4 15.2 %collective-permute-start.21 = (f32[16,1024]{1,0:T(8,128)S(1)}, f32[16,1024]{1,0:T(8,128)S(1)}, u32[]{:S(2)}, u32[]{:S(2)}) collective-permute-start(f32[16,1024]{1,0:T(8,128)S(1)} %add.44), channel_id=1, source_target_pairs={{0,8},{8,0},{16,24},{24,16},{1,9},{9,1},{17,25},{25,17},{2,10},{10... | collective-permute-start | bytes 196616 | tf_op jit(solution)/shard_map/ppermute | solution.py:1074
  190.1 11.5 %collective-permute-start.25 = (bf16[512,128]{1,0:T(8,128)(2,1)S(1)}, bf16[512,128]{1,0:T(8,128)(2,1)S(1)}, u32[]{:S(2)}, u32[]{:S(2)}) collective-permute-start(bf16[512,128]{1,0:T(8,128)(2,1)S(1)} %get-tuple-element.197), channel_id=1, source_target_pairs={{0,24},{8,16},{16,8},{24,0},{1,25},{9,17},{17,9},{25,1},{2,26},{10... | collective-permute-start | bytes 393224 | tf_op jit(solution)/shard_map/ppermute | solution.py:614
  193.8 13.3 %collective-permute-start.24 = (bf16[512,128]{1,0:T(8,128)(2,1)S(1)}, bf16[512,128]{1,0:T(8,128)(2,1)S(1)}, u32[]{:S(2)}, u32[]{:S(2)}) collective-permute-start(bf16[512,128]{1,0:T(8,128)(2,1)S(1)} %get-tuple-element.198), channel_id=1, source_target_pairs={{0,16},{8,24},{16,0},{24,8},{1,17},{9,25},{17,1},{25,9},{2,18},{10... | collective-permute-start | bytes 393224 | tf_op jit(solution)/shard_map/ppermute | solution.py:614
  193.8 13.3 %collective-permute-start.23 = (bf16[512,128]{1,0:T(8,128)(2,1)S(1)}, bf16[512,128]{1,0:T(8,128)(2,1)S(1)}, u32[]{:S(2)}, u32[]{:S(2)}) collective-permute-start(bf16[512,128]{1,0:T(8,128)(2,1)S(1)} %get-tuple-element.199), channel_id=1, source_target_pairs={{0,8},{8,0},{16,24},{24,16},{1,9},{9,1},{17,25},{25,17},{2,10},{10... | collective-permute-start | bytes 393224 | tf_op jit(solution)/shard_map/ppermute | solution.py:614
  207.1 6.0 %collective-permute-start.26 = (f32[16,1024]{1,0:T(8,128)S(1)}, f32[16,1024]{1,0:T(8,128)S(1)}, u32[]{:S(2)}, u32[]{:S(2)}) collective-permute-start(f32[16,1024]{1,0:T(8,128)S(1)} %add.45), channel_id=1, source_target_pairs={{0,16},{8,24},{16,0},{24,8},{1,17},{9,25},{17,1},{25,9},{2,18},{10... | collective-permute-start | bytes 196616 | tf_op jit(solution)/shard_map/ppermute | solution.py:1074
  (27 other events, 131.1 us)
Sparse Core Ops, SparseCore 0:
  11.3 35.0 all-gather.4
  55.2 28.6 all-gather.2
  114.8 46.3 reduce-scatter.1

commit v3 on v2

--- a/solution.py
+++ b/solution.py
@@ -122,12 +122,36 @@
     return high, (values - high.astype(f32)).astype(bf16)
 
 
-def patch_kernel(
-    frames, scalars, patches, time, gain, bias, wk, wv, lat_low, low_o, k_o, v_o, kl_o, vl_o, stat_o, once_o, vec_o
-):
+def masked_scores(query, keys, frames, first, count):
+    scores = mul(query, keys, NT)
+    parts = []
+    for f in range(frames):
+        part = scores[:, f * PATCH : (f + 1) * PATCH]
+        parts.append(jnp.where(first + f < count, part, NEG))
+    return jnp.concatenate(parts + [scores[:, frames * PATCH :]], 1)
+
+
+def patch_kernel(n_keys, frames, scalars, counts, patches, time, gain, bias, wk, wv, lat_low, *refs):
+    q = refs[:n_keys]
+    low_o, k_o, v_o, kl_o, vl_o, stat_o, once_o, vec_o = refs[n_keys : n_keys + 8]
+    outs = refs[n_keys + 8 :]
+    step = pl.program_id(0)
+
+    @pl.when(step == 0)
+    def _():
+        kl_o[...] = mul(lat_low[...], wk[...]).astype(bf16)
+        vl_o[...] = mul(lat_low[...], wv[...]).astype(bf16)
+        row = lax.broadcasted_iota(jnp.int32, (16, gain.shape[1]), 0)
+        both = jnp.where(row % 2 == 0, gain[...], bias[...])
+        high, low = two_parts(both)
+        both = jnp.where(row < 2, high.astype(f32), jnp.where(row < 4, low.astype(f32), 0.0)).astype(bf16)
+        for i, w in enumerate((wk, wv)):
+            term = mul(both, w[...])
+            vec_o[:, i * w.shape[1] : (i + 1) * w.shape[1]] = term[:8] + pltpu.roll(term, 14, 0)[:8]
+
     for f in range(frames):
         rows = pl.ds(f * PATCH, PATCH)
-        framed = patches[0, rows, :].astype(f32) + time[0, f : f + 1, :]
+        framed = patches[0, rows, :].astype(f32) + time[pl.ds(scalars[0] * frames + f, 1), :]
         centre, scale, shifted = norm_parts(framed)
         low = (shifted * scale * gain[...] + bias[...]).astype(bf16)
         low_o[0, rows, :] = low
@@ -140,54 +164,27 @@
         once = jnp.where(lane == 0, 1.0, jnp.where(lane == 1 + f, high, 0.0))
         once_o[0, rows, :] = jnp.where(lane == 1 + frames + f, scale - high, once).astype(bf16)
 
-    @pl.when(pl.program_id(0) == pl.num_programs(0) - 1)
-    def _():
-        kl_o[...] = mul(lat_low[...], wk[...]).astype(bf16)
-        vl_o[...] = mul(lat_low[...], wv[...]).astype(bf16)
-        row = lax.broadcasted_iota(jnp.int32, (16, gain.shape[1]), 0)
-        both = jnp.where(row % 2 == 0, gain[...], bias[...])
-        high, low = two_parts(both)
-        both = jnp.where(row < 2, high.astype(f32), jnp.where(row < 4, low.astype(f32), 0.0)).astype(bf16)
-        for i, w in enumerate((wk, wv)):
-            term = mul(both, w[...])
-            vec_o[:, i * w.shape[1] : (i + 1) * w.shape[1]] = term[:8] + pltpu.roll(term, 14, 0)[:8]
-
-
-def masked_scores(query, keys, frames, first, count):
-    scores = mul(query, keys, NT)
-    parts = []
-    for f in range(frames):
-        part = scores[:, f * PATCH : (f + 1) * PATCH]
-        parts.append(jnp.where(first + f < count, part, NEG))
-    return jnp.concatenate(parts, 1) if frames > 1 else parts[0]
-
-
-def attend_kernel(n_keys, frames, scalars, counts, *refs):
-    q = refs[:n_keys]
-    kp, vp, kl, vl = refs[n_keys : n_keys + 4]
-    outs = refs[n_keys + 4 :]
-    own = q[0].shape[0]
+    own = q[0].shape[0] // pl.num_programs(0)
     inner = q[0].shape[1]
     heads = inner // HEAD
-    count = counts[pl.program_id(0)]
+    count = counts[step]
     first = scalars[0] * frames
-    query = jnp.concatenate([r[...] for r in q], 0)
+    here = pl.ds(pl.multiple_of(step * own, own), own)
+    query = jnp.concatenate([r[here, :] for r in q], 0)
     rows = query.shape[0]
     stats = jnp.zeros((rows, LANES), f32)
     shares = []
     for g in range(inner // GROUP):
         cols = slice(g * GROUP, (g + 1) * GROUP)
         wide = spread_heads(query[:, cols] * bf16(HEAD**-0.5))
-        scores = masked_scores(wide, kp[0, :, cols], frames, first, count)
-        lat_scores = mul(wide, kl[:, cols], NT)
-        top = jnp.maximum(
-            jnp.max(scores, -1, keepdims=True), jnp.max(lat_scores, -1, keepdims=True)
-        )
+        keys = jnp.concatenate([k_o[0, :, cols], kl_o[here, cols]], 0)
+        values = jnp.concatenate([v_o[0, :, cols], vl_o[here, cols]], 0)
+        scores = masked_scores(wide, keys, frames, first, count)
+        top = jnp.max(scores, -1, keepdims=True)
         raw = jnp.exp(scores - top)
-        lat_raw = jnp.exp(lat_scores - top)
-        total = jnp.sum(raw, -1, keepdims=True) + jnp.sum(lat_raw, -1, keepdims=True)
-        share = mul(raw.astype(bf16), vp[0, :, cols]) + mul(lat_raw.astype(bf16), vl[:, cols])
-        shares.append(fold_heads(share / total).astype(bf16))
+        total = jnp.sum(raw, -1, keepdims=True)
+        share = mul(raw.astype(bf16), values) * (1.0 / total)
+        shares.append(fold_heads(share).astype(bf16))
         level = top + jnp.log(total)
         row, lane = head_mask(rows, LANES, GROUP // HEAD)
         kept = jnp.where(lane % heads == row + g * (GROUP // HEAD), level, 0.0)
@@ -196,7 +193,7 @@
     lane = lax.broadcasted_iota(jnp.int32, stats.shape, 1)
     packed = jnp.concatenate(shares + [three_parts(stats, lane, 0, heads).astype(bf16)], 1)
     for s in range(n_keys):
-        outs[s][...] = packed[s * own : (s + 1) * own]
+        outs[s][here, :] = packed[s * own : (s + 1) * own]
 
 
 def sum_runs(stats, heads, start):
@@ -309,8 +306,7 @@
     for s in range(n_keys):
         owner = (scalars[0] ^ s) * c
         for m in range(n_media):
-            place = (scalars[2] ^ (m // PAIR)) * PAIR + m % PAIR
-            place = pl.ds(pl.multiple_of(place * lanes, lanes), lanes)
+            place = slice(m * lanes, (m + 1) * lanes)
             for h in range(c // lanes):
                 start = pl.multiple_of(owner + h * lanes, lanes)
                 out[s, h * r : (h + 1) * r, place] = full[
@@ -335,25 +331,49 @@
         grad_o[:units, :] = up_grad
 
 
-def attend_back_kernel(n_keys, frames, turn, heads, scalars, counts, *refs):
-    q = refs[:n_keys]
-    grads = refs[n_keys : 2 * n_keys]
-    stat = refs[2 * n_keys : 3 * n_keys]
-    kp, vp, kl, vl, k_vec, v_vec = refs[3 * n_keys : 3 * n_keys + 6]
-    n_out = 4 + n_keys
-    kv_t_o, stat_o, kl_o, vl_o = refs[-n_out : -n_keys]
-    q_o = refs[-n_keys:]
-    q_before = refs[3 * n_keys + 6 : -n_out]
-    own = q[0].shape[0]
+def attend_back_kernel(n_keys, frames, turn, heads, width, aligned, scalars, counts, *refs):
+    refs = list(refs)
+    take = lambda n: [refs.pop(0) for _ in range(n)]
+    q, grads, stat = take(n_keys), take(n_keys), take(n_keys)
+    kp, vp, kl, vl, k_vec, v_vec, low, once, norm_stat, lat_own, gain, bias = take(12)
+    rows_far, wo_far, wk_far, wv_far = take(4)
+    q_before = take(n_keys if turn else 0)
+    small_before = take(turn)
+    kv_t_o, stat_o, kl_o, vl_o, given, kept, small = take(7)
+    q_o = take(n_keys)
+    grad_acc, sums, scalar_sums, q_acc, rows_all, wo_g, wk, wv, sems = refs
+    rows = kl_o.shape[0]
+    own = rows // pl.num_programs(0)
+    dim = low.shape[2]
     per = GROUP // HEAD
-    count = counts[pl.program_id(0)]
-    first = scalars[0] * frames
+    step = pl.program_id(0)
+    count = counts[step]
+    first_frame = scalars[0] * frames
     group = scalars[5] ^ (1 - turn)
-    query = jnp.concatenate([r[...] for r in q], 0)
-    grad = jnp.concatenate([r[...] for r in grads], 0)
-    stats = jnp.concatenate([r[...] for r in stat], 0).astype(f32)
-    rows = query.shape[0]
-    row, lane = head_mask(rows, LANES, per)
+    owners = GROUP // width
+    group_cols = pl.ds(pl.multiple_of(group * GROUP, GROUP), GROUP)
+    near_rows = pl.ds(pl.multiple_of(scalars[1] * n_keys * rows, 8), n_keys * rows)
+    fetches = [
+        pltpu.make_async_copy(rows_far.at[near_rows, pl.ds(0, dim)], rows_all, sems.at[0]),
+        pltpu.make_async_copy(wo_far.at[pl.ds(owners * (1 - turn), owners)], wo_g, sems.at[1]),
+        pltpu.make_async_copy(wk_far.at[:, group_cols], wk, sems.at[2]),
+        pltpu.make_async_copy(wv_far.at[:, group_cols], wv, sems.at[3]),
+    ]
+
+    @pl.when(step == 0)
+    def _():
+        for fetch in fetches:
+            fetch.start()
+        grad_acc[...] = jnp.zeros_like(grad_acc)
+        sums[...] = jnp.zeros_like(sums)
+        scalar_sums[...] = jnp.zeros_like(scalar_sums)
+
+    here = pl.ds(pl.multiple_of(step * own, own), own)
+    query = jnp.concatenate([r[here, :] for r in q], 0)
+    grad = jnp.concatenate([r[here, :] for r in grads], 0)
+    stats = jnp.concatenate([r[here, :] for r in stat], 0).astype(f32)
+    n_query = query.shape[0]
+    row, lane = head_mask(n_query, LANES, per)
     tiled = jnp.concatenate([stats] * per, 0)
     mine = lane % heads == row + group * per
     level = jnp.sum(jnp.where(mine & (lane < 3 * heads), tiled, 0.0), -1, keepdims=True)
@@ -362,9 +382,12 @@
     )
     wide = spread_heads(query * bf16(HEAD**-0.5))
     wide_grad = spread_heads(grad)
-    scores = masked_scores(wide, kp[0], frames, first, count)
+    keys = jnp.concatenate([kp[0], kl[here, :]], 0)
+    values = jnp.concatenate([vp[0], vl[here, :]], 0)
+    n_patch = kp.shape[1]
+    scores = masked_scores(wide, keys, frames, first_frame, count)
     probs = jnp.exp(scores - level)
-    prob_grad = mul(wide_grad, vp[0], NT)
+    prob_grad = mul(wide_grad, values, NT)
     score_grad = probs * (prob_grad - delta)
     along = jnp.sum(score_grad * scores + probs * prob_grad, 0, keepdims=True)
     score_grad = score_grad.astype(bf16)
@@ -374,121 +397,110 @@
     )
     key_t = mul(key_side, score_grad, TN)
     value_t = mul(value_side, probs.astype(bf16), TN)
-    kv_t_o[0] = key_t[:GROUP].astype(bf16)
-    kv_t_o[1] = value_t[:GROUP].astype(bf16)
-    ends = key_t[GROUP:] + value_t[GROUP:]
+    kl_o[here, :] = key_t[:GROUP, n_patch:].T.astype(bf16)
+    vl_o[here, :] = value_t[:GROUP, n_patch:].T.astype(bf16)
+    kv = jnp.concatenate([key_t[:GROUP, :n_patch], value_t[:GROUP, :n_patch]], 0).astype(bf16)
+    kv_t_o[0] = kv[:GROUP]
+    kv_t_o[1] = kv[GROUP:]
+    ends = key_t[GROUP:, :n_patch] + value_t[GROUP:, :n_patch]
     line = lax.broadcasted_iota(jnp.int32, ends.shape, 0)
-    stat_o[...] = jnp.where(line == 1, along - ends, ends)
-    lat_probs = jnp.exp(mul(wide, kl[...], NT) - level)
-    lat_prob_grad = mul(wide_grad, vl[...], NT)
-    lat_score_grad = (lat_probs * (lat_prob_grad - delta)).astype(bf16)
-    kl_o[...] = mul(lat_score_grad, wide, TN).astype(bf16)
-    vl_o[...] = mul(lat_probs.astype(bf16), wide_grad, TN).astype(bf16)
-    query_grad = mul(score_grad, kp[0]) + mul(lat_score_grad, kl[...])
+    stat_rows = jnp.where(line == 1, along[:, :n_patch] - ends, ends)
+    span = pl.ds(pl.multiple_of(step * n_patch, n_patch), n_patch)
+    stat_o[:, span] = stat_rows
+
+    scale = norm_stat[1:2, span] * (1.0 / dim)
+    first = stat_rows[0:1, :] * scale
+    second = stat_rows[1:2, :] * scale
+    frame = lax.broadcasted_iota(jnp.int32, (16, n_patch), 1) // PATCH
+    row16 = lax.broadcasted_iota(jnp.int32, (16, n_patch), 0)
+    high = second.astype(bf16).astype(f32)
+    same = frame == row16 % frames
+    ends = jnp.where(same & (row16 < frames), high, 0.0)
+    ends = jnp.where(same & (row16 >= frames) & (row16 < 2 * frames), second - high, ends)
+    grad_acc[...] += mul(jnp.concatenate([kv, ends.astype(bf16)], 0), low[0])
+    sums[...] += mul(kv, once[0])
+    line = lax.broadcasted_iota(jnp.int32, scalar_sums.shape, 0)
+    adds = jnp.zeros(scalar_sums.shape, f32)
+    for f in range(frames):
+        span = slice(f * PATCH, (f + 1) * PATCH)
+        adds = jnp.where(line == f, jnp.sum(first[:, span], -1, keepdims=True), adds)
+        adds = jnp.where(line == frames + f, jnp.sum(second[:, span], -1, keepdims=True), adds)
+    scalar_sums[...] += adds
+
+    query_grad = mul(score_grad, keys)
     query_grad = (fold_heads(query_grad) * HEAD**-0.5).astype(bf16)
-    if turn == 0:
-        for s in range(n_keys):
-            q_o[s][...] = query_grad[s * own : (s + 1) * own]
+    for s in range(n_keys):
+        part = query_grad[s * own : (s + 1) * own]
+        place = pl.multiple_of((scalars[0] ^ s) * rows + step * own, own)
+        q_acc[pl.ds(place, own), :] = part
+        if turn == 0:
+            q_o[s][here, :] = part
+        else:
+            other = pl.ds(pl.multiple_of((1 - group) * GROUP, GROUP), GROUP)
+            q_o[s][here, group_cols] = part
+            q_o[s][here, other] = q_before[s][here, :]
+
+    @pl.when(step == pl.num_programs(0) - 1)
+    def _():
+        for fetch in fetches:
+            fetch.wait()
+        behind = None
+        for part in two_parts(sums[...]):
+            for i, w in enumerate((wk, wv)):
+                term = mul(part[i * GROUP : (i + 1) * GROUP], w[...], ((0,), (1,)))
+                behind = term if behind is None else behind + term
+        bias_grad = behind[0:1]
+        main = grad_acc[: 2 * GROUP, :]
+        ends = grad_acc[2 * GROUP :, :]
+        total = jnp.sum(main[:GROUP] * wk[...].astype(f32).T, 0, keepdims=True)
+        total = total + jnp.sum(main[GROUP:] * wv[...].astype(f32).T, 0, keepdims=True)
+        over = 1.0 / gain[...]
+        lines = []
+        for f in range(frames):
+            along = ends[f : f + 1] + ends[frames + f : frames + f + 1]
+            scaled = behind[1 + f : 2 + f] + behind[1 + frames + f : 2 + frames + f]
+            second_sum = scalar_sums[frames + f : frames + f + 1, 0:1]
+            lines.append(
+                gain[...] * scaled
+                - scalar_sums[f : f + 1, 0:1]
+                - (along - bias[...] * second_sum) * over
+            )
+        lines += [(total - bias[...] * bias_grad) * over, bias_grad]
+        for i, value in enumerate(lines):
+            small[i : i + 1, :] = value + small_before[0][i : i + 1, :] if turn else value
+        kv_lat = jnp.concatenate([kl_o[...], vl_o[...]], 1)
+        grad_acc[: 2 * GROUP, :] = main + mul(kv_lat, lat_own[...], TN)
+        q_grad = mul(q_acc[...], rows_all[...], TN)
+        sums_q = q_grad.astype(bf16)
+        near = scalars[1] if aligned else 0
+        runs = dim // PAIR // LANES
+        for j in range(owners):
+            out = (given, kept)[j % 2]
+            slot = 2 * (j // 2) + 1 - j % 2
+            start = ((scalars[0] ^ slot) % owners) * width
+            for part in range(3):
+                at = pl.multiple_of((part - 1) * GROUP + start, width)
+                if part == 0:
+                    piece = jnp.zeros((width, dim), bf16)
+                    for o in range(owners):
+                        same = start == o * width
+                        piece = jnp.where(same, sums_q[o * width : (o + 1) * width], piece)
+                else:
+                    piece = grad_acc[pl.ds(at, width), :].astype(bf16)
+                place_rows(out, scalars, j // 2, part * width, piece, aligned)
+            place_rows(out, scalars, j // 2, 3 * width, wo_g[slot], aligned)
+
+
+def place_rows(out, scalars, slot, start, piece, aligned):
+    rows = slice(start, start + piece.shape[0])
+    half = piece.shape[1] // PAIR
+    if aligned:
+        for m in range(piece.shape[1] // LANES):
+            place = pl.ds(pl.multiple_of((scalars[2] ^ (m // PAIR)) * LANES, LANES), LANES)
+            out[slot, scalars[1] ^ (m % PAIR), rows, place] = piece[:, m * LANES : (m + 1) * LANES]
     else:
-        here = pl.ds(pl.multiple_of(group * GROUP, GROUP), GROUP)
-        there = pl.ds(pl.multiple_of((1 - group) * GROUP, GROUP), GROUP)
-        for s in range(n_keys):
-            q_o[s][:, here] = query_grad[s * own : (s + 1) * own]
-            q_o[s][:, there] = q_before[s][...]
-
-
-def weight_kernel(
-    n_keys,
-    turn,
-    width,
-    frames,
-    aligned,
-    scalars,
-    kv_t,
-    low,
-    kl_g,
-    vl_g,
-    lat_own,
-    rows_all,
-    wo_g,
-    once,
-    norm_stat,
-    grad_stat,
-    wk,
-    wv,
-    gain,
-    bias,
-    *refs,
-):
-    q_grads = refs[:n_keys]
-    before = refs[n_keys:-5]
-    given, kept, small, total, sums = refs[-5:]
-    rows = q_grads[0].shape[0]
-    per = GROUP // width
-    kv = jnp.concatenate([kv_t[0], kv_t[1]], 0)
-    keys = kv.shape[1]
-
-    @pl.when(pl.program_id(0) == 0)
-    def _():
-        sums[...] = mul(kv, once[...])
-
-    inverse = 1.0 / (scalars[6].astype(f32))
-    scale = norm_stat[1:2, :] * inverse
-    first = grad_stat[0:1, :] * scale
-    second = grad_stat[1:2, :] * scale
-    frame = (lax.broadcasted_iota(jnp.int32, (16, keys), 1) // PATCH) % frames
-    row = lax.broadcasted_iota(jnp.int32, (16, keys), 0)
-    high = second.astype(bf16).astype(f32)
-    mine = frame == row % frames
-    ends = jnp.where(mine & (row < frames), high, 0.0)
-    ends = jnp.where(mine & (row >= frames) & (row < 2 * frames), second - high, ends)
-    out = mul(jnp.concatenate([kv, ends.astype(bf16)], 0), low[...])
-    main = out[: 2 * GROUP]
-    ends = out[2 * GROUP :]
-    behind = None
-    for part in two_parts(sums[...]):
-        for i, w in enumerate((wk, wv)):
-            term = mul(part[i * GROUP : (i + 1) * GROUP], w[...], ((0,), (1,)))
-            behind = term if behind is None else behind + term
-    bias_grad = behind[0:1]
-    turned = jnp.concatenate([wk[...].astype(f32).T, wv[...].astype(f32).T], 0)
-    over = 1.0 / gain[...]
-    gain_grad = (jnp.sum(main * turned, 0, keepdims=True) - bias[...] * bias_grad) * over
-    lines = []
-    for f in range(frames):
-        here = frame[0:1] == f
-        first_sum = jnp.sum(jnp.where(here, first, 0.0), -1, keepdims=True)
-        second_sum = jnp.sum(jnp.where(here, second, 0.0), -1, keepdims=True)
-        along = ends[f : f + 1] + ends[frames + f : frames + f + 1]
-        scaled = behind[1 + f : 2 + f] + behind[1 + frames + f : 2 + frames + f]
-        lines.append(gain[...] * scaled - first_sum - (along - bias[...] * second_sum) * over)
-    for i, line in enumerate(lines + [gain_grad, bias_grad]):
-        small[i : i + 1, :] = line + before[0][i : i + 1, :] if turn else line
-
-    kv_lat = jnp.concatenate([kl_g[...], vl_g[...]], 1)
-    total[GROUP:, :] = main + mul(kv_lat, lat_own[...], TN)
-    base = scalars[1] * n_keys
-    query = None
-    for s in range(n_keys):
-        slot = pl.ds(pl.multiple_of((base + (scalars[0] ^ s)) * rows, 8), rows)
-        term = mul(q_grads[s][...], rows_all[slot, :], TN)
-        query = term if query is None else query + term
-    total[:GROUP, :] = query
-    near = scalars[1] if aligned else 0
-    lanes = total.shape[1] // PAIR
-    for j in range(per):
-        out = (given, kept)[j % 2]
-        slot = per * (1 - turn) + 2 * (j // 2) + 1 - j % 2
-        start = ((scalars[0] ^ slot) % per) * width
-        for part in range(3):
-            piece = total[pl.ds(pl.multiple_of(part * GROUP + start, width), width), :].astype(bf16)
-            for n in range(PAIR):
-                out[j // 2, near ^ n, part * width : (part + 1) * width, :] = piece[
-                    :, n * lanes : (n + 1) * lanes
-                ]
-        piece = wo_g[slot]
         for n in range(PAIR):
-            out[j // 2, near ^ n, 3 * width :, :] = piece[:, n * lanes : (n + 1) * lanes]
+            out[slot, n, rows, :] = piece[:, n * half : (n + 1) * half]
 
 
 def patch_back_kernel(
@@ -510,7 +522,7 @@
         grad = grad + mul(kv_a[1, :, span], wv_a[...], turned)
         grad = grad + mul(kv_b[0, :, span], wk_b[...], turned)
         grad = grad + mul(kv_b[1, :, span], wv_b[...], turned)
-        framed = patches[0, rows, :].astype(f32) + time[0, f : f + 1, :]
+        framed = patches[0, rows, :].astype(f32) + time[pl.ds(scalars[0] * frames + f, 1), :]
         back = grad * gain[...] * columns[:, 0:1] - columns[:, 1:2] - framed * columns[:, 2:3]
         grad_o[0, rows, :] = back.astype(bf16)
 
@@ -536,24 +548,22 @@
     small_o[n_frames + 4 : n_frames + 6, :] = ff_small[...]
 
 
-def finish_kernel(width, scalars, *refs):
-    parts = refs[:-4]
-    q_o, k_o, v_o, out_o = refs[-4:]
+def finish_kernel(width, scalars, up_keep, up_got, down, *refs):
+    parts = refs[:-6]
+    q_o, k_o, v_o, out_o, up_o, down_o = refs[-6:]
     total = functools.reduce(jnp.add, [r[...].astype(f32) for r in parts])
     for i, ref in enumerate((q_o, k_o, v_o)):
         ref[...] = total[i * width : (i + 1) * width].T
     r = out_o.shape[0]
     for h in range(out_o.shape[1] // LANES):
         out_o[:, h * LANES : (h + 1) * LANES] = total[3 * width + h * r : 3 * width + (h + 1) * r]
-
-
-def finish_up_kernel(scalars, keep, got, out):
-    units = keep.shape[0]
+    units = up_keep.shape[0]
     near = scalars[1]
     own = pl.ds(pl.multiple_of(near * units, LANES), units)
     other = pl.ds(pl.multiple_of((1 - near) * units, LANES), units)
-    out[:, own] = keep[...].astype(f32).T
-    out[:, other] = got[...].astype(f32).T
+    up_o[:, own] = up_keep[...].astype(f32).T
+    up_o[:, other] = up_got[...].astype(f32).T
+    down_o[...] = down[...].astype(f32)
 
 
 def whole(shape):
@@ -562,6 +572,12 @@
 
 def struct(shape, dtype):
     return jax.ShapeDtypeStruct(shape, dtype)
+
+
+def tree_sum(parts):
+    while len(parts) > 1:
+        parts = [parts[i] + parts[i + 1] for i in range(0, len(parts), 2)]
+    return parts[0]
 
 
 def shards(
@@ -630,12 +646,10 @@
     lat = latents.reshape(rows, dim)
     cot = cotangent.reshape(rows, dim)
     row = lambda v: v.reshape(1, dim)
-    time_blocks = time_embedding.reshape(n_keys, frames, dim)
     packed = inner + LANES
-    own_block = lambda w: pl.BlockSpec((own, w), lambda i, *_: (i, 0))
     patch_block = pl.BlockSpec((1, key_rows, dim), lambda i, *_: (i, 0, 0))
     inner_block = pl.BlockSpec((1, key_rows, inner), lambda i, *_: (i, 0, 0))
-    time_block = pl.BlockSpec((1, frames, dim), lambda i, s, *_: (s[0], 0, 0))
+    time_block = whole((n_frames, dim))
     stat_block = pl.BlockSpec((8, key_rows), lambda i, *_: (0, i))
     patch_flops = 4 * all_rows * dim * inner
     att_flops = 4 * media * n_keys * own * (key_rows + own) * inner * (GROUP // HEAD)
@@ -678,9 +692,9 @@
     q_all = exchange_keys([q_own] * n_keys)
     rows_all = lax.all_gather(own_rows, ("near", "keys"), axis=0, tiled=True)
 
-    media_low, kp, vp, kl, vl, norm_stat, once, norm_vec = call(
-        functools.partial(patch_kernel, frames),
-        "patch_project",
+    out = call(
+        functools.partial(patch_kernel, n_keys, frames),
+        "project_attend",
         (media,),
         [
             patch_block,
@@ -690,7 +704,8 @@
             whole((dim, inner)),
             whole((dim, inner)),
             whole((rows, dim)),
-        ],
+        ]
+        + [whole((rows, inner))] * n_keys,
         [
             patch_block,
             inner_block,
@@ -700,8 +715,9 @@
             stat_block,
             pl.BlockSpec((1, key_rows, LANES), lambda i, *_: (i, 0, 0)),
             whole((8, 2 * inner)),
-        ],
-        (
+        ]
+        + [whole((rows, packed))] * n_keys,
+        [
             struct(patches.shape, bf16),
             struct((media, key_rows, inner), bf16),
             struct((media, key_rows, inner), bf16),
@@ -710,30 +726,24 @@
             struct((8, all_rows), f32),
             struct((media, key_rows, LANES), bf16),
             struct((8, 2 * inner), f32),
-        ),
-        cost(patch_flops, 12 * all_rows * dim),
+        ]
+        + [struct((rows, packed), bf16)] * n_keys,
+        cost(patch_flops + att_flops, 12 * all_rows * dim),
+        prefetch=2,
     )(
         scalars,
+        frame_counts,
         patches,
-        time_blocks,
+        time_embedding,
         row(media_gain),
         row(media_bias),
         key_weight,
         value_weight,
         own_rows,
+        *q_all,
     )
-
-    shares = call(
-        functools.partial(attend_kernel, n_keys, frames),
-        "attend",
-        (media,),
-        [own_block(inner)] * n_keys
-        + [inner_block, inner_block, own_block(inner), own_block(inner)],
-        [own_block(packed)] * n_keys,
-        [struct((rows, packed), bf16)] * n_keys,
-        cost(att_flops, 4 * all_rows * inner),
-        prefetch=2,
-    )(scalars, frame_counts, *q_all, kp, vp, kl, vl)
+    media_low, kp, vp, kl, vl, norm_stat, once, norm_vec = out[:8]
+    shares = out[8:]
     joined = exchange_keys(shares)
 
     attended, att_low, middle, ff_low, lse = call(
@@ -758,9 +768,10 @@
         ),
         cost(2 * rows * inner * dim, 2 * inner * dim + 16 * rows * dim),
     )(scalars, lat, row(ff_gain), row(ff_bias), out_weight, *joined)
+    ff_low, rows_all = tie(ff_low, rows_all)
     ff_all = lax.all_gather(ff_low, ("near", "keys"), axis=0, tiled=True)
 
-    chunk = min(512, hidden)
+    chunk = min(1024, hidden)
     wo_rows = inner * dim // n_keys // dim
     wo_shape = (n_keys, wo_rows, dim) if aligned else (inner, dim)
     resampled, mid_grad, pack, ff_small, out_slots = call(
@@ -827,14 +838,23 @@
     pick = lambda turn: (lambda s: s[5] ^ (1 - turn))
     high = 3 * width + wo_rows
 
-    def attend_back(turn, packs, before):
+    def regroup(value):
+        value = jnp.moveaxis(value, 1, 2).reshape(-1, high, n_far, PAIR, each)
+        value = value.transpose(0, 3, 1, 2, 4).reshape(-1, PAIR, high, n_far * each)
+        return jnp.where(near == 0, value, value[:, ::-1])
+
+    def attend_back(turn, packs, q_before, small_before):
         g = pick(turn)
-        own_cols = pl.BlockSpec((own, GROUP), lambda i, s, *_: (i, g(s)))
-        stat_cols = pl.BlockSpec((own, LANES), lambda i, *_: (i, inner // LANES))
+        own_cols = pl.BlockSpec((rows, GROUP), lambda i, s, *_: (0, g(s)))
+        stat_cols = pl.BlockSpec((rows, LANES), lambda i, *_: (0, inner // LANES))
         key_cols = pl.BlockSpec((1, key_rows, GROUP), lambda i, s, *_: (i, 0, g(s)))
+        far_spec = pl.BlockSpec(memory_space=pl.ANY)
         q_width = GROUP if turn == 0 else inner
+        chain = (n_keys // 4, PAIR, high, dim // PAIR)
         out = call(
-            functools.partial(attend_back_kernel, n_keys, frames, turn, inner // HEAD),
+            functools.partial(
+                attend_back_kernel, n_keys, frames, turn, inner // HEAD, width, aligned
+            ),
             "attend_back",
             (media,),
             [own_cols] * (2 * n_keys)
@@ -843,24 +863,49 @@
             + [
                 pl.BlockSpec((8, GROUP), lambda i, s, *_: (0, g(s))),
                 pl.BlockSpec((8, GROUP), lambda i, s, *_: (0, inner // GROUP + g(s))),
+                patch_block,
+                pl.BlockSpec((1, key_rows, LANES), lambda i, *_: (i, 0, 0)),
+                whole((8, all_rows)),
+                pl.BlockSpec((rows, dim), lambda i, *_: (0, 0)),
+                whole((1, dim)),
+                whole((1, dim)),
             ]
-            + [own_block(GROUP)] * len(before),
+            + [far_spec] * 4
+            + [whole((rows, GROUP))] * len(q_before)
+            + [whole((8, dim))] * len(small_before),
             [
                 pl.BlockSpec((2, GROUP, key_rows), lambda i, *_: (0, 0, i)),
-                stat_block,
-                own_block(GROUP),
-                own_block(GROUP),
+                whole((8, all_rows)),
+                whole((rows, GROUP)),
+                whole((rows, GROUP)),
+                whole(chain),
+                whole(chain),
+                whole((8, dim)),
             ]
-            + [own_block(q_width)] * n_keys,
+            + [whole((rows, q_width))] * n_keys,
             [
                 struct((2, GROUP, all_rows), bf16),
                 struct((8, all_rows), f32),
                 struct((rows, GROUP), bf16),
                 struct((rows, GROUP), bf16),
+                struct(chain, bf16),
+                struct(chain, bf16),
+                struct((8, dim), f32),
             ]
             + [struct((rows, q_width), bf16)] * n_keys,
-            cost(5 * att_flops // 4, 4 * all_rows * inner),
+            cost(5 * att_flops // 4 + patch_flops // 2, 4 * all_rows * (inner + dim)),
             prefetch=2,
+            scratch_shapes=[
+                pltpu.VMEM((2 * GROUP + 16, dim), f32),
+                pltpu.VMEM((2 * GROUP, LANES), f32),
+                pltpu.VMEM((8, LANES), f32),
+                pltpu.VMEM((n_keys * rows, GROUP), bf16),
+                pltpu.VMEM((n_keys * rows, dim), bf16),
+                pltpu.VMEM((GROUP // width, wo_rows, dim), bf16),
+                pltpu.VMEM((dim, GROUP), bf16),
+                pltpu.VMEM((dim, GROUP), bf16),
+                pltpu.SemaphoreType.DMA((4,)),
+            ],
         )(
             scalars,
             frame_counts,
@@ -873,80 +918,24 @@
             vl,
             norm_vec,
             norm_vec,
-            *before,
-        )
-        return out[:4], out[4:]
-
-    def regroup(value):
-        value = jnp.moveaxis(value, 1, 2).reshape(-1, high, n_far, PAIR, each)
-        value = value.transpose(0, 3, 1, 2, 4).reshape(-1, PAIR, high, n_far * each)
-        return jnp.where(near == 0, value, value[:, ::-1])
-
-    def weights(turn, kv_t, stat, kl_g, vl_g, q_grads, before):
-        g = pick(turn)
-        lanes = dim // n_far
-        cols = pl.BlockSpec((rows, GROUP), lambda i, s: (0, g(s) if turn else 0))
-        place = (lambda i, s: (0, 0, 0, i ^ s[2])) if aligned else (lambda i, s: (0, 0, 0, i))
-        if aligned:
-            grid, run = (n_far,), lanes
-            out = [pl.BlockSpec((n_keys // 4, PAIR, high, run // PAIR), place)] * 2
-        else:
-            grid, run = (1,), dim
-            out = [whole((n_keys // 4, PAIR, high, dim // PAIR))] * 2
-        small_run = pl.BlockSpec((8, run), lambda i, s: (0, i))
-        wo_run = pl.BlockSpec((n_keys, wo_rows, run), (lambda i, s: (0, 0, i ^ s[2])) if aligned else (lambda i, s: (0, 0, 0)))
-        grads = call(
-            functools.partial(weight_kernel, n_keys, turn, width, frames, aligned),
-            "projection_weights",
-            grid,
-            [
-                whole((2, GROUP, all_rows)),
-                pl.BlockSpec((all_rows, run), lambda i, s: (0, i)),
-                whole((rows, GROUP)),
-                whole((rows, GROUP)),
-                pl.BlockSpec((rows, run), lambda i, s: (0, i)),
-                pl.BlockSpec((group_rows, run), lambda i, s: (0, i)),
-                wo_run,
-                whole((all_rows, LANES)),
-                whole((8, all_rows)),
-                whole((8, all_rows)),
-                pl.BlockSpec((run, GROUP), lambda i, s: (i, g(s))),
-                pl.BlockSpec((run, GROUP), lambda i, s: (i, g(s))),
-                pl.BlockSpec((1, run), lambda i, s: (0, i)),
-                pl.BlockSpec((1, run), lambda i, s: (0, i)),
-            ]
-            + [cols] * n_keys
-            + [small_run] * len(before),
-            out + [small_run],
-            [struct((n_keys // 4, PAIR, high, dim // PAIR), bf16)] * 2 + [struct((8, dim), f32)],
-            cost(patch_flops // 2, 4 * all_rows * dim),
-            scratch_shapes=[pltpu.VMEM((3 * GROUP, run), f32), pltpu.VMEM((2 * GROUP, LANES), f32)],
-        )(
-            scalars,
-            kv_t,
-            media_low.reshape(all_rows, dim),
-            kl_g,
-            vl_g,
+            media_low,
+            once,
+            norm_stat,
             own_rows,
+            row(media_gain),
+            row(media_bias),
             rows_all,
             out_slots,
-            once.reshape(all_rows, LANES),
-            norm_stat,
-            stat,
             key_weight,
             value_weight,
-            row(media_gain),
-            row(media_bias),
-            *q_grads,
-            *before,
+            *q_before,
+            *small_before,
         )
-        return grads if aligned else [regroup(v) for v in grads[:2]] + [grads[2]]
+        chains = out[4:6] if aligned else [regroup(v) for v in out[4:6]]
+        return out[:4], chains, out[6], out[7:]
 
     group_rows = PAIR * n_keys * rows
-    (kv_a, stat_a, kl_a, vl_a), q_a = attend_back(0, packs, [])
-    given_a, kept_a, media_small = weights(0, kv_a, stat_a, kl_a, vl_a, q_a, [])
-    far_core = over_keys(given_a, 1)
-    ff_all, kept_a = tie(ff_all, kept_a)
+    ff_all, *packs = tie(ff_all, *packs)
 
     units = hidden // (n_keys * PAIR)
     ff_partial = call(
@@ -971,54 +960,19 @@
         ups = ff_partial[:units].reshape(units, n_far, PAIR, each)
         ups = jnp.where(near == 0, ups, ups[:, :, ::-1]).reshape(units, dim)
         ff_partial = jnp.concatenate([ups, pieces], 0)
-    far_core, ff_partial = tie(far_core, ff_partial)
+    ff_partial, packs[0] = tie(ff_partial, packs[0])
     ff_sum = lax.psum_scatter(ff_partial, "far", scatter_dimension=1, tiled=True)
+
+    (kv_a, stat_a, kl_a, vl_a), (given_a, kept_a), media_small, q_a = attend_back(0, packs, [], [])
+    far_core = over_keys(given_a, 1)
+    (kv_b, stat_b, kl_b, vl_b), (given_b, kept_b), media_small, q_b = attend_back(
+        1, packs, q_a, [media_small]
+    )
+    far_core, given_b, *q_b = tie(far_core, given_b, *q_b)
     far_sum = add(kept_a, far_core)
-    far_sum, packs[0] = tie(far_sum, packs[0])
-    far_near = over_near(far_sum[:, 1])
-    (kv_b, stat_b, kl_b, vl_b), q_b = attend_back(1, packs, q_a)
-    q_slots = exchange_keys(q_b)
-    far_near, kv_b = tie(far_near, kv_b)
-    far_half = add(far_sum[:, 0], far_near)
-    far_half, kv_b = tie(far_half, kv_b)
-    far_got = [over_keys(far_half[j], half_keys + 2 * j) for j in range(n_keys // 4)]
-    given_b, kept_b, media_small = weights(1, kv_b, stat_b, kl_b, vl_b, q_b, [media_small])
-    near_core = over_keys(given_b, 1)
-    kept_b, lat = tie(kept_b, lat)
 
     col = lambda turn: pl.BlockSpec((dim, GROUP), lambda i, s: (0, s[5] ^ (1 - turn)))
     both = lambda value: [value, value]
-    small_rows = -(-(n_frames + 6) // 8) * 8
-    latents_grad, small = call(
-        functools.partial(latent_back_kernel, n_keys, frames, n_frames),
-        "latent_back",
-        (1,),
-        [whole((rows, dim)), whole((1, dim)), whole((rows, dim)), whole((8, dim)), whole((2, dim))]
-        + [whole((rows, GROUP)), col(0), whole((rows, GROUP)), col(0)]
-        + [whole((rows, GROUP)), col(1), whole((rows, GROUP)), col(1)]
-        + [whole((dim, inner))]
-        + [whole((rows, inner))] * n_keys,
-        [whole((rows, dim)), whole((small_rows, dim))],
-        (struct((rows, dim), f32), struct((small_rows, dim), f32)),
-        cost(6 * rows * dim * inner, 6 * dim * inner + 20 * rows * dim),
-    )(
-        scalars,
-        lat,
-        row(latent_gain),
-        mid_grad,
-        media_small,
-        ff_small,
-        kl_a,
-        key_weight,
-        vl_a,
-        value_weight,
-        kl_b,
-        key_weight,
-        vl_b,
-        value_weight,
-        query_weight,
-        *q_slots,
-    )
 
     pieces = 3
     each_piece = media // pieces
@@ -1059,7 +1013,7 @@
             stat_b,
             norm_stat,
             patches,
-            time_blocks,
+            time_embedding,
             gain,
             key_weight,
             value_weight,
@@ -1068,40 +1022,74 @@
             gain if piece == 0 else patches_grad,
         )
 
-    def butterfly(value, step):
-        axis, shift = step
-        size = {"keys": n_keys, "near": PAIR, "far": n_far}[axis]
-        return lax.ppermute(value, axis, [(i, i ^ shift) for i in range(size)])
-
-    steps = [
-        (axis, 1 << i)
-        for axis, size in (("keys", n_keys), ("near", PAIR), ("far", n_far))
-        for i in range(size.bit_length() - 1)
-    ]
+    def sum_far(value):
+        return tree_sum([value] + [over_far(value, s) for s in range(1, n_far)])
+
     gain = row(media_gain)
-    small = small + butterfly(small, steps[0])
-    near_core, latents_grad = tie(near_core, latents_grad)
+    far_sum, gain, given_b, *q_b = tie(far_sum, gain, given_b, *q_b)
+    far_near = over_near(far_sum[:, 1])
+    near_core = over_keys(given_b, 1)
+    q_slots = exchange_keys(q_b)
+    patches_grad = patch_back(0, gain, None)
+    patches_grad, far_near, near_core, *q_slots = tie(patches_grad, far_near, near_core, *q_slots)
+    far_half = add(far_sum[:, 0], far_near)
     near_sum = add(kept_b, near_core)
+    near_sum, far_half, lat, ff_sum = tie(near_sum, far_half, lat, ff_sum)
+    far_got = [over_keys(far_half[j], half_keys + 2 * j) for j in range(n_keys // 4)]
     total = near_sum[0]
     for j in range(1, n_keys // 4):
         total = add(total, over_keys(near_sum[j], 2 * j))
-    total, small, gain = tie(total, small, gain)
     near_got = over_near(total[1])
-    small_got = butterfly(small, steps[1])
-    patches_grad = patch_back(0, gain, None)
-    patches_grad, small_got, *far_got = tie(patches_grad, small_got, *far_got)
+    route = []
+    for m in range(n_media):
+        for k in range(n_keys):
+            block, owner = divmod(m // PAIR, n_keys)
+            target = (k * PAIR + m % PAIR) * blocks + block
+            route.append((m * n_keys + k, target * n_keys + owner))
+    down_grad = lax.ppermute(ff_sum[units:], ("far", "near", "keys"), route)
+    small_rows = -(-(n_frames + 6) // 8) * 8
+    latents_grad, small = call(
+        functools.partial(latent_back_kernel, n_keys, frames, n_frames),
+        "latent_back",
+        (1,),
+        [whole((rows, dim)), whole((1, dim)), whole((rows, dim)), whole((8, dim)), whole((2, dim))]
+        + [whole((rows, GROUP)), col(0), whole((rows, GROUP)), col(0)]
+        + [whole((rows, GROUP)), col(1), whole((rows, GROUP)), col(1)]
+        + [whole((dim, inner))]
+        + [whole((rows, inner))] * n_keys,
+        [whole((rows, dim)), whole((small_rows, dim))],
+        (struct((rows, dim), f32), struct((small_rows, dim), f32)),
+        cost(6 * rows * dim * inner, 6 * dim * inner + 20 * rows * dim),
+    )(
+        scalars,
+        lat,
+        row(latent_gain),
+        mid_grad,
+        media_small,
+        ff_small,
+        kl_a,
+        key_weight,
+        vl_a,
+        value_weight,
+        kl_b,
+        key_weight,
+        vl_b,
+        value_weight,
+        query_weight,
+        *q_slots,
+    )
+
+    gain, small, ff_sum = tie(gain, small, ff_sum)
+    small_got = over_keys(small, 1)
+    up_keep = ff_sum[:units, :each]
+    up_got = over_near(ff_sum[:units, each:])
+    patches_grad = patch_back(1, gain, patches_grad)
+    patches_grad, small_got, near_got, *far_got = tie(patches_grad, small_got, near_got, *far_got)
+    small = small + small_got
     total = total[0]
     for value in far_got:
         total = add(total, value)
-    small = small + small_got
-    total, small, gain, ff_sum = tie(total, small, gain, ff_sum)
-    small_got = butterfly(small, steps[2])
-    up_keep = ff_sum[:units, :each]
-    up_got = over_near(ff_sum[:units, each:])
-    patches_grad = patch_back(1, gain, patches_grad)
-    patches_grad, small_got, near_got, up_got = tie(patches_grad, small_got, near_got, up_got)
     total = add(total, near_got)
-    small = small + small_got
     if not aligned:
         total = total.reshape(-1, n_far, each)
         total = jnp.concatenate(
@@ -1109,54 +1097,48 @@
         )
     total, small, gain = tie(total, small, gain)
     parts = [over_far(total[:, s * each : (s + 1) * each], s) for s in range(1, n_far)]
-    small_got = butterfly(small, steps[3])
-    route = []
-    for m in range(n_media):
-        for k in range(n_keys):
-            block, owner = divmod(m // PAIR, n_keys)
-            target = (k * PAIR + m % PAIR) * blocks + block
-            route.append((m * n_keys + k, target * n_keys + owner))
-    down_grad = lax.ppermute(ff_sum[units:], ("far", "near", "keys"), route)
+    small = tree_sum([small] + [over_keys(small, s) for s in range(2, n_keys, 2)])
     patches_grad = patch_back(2, gain, patches_grad)
-    patches_grad, small_got, down_grad, *parts = tie(patches_grad, small_got, down_grad, *parts)
+    patches_grad, small, up_got, down_grad, *parts = tie(
+        patches_grad, small, up_got, down_grad, *parts
+    )
+    small = small + over_near(small)
+    small, up_got = tie(small, up_got)
+    small = sum_far(small)
     parts = [total[:, :each]] + parts
-    small = small + small_got
-    for step in steps[4:]:
-        small = small + butterfly(small, step)
     if aligned:
-        up_grad = call(
-            finish_up_kernel,
-            "finish_up",
+        q_grad, k_grad, v_grad, out_grad, up_grad, down_grad = call(
+            functools.partial(finish_kernel, width),
+            "finish_weights",
             (1,),
-            [whole((units, each))] * 2,
-            whole((each, PAIR * units)),
-            struct((each, PAIR * units), f32),
-            cost(0, 8 * units * each),
-        )(scalars, up_keep, up_got)
+            [whole((units, each))] * 2
+            + [whole((units, dim // n_keys))]
+            + [whole(p.shape) for p in parts],
+            [whole((each, width))] * 3
+            + [
+                whole((inner // n_media, dim // n_keys)),
+                whole((each, PAIR * units)),
+                whole((units, dim // n_keys)),
+            ],
+            [struct((each, width), f32)] * 3
+            + [
+                struct((inner // n_media, dim // n_keys), f32),
+                struct((each, PAIR * units), f32),
+                struct((units, dim // n_keys), f32),
+            ],
+            cost(0, 16 * width * each + 12 * units * each),
+        )(scalars, up_keep, up_got, down_grad, *parts)
     else:
+        total = functools.reduce(jnp.add, [p.astype(f32) for p in parts])
+        q_grad, k_grad, v_grad = (total[i * width : (i + 1) * width].T for i in range(3))
+        out_grad = total[3 * width :].reshape(-1, inner // n_media, each)
+        out_grad = out_grad.transpose(1, 0, 2).reshape(inner // n_media, dim // n_keys)
         up_grad = jnp.where(
             near == 0,
             jnp.concatenate([up_keep, up_got], 0),
             jnp.concatenate([up_got, up_keep], 0),
         ).T.astype(f32)
-    down_grad = down_grad.reshape(units // blocks, dim // n_keys).astype(f32)
-
-    if aligned:
-        q_grad, k_grad, v_grad, out_grad = call(
-            functools.partial(finish_kernel, width),
-            "finish_projections",
-            (1,),
-            [whole(p.shape) for p in parts],
-            [whole((each, width))] * 3 + [whole((inner // n_media, dim // n_keys))],
-            [struct((each, width), f32)] * 3
-            + [struct((inner // n_media, dim // n_keys), f32)],
-            cost(0, 16 * width * each),
-        )(scalars, *parts)
-    else:
-        total = functools.reduce(jnp.add, [p.astype(f32) for p in parts])
-        q_grad, k_grad, v_grad = (total[i * width : (i + 1) * width].T for i in range(3))
-        out_grad = total[3 * width :].reshape(-1, inner // n_media, each)
-        out_grad = out_grad.transpose(1, 0, 2).reshape(inner // n_media, dim // n_keys)
+        down_grad = down_grad.reshape(units // blocks, dim // n_keys).astype(f32)
 
     return (
         resampled.reshape(latents.shape),

time: 222 us -> 201 us (0.905)
  Pallas kernels: 139 us -> 116 us
  waiting for transfers between devices: 27.9 us -> 34.3 us
  local copies, waits for them, and re-layouts: 9.35 us -> 6.45 us
    pallas_call x16 -> x12, Pallas kernels: 139 us -> 116 us  [pinned(): return run(*args)]
    ppermute x5 -> x0, starting transfers between devices: 5.95 us -> none  [butterfly(): return lax.ppermute(value, axis, [(i, i ^ shift) for i in range(size)])]
    ppermute x3 -> x4, waiting for transfers between devices: 1.39 us -> 6.54 us  [over_near(): return lax.ppermute(value, 'near', [(0, 1), (1, 0)])]
    ppermute x3 -> x6, starting transfers between devices: 4.39 us -> 8.22 us  [over_far(): return lax.ppermute(value, 'far', [(i, i ^ shift) for i in range(n_far)])]
    all_gather x1, waiting for transfers between devices: 0.01 us -> 2.42 us  [shards(): ff_all = lax.all_gather(ff_low, ('near', 'keys'), axis=0, tiled=True)]
    ppermute x15 -> x17, starting transfers between devices: 12.1 us -> 14.4 us  [over_keys(): return lax.ppermute(value, 'keys', [(i, i ^ shift) for i in range(n_keys)])]
    ppermute x3 -> x6, waiting for transfers between devices: 5.41 us -> 3.43 us  [over_far(): return lax.ppermute(value, 'far', [(i, i ^ shift) for i in range(n_far)])]
    ppermute x15 -> x17, waiting for transfers between devices: 20.3 us -> 21.8 us  [over_keys(): return lax.ppermute(value, 'keys', [(i, i ^ shift) for i in range(n_keys)])]
  transfers between devices with their start and end apart: 30 -> 31, of which waited for: 10 -> 11; matrix products, arithmetic and copies ran while one was open for 4% -> 2% of each run, Pallas kernels for 61% -> 52%
where the time goes in v3:
time: 201 us
  Pallas kernels  116 us (58%)
  waiting for transfers between devices  34.3 us (17%)
  starting transfers between devices  28.5 us (14%)
  between operations  14.1 us (7%)
  local copies, waits for them, and re-layouts  6.45 us (3%)
    pallas_call x12, Pallas kernels, pinned(): return run(*args)  116 us
    ppermute x17, waiting for transfers between devices, over_keys(): return lax.ppermute(value, 'keys', [(i, i ^ shift) for i in range(n_keys)])  21.8 us
    ppermute x17, starting transfers between devices, over_keys(): return lax.ppermute(value, 'keys', [(i, i ^ shift) for i in range(n_keys)])  14.4 us
    ppermute x6, starting transfers between devices, over_far(): return lax.ppermute(value, 'far', [(i, i ^ shift) for i in range(n_far)])  8.22 us
    ppermute x4, waiting for transfers between devices, over_near(): return lax.ppermute(value, 'near', [(0, 1), (1, 0)])  6.54 us
    ppermute x4, starting transfers between devices, over_near(): return lax.ppermute(value, 'near', [(0, 1), (1, 0)])  4.91 us
  transfers between devices with their start and end apart: 31, of which 11 were waited for; matrix products, arithmetic and copies ran while one was open for 2% of the time, Pallas kernels for 52%

profile of v3, /device:TPU:0, one launch (start us, length us, event | category | flops | bytes accessed | tf_op | source)
XLA Modules:
  0.0 200.8 jit_solution(16976963345294316490)
XLA Ops:
  7.8 3.3 %latent_project.1 = (bf16[96,2048]{1,0:T(8,128)(2,1)}, bf16[96,512]{1,0:T(8,128)(2,1)}) custom-call(s32[7]{0:T(128)} %stack.24._.scalars, f32[96,1024]{1,0:T(8,128)} %bitcast.32, f32[1,1024]{1,0:T(1,128)} %bitcast.48, f32[1,1024]{1,0:T(1,128)} %bitcast.52, f32[96,1024]{1,0:T(8,128)} %bitcast.35, bf16[1024,512]{1,0:T(8,128)(2,1)} %refs_8_.1), custom_call_target="tpu_custom_call" | custom-call | flops 100663296 | bytes 2424832 | tf_op jit(solution)/shard_map/latent_project/pallas_call | solution.py:679
  11.2 2.5 %collective-permute-start.2 = (bf16[96,512]{1,0:T(8,128)(2,1)}, bf16[96,512]{1,0:T(8,128)(2,1)S(1)}, u32[]{:S(2)}, u32[]{:S(2)}) collective-permute-start(bf16[96,512]{1,0:T(8,128)(2,1)} %get-tuple-element.123.refs_0_), channel_id=1, source_target_pairs={{0,3},{1,2},{2,1},{3,0},{4,7},{5,6},{6,5},{7,4},{8,11},{9,10},{10,... | collective-permute-start | bytes 294920 | tf_op jit(solution)/shard_map/ppermute | solution.py:624
  14.4 2.8 %collective-permute-done.2.refs_3_ = bf16[96,512]{1,0:T(8,128)(2,1)S(1)} collective-permute-done((bf16[96,512]{1,0:T(8,128)(2,1)}, bf16[96,512]{1,0:T(8,128)(2,1)S(1)}, u32[]{:S(2)}, u32[]{:S(2)}) %collective-permute-start.2) | collective-permute-done | bytes 98336 | tf_op jit(solution)/shard_map/ppermute | solution.py:624
  20.0 19.7 %project_attend.1 = (bf16[6,512,1024]{2,1,0:T(8,128)(2,1)}, bf16[6,512,512]{2,1,0:T(8,128)(2,1)}, bf16[6,512,512]{2,1,0:T(8,128)(2,1)}, bf16[96,512]{1,0:T(8,128...) custom-call(s32[7]{0:T(128)} %stack.24._.scalars, ...), custom_call_target="tpu_custom_call" | custom-call | flops 8103395328 | bytes 37748736 | tf_op jit(solution)/shard_map/project_attend/pallas_call | solution.py:679
  39.8 2.3 %collective-permute-start.4 = (bf16[96,640]{1,0:T(8,128)(2,1)}, bf16[96,640]{1,0:T(8,128)(2,1)S(1)}, u32[]{:S(2)}, u32[]{:S(2)}) collective-permute-start(bf16[96,640]{1,0:T(8,128)(2,1)} %get-tuple-element.126), channel_id=1, source_target_pairs={{0,2},{1,3},{2,0},{3,1},{4,6},{5,7},{6,4},{7,5},{8,10},{9,11},{10,... | collective-permute-start | bytes 368648 | tf_op jit(solution)/shard_map/ppermute | solution.py:624
  42.2 5.2 %collective-permute-done.4.refs_2_ = bf16[96,640]{1,0:T(8,128)(2,1)S(1)} collective-permute-done((bf16[96,640]{1,0:T(8,128)(2,1)}, bf16[96,640]{1,0:T(8,128)(2,1)S(1)}, u32[]{:S(2)}, u32[]{:S(2)}) %collective-permute-start.4) | collective-permute-done | bytes 122912 | tf_op jit(solution)/shard_map/ppermute | solution.py:624
  47.4 2.4 %collective-permute-done.5.refs_3_ = bf16[96,640]{1,0:T(8,128)(2,1)S(1)} collective-permute-done((bf16[96,640]{1,0:T(8,128)(2,1)}, bf16[96,640]{1,0:T(8,128)(2,1)S(1)}, u32[]{:S(2)}, u32[]{:S(2)}) %collective-permute-start.5) | collective-permute-done | bytes 122912 | tf_op jit(solution)/shard_map/ppermute | solution.py:624
  50.5 4.2 %join.1 = (f32[96,512]{1,0:T(8,128)}, bf16[96,512]{1,0:T(8,128)(2,1)}, f32[96,1024]{1,0:T(8,128)}, bf16[96,1024]{1,0:T(8,128)(2,1)}, f32[96,128]{1,0:T(8,128)}) custom-call(s32[7]{0:T(128)} %stack.24._.scalars, f32[96,1024]{1,0:T(8,128)} %bitcast.33, f32[1,1024]{1,0:T(1,128)} %bitcast.50, f32[1,1024]{1,0:T(1,128)} %bitcast.53, bf16[512,1024]{1,0:T(8,128)(2,1)} %wo.3, ...), custom_call_target="tpu_custom_call" | custom-call | flops 100663296 | bytes 2621440 | tf_op jit(solution)/shard_map/join/pallas_call | solution.py:679
  54.9 15.4 %feed_forward.1 = (f32[96,1024]{1,0:T(8,128)}, f32[96,1024]{1,0:T(8,128)}, bf16[96,640]{1,0:T(8,128)(2,1)}, f32[2,1024]{1,0:T(2,128)}, bf16[4,128,1024]{2,1,0:T(8,128)(2,1)}) custom-call(s32[7]{0:T(128)} %stack.24._.scalars, f32[96,512]{1,0:T(8,128)} %get-tuple-element.128.attended, bf16[96,512]{1,0:T(8,128)(2,1)} %get-tuple-element.129.att_low, ...), custom_call_target="tpu_custom_call" | custom-call | flops 3221225472 | bytes 19136512 | tf_op jit(solution)/shard_map/feed_forward/pallas_call | solution.py:679
  70.7 7.2 %collective-permute-done.7.refs_6_.refs_10_ = bf16[96,640]{1,0:T(8,128)(2,1)S(1)} collective-permute-done((bf16[96,640]{1,0:T(8,128)(2,1)}, bf16[96,640]{1,0:T(8,128)(2,1)S(1)}, u32[]{:S(2)}, u32[]{:S(2)}) %collective-permute-start.7) | collective-permute-done | bytes 122912 | tf_op jit(solution)/shard_map/ppermute | solution.py:624
  79.3 2.4 %all-gather.5.cloned.1.call-done.ff_all = bf16[768,1024]{1,0:T(8,128)(2,1)} async-done(((bf16[96,1024]{1,0:T(8,128)(2,1)}), bf16[768,1024]{1,0:T(8,128)(2,1)}) %all-gather.5.cloned.1.call-update) | async-done | bytes 1572880 | tf_op jit(solution)/shard_map/all_gather | solution.py:772
  81.7 8.3 %feed_forward_weights.1 = bf16[1024,1024]{1,0:T(8,128)(2,1)} custom-call(s32[7]{0:T(128)} %stack.24._.scalars, bf16[768,1024]{1,0:T(8,128)(2,1)} %all-gather.5.cloned.1.call-done.ff_all, bf16[768,2048]{1,0:T(8,128)(2,1)} %all-gather.3.cloned.1.call-done.out_all.refs_24_, bf16[1024,4096]{1,0:T(8,128)(2,1)} %up.3, bf16[4096,1024]{1,0:T(8,128)(2,1)} %down.3), custom_call_target="tpu_custom_call" | custom-call | flops 3221225472 | bytes 7340032 | tf_op jit(solution)/shard_map/feed_forward_weights/pallas_call | solution.py:679
  90.0 17.3 %attend_back.2 = (bf16[2,256,3072]{2,1,0:T(8,128)(2,1)}, f32[8,3072]{1,0:T(8,128)}, bf16[96,256]{1,0:T(8,128)(2,1)}, bf16[96,256]{1,0:T(8,128)(2,1)}, bf16[1,2,5...) custom-call(s32[7]{0:T(128)} %stack.24._.scalars, ...), custom_call_target="tpu_custom_call" | custom-call | flops 5297405952 | bytes 18874368 | tf_op jit(solution)/shard_map/attend_back/pallas_call | solution.py:679
  107.6 17.8 %attend_back.3 = (bf16[2,256,3072]{2,1,0:T(8,128)(2,1)}, f32[8,3072]{1,0:T(8,128)}, bf16[96,256]{1,0:T(8,128)(2,1)}, bf16[96,256]{1,0:T(8,128)(2,1)}, bf16[1,2,5...) custom-call(s32[7]{0:T(128)} %stack.24._.scalars, ...), custom_call_target="tpu_custom_call" | custom-call | flops 5297405952 | bytes 18874368 | tf_op jit(solution)/shard_map/attend_back/pallas_call | solution.py:679
  130.1 7.3 %patch_back.3._ = bf16[6,512,1024]{2,1,0:T(8,128)(2,1)} custom-call(s32[7]{0:T(128)} %stack.24._.scalars, bf16[2,256,3072]{2,1,0:T(8,128)(2,1)} %get-tuple-element.152.kv_a, bf16[2,256,3072]{2,1,0:T(8,128)(2,1)} %get-tuple-element.158.kv_b, f32[8,3072]{1,0:T(8,128)} %get-tuple-element.159.stat_a, f32[8,3072]{1,0:T(8,128)} %get-tuple-element.160.stat_b, ...), custom_call_target="tpu_custom_call" | custom-call | flops 2147483648 | bytes 8388608 | tf_op jit(solution)/shard_map/patch_back/pallas_call | solution.py:679
  137.4 3.7 %collective-permute-done.10 = bf16[1,512,512]{2,1,0:T(8,128)(2,1)S(1)} collective-permute-done((bf16[1,512,512]{2,1,0:T(8,128)(2,1)}, bf16[1,512,512]{2,1,0:T(8,128)(2,1)S(1)}, u32[]{:S(2)}, u32[]{:S(2)}) %collective-permute-start.10) | collective-permute-done | bytes 524320 | tf_op jit(solution)/shard_map/ppermute | solution.py:627
  145.6 5.1 %latent_back.1 = (f32[96,1024]{1,0:T(8,128)}, f32[16,1024]{1,0:T(8,128)}) custom-call(s32[7]{0:T(128)} %stack.24._.scalars, f32[96,1024]{1,0:T(8,128)} %bitcast.34, f32[1,1024]{1,0:T(1,128)} %bitcast.49, f32[96,1024]{1,0:T(8,128)} %get-tuple-element.187.mid_grad, f32[8,1024]{1,0:T(8,128)} %get-tuple-element.188.media_small, ...), custom_call_target="tpu_custom_call" | custom-call | flops 301989888 | bytes 5111808 | tf_op jit(solution)/shard_map/latent_back/pallas_call | solution.py:679
  152.6 7.1 %patch_back.4._ = bf16[6,512,1024]{2,1,0:T(8,128)(2,1)} custom-call(s32[7]{0:T(128)} %stack.24._.scalars, bf16[2,256,3072]{2,1,0:T(8,128)(2,1)} %get-tuple-element.152.kv_a, bf16[2,256,3072]{2,1,0:T(8,128)(2,1)} %get-tuple-element.158.kv_b, f32[8,3072]{1,0:T(8,128)} %get-tuple-element.159.stat_a, ...), custom_call_target="tpu_custom_call", output_to_operand_aliasing={{}: (13, {})} | custom-call | flops 2147483648 | bytes 8388608 | tf_op jit(solution)/shard_map/patch_back/pallas_call | solution.py:679
  160.0 5.3 %collective-permute-start.18 = (f32[16,1024]{1,0:T(8,128)S(1)}, f32[16,1024]{1,0:T(8,128)S(1)}, u32[]{:S(2)}, u32[]{:S(2)}) collective-permute-start(f32[16,1024]{1,0:T(8,128)S(1)} %add.45), channel_id=1, source_target_pairs={{0,2},{1,3},{2,0},{3,1},{4,6},{5,7},{6,4},{7,5},{8,10},{9,11},{10,... | collective-permute-start | bytes 196616 | tf_op jit(solution)/shard_map/ppermute | solution.py:624
  170.4 7.1 %patch_back.5 = bf16[6,512,1024]{2,1,0:T(8,128)(2,1)} custom-call(s32[7]{0:T(128)} %stack.24._.scalars, bf16[2,256,3072]{2,1,0:T(8,128)(2,1)} %get-tuple-element.152.kv_a, bf16[2,256,3072]{2,1,0:T(8,128)(2,1)} %get-tuple-element.158.kv_b, f32[8,3072]{1,0:T(8,128)} %get-tuple-element.159.stat_a, ...), custom_call_target="tpu_custom_call", output_to_operand_aliasing={{}: (13, {})} | custom-call | flops 2147483648 | bytes 8388608 | tf_op jit(solution)/shard_map/patch_back/pallas_call | solution.py:679
  177.6 3.4 %collective-permute-done.22.refs_2_ = bf16[512,128]{1,0:T(8,128)(2,1)S(1)} collective-permute-done((bf16[512,128]{1,0:T(8,128)(2,1)S(1)}, bf16[512,128]{1,0:T(8,128)(2,1)S(1)}, u32[]{:S(2)}, u32[]{:S(2)}) %collective-permute-start.22) | collective-permute-done | bytes 131104 | tf_op jit(solution)/shard_map/ppermute | solution.py:630
  182.5 2.8 %collective-permute-done.24 = f32[16,1024]{1,0:T(8,128)S(1)} collective-permute-done((f32[16,1024]{1,0:T(8,128)S(1)}, f32[16,1024]{1,0:T(8,128)S(1)}, u32[]{:S(2)}, u32[]{:S(2)}) %collective-permute-start.24) | collective-permute-done | bytes 65568 | tf_op jit(solution)/shard_map/ppermute | solution.py:627
  185.7 4.1 %collective-permute-start.25 = (f32[16,1024]{1,0:T(8,128)S(1)}, f32[16,1024]{1,0:T(8,128)S(1)}, u32[]{:S(2)}, u32[]{:S(2)}) collective-permute-start(f32[16,1024]{1,0:T(8,128)S(1)} %add.47), channel_id=1, source_target_pairs={{0,8},{8,0},{16,24},{24,16},{1,9},{9,1},{17,25},{25,17},{2,10},{10... | collective-permute-start | bytes 196616 | tf_op jit(solution)/shard_map/ppermute | solution.py:630
  189.8 3.1 %finish_weights.1 = (f32[128,128]{1,0:T(8,128)}, f32[128,128]{1,0:T(8,128)}, f32[128,128]{1,0:T(8,128)}, f32[64,256]{1,0:T(8,128)}, f32[128,1024]{1,0:T(8,128)}, /*index=5*/f32[512,256]{1,0:T(8,128)}) custom-call(s32[7]{0:T(128)} %stack.24._.scalars, bf16[512,128]{1,0:T(8,128)(2,1)} %get-tuple-element.232.up_keep, bf16[512,128]{1,0:T(8,128)(2,1)} %copy-done.10, ...), custom_call_target="tpu_custom_call" | custom-call | bytes 1048576 | tf_op jit(solution)/shard_map/finish_weights/pallas_call | solution.py:679
  (113 shorter events, 26.7 us)
Async XLA Ops:
  7.2 47.4 %all-gather.3.cloned.1.call-start = ((), (), s32[]{:S(2)}) async-start(), calls=%async_computation.1 | async-start | bytes 3538944 | tf_op jit(solution)/shard_map/all_gather | solution.py:693
  11.2 70.5 %all-gather.5.cloned.1.call-start = ((), (), s32[]{:S(2)}) async-start(), calls=%async_computation.2 | async-start | bytes 1769472 | tf_op jit(solution)/shard_map/all_gather | solution.py:772
  39.8 7.6 %collective-permute-start.4 = (bf16[96,640]{1,0:T(8,128)(2,1)}, bf16[96,640]{1,0:T(8,128)(2,1)S(1)}, u32[]{:S(2)}, u32[]{:S(2)}) collective-permute-start(bf16[96,640]{1,0:T(8,128)(2,1)} %get-tuple-element.126), channel_id=1, source_target_pairs={{0,2},{1,3},{2,0},{3,1},{4,6},{5,7},{6,4},{7,5},{8,10},{9,11},{10,... | collective-permute-start | bytes 368648 | tf_op jit(solution)/shard_map/ppermute | solution.py:624
  42.1 7.7 %collective-permute-start.5 = (bf16[96,640]{1,0:T(8,128)(2,1)}, bf16[96,640]{1,0:T(8,128)(2,1)S(1)}, u32[]{:S(2)}, u32[]{:S(2)}) collective-permute-start(bf16[96,640]{1,0:T(8,128)(2,1)} %get-tuple-element.127), channel_id=1, source_target_pairs={{0,3},{1,2},{2,1},{3,0},{4,7},{5,6},{6,5},{7,4},{8,11},{9,10},{10,... | collective-permute-start | bytes 368648 | tf_op jit(solution)/shard_map/ppermute | solution.py:624
  54.6 87.8 %reduce-scatter.2.cloned.1.call-start = ((), (), s32[]{:S(2)}) async-start(), calls=%async_computation.3 | async-start | bytes 2621440 | tf_op jit(solution)/shard_map/reduce_scatter | solution.py:964
  70.3 7.6 %collective-permute-start.7 = (bf16[96,640]{1,0:T(8,128)(2,1)}, bf16[96,640]{1,0:T(8,128)(2,1)S(1)}, u32[]{:S(2)}, u32[]{:S(2)}) collective-permute-start(bf16[96,640]{1,0:T(8,128)(2,1)} %get-tuple-element.139.refs_4_.refs_8_), channel_id=1, source_target_pairs={{0,2},{1,3},{2,0},{3,1},{4,6},{5,7},{6,4},{7,5},{8,10},{9,11},{10,... | collective-permute-start | bytes 368648 | tf_op jit(solution)/shard_map/ppermute | solution.py:624
  107.3 18.1 %collective-permute-start.9 = (bf16[1,2,512,512]{3,2,1,0:T(8,128)(2,1)}, bf16[1,2,512,512]{3,2,1,0:T(8,128)(2,1)S(1)}, u32[]{:S(2)}, u32[]{:S(2)}) collective-permute-start(bf16[1,2,512,512]{3,2,1,0:T(8,128)(2,1)} %get-tuple-element.163), channel_id=1, source_target_pairs={{0,1},{1,0},{2,3},{3,2},{4,5},{5,4},{6,7},{7,6},{8,9},{9,8},{10,11... | collective-permute-start | bytes 3145736 | tf_op jit(solution)/shard_map/ppermute | solution.py:624
  125.7 15.4 %collective-permute-start.11 = (bf16[1,2,512,512]{3,2,1,0:T(8,128)(2,1)}, bf16[1,2,512,512]{3,2,1,0:T(8,128)(2,1)S(1)}, u32[]{:S(2)}, u32[]{:S(2)}) collective-permute-start(bf16[1,2,512,512]{3,2,1,0:T(8,128)(2,1)} %get-tuple-element.177), channel_id=1, source_target_pairs={{0,1},{1,0},{2,3},{3,2},{4,5},{5,4},{6,7},{7,6},{8,9},{9,8},{10,11... | collective-permute-start | bytes 3145736 | tf_op jit(solution)/shard_map/ppermute | solution.py:624
  126.8 14.3 %collective-permute-start.10 = (bf16[1,512,512]{2,1,0:T(8,128)(2,1)}, bf16[1,512,512]{2,1,0:T(8,128)(2,1)S(1)}, u32[]{:S(2)}, u32[]{:S(2)}) collective-permute-start(bf16[1,512,512]{2,1,0:T(8,128)(2,1)} %slice_bitcast_fusion.1), channel_id=1, source_target_pairs={{0,4},{4,0},{1,5},{5,1},{2,6},{6,2},{3,7},{7,3},{8,12},{12,8},{9,1... | collective-permute-start | bytes 1572872 | tf_op jit(solution)/shard_map/ppermute | solution.py:627
  128.2 9.1 %collective-permute-start.12 = (bf16[96,512]{1,0:T(8,128)(2,1)}, bf16[96,512]{1,0:T(8,128)(2,1)S(1)}, u32[]{:S(2)}, u32[]{:S(2)}) collective-permute-start(bf16[96,512]{1,0:T(8,128)(2,1)} %get-tuple-element.179), channel_id=1, source_target_pairs={{0,1},{1,0},{2,3},{3,2},{4,5},{5,4},{6,7},{7,6},{8,9},{9,8},{10,11... | collective-permute-start | bytes 294920 | tf_op jit(solution)/shard_map/ppermute | solution.py:624
  128.2 9.1 %collective-permute-start.13 = (bf16[96,512]{1,0:T(8,128)(2,1)}, bf16[96,512]{1,0:T(8,128)(2,1)S(1)}, u32[]{:S(2)}, u32[]{:S(2)}) collective-permute-start(bf16[96,512]{1,0:T(8,128)(2,1)} %get-tuple-element.180), channel_id=1, source_target_pairs={{0,2},{1,3},{2,0},{3,1},{4,6},{5,7},{6,4},{7,5},{8,10},{9,11},{10,... | collective-permute-start | bytes 294920 | tf_op jit(solution)/shard_map/ppermute | solution.py:624
  128.9 8.5 %collective-permute-start.14 = (bf16[96,512]{1,0:T(8,128)(2,1)S(1)}, bf16[96,512]{1,0:T(8,128)(2,1)S(1)}, u32[]{:S(2)}, u32[]{:S(2)}) collective-permute-start(bf16[96,512]{1,0:T(8,128)(2,1)S(1)} %copy-done.21), channel_id=1, source_target_pairs={{0,3},{1,2},{2,1},{3,0},{4,7},{5,6},{6,5},{7,4},{8,11},{9,10},{10,... | collective-permute-start | bytes 294920 | tf_op jit(solution)/shard_map/ppermute | solution.py:624
  142.4 17.3 %collective-permute-start.16 = (bf16[512,512]{1,0:T(8,128)(2,1)S(1)}, bf16[512,512]{1,0:T(8,128)(2,1)S(1)}, u32[]{:S(2)}, u32[]{:S(2)}) collective-permute-start(bf16[512,512]{1,0:T(8,128)(2,1)S(1)} %slice_bitcast_fusion), channel_id=1, source_target_pairs={{0,4},{4,0},{1,5},{5,1},{2,6},{6,2},{3,7},{7,3},{8,12},{12,8},{9,1... | collective-permute-start | bytes 1572872 | tf_op jit(solution)/shard_map/ppermute | solution.py:627
  143.9 15.8 %collective-permute-start.17 = (bf16[512,512]{1,0:T(8,128)(2,1)}, bf16[512,512]{1,0:T(8,128)(2,1)S(1)}, u32[]{:S(2)}, u32[]{:S(2)}) collective-permute-start(bf16[512,512]{1,0:T(8,128)(2,1)} %bitcast.37), channel_id=1, source_target_pairs={{0,2},{1,3},{2,0},{3,1},{4,6},{5,7},{6,4},{7,5},{8,10},{9,11},{10,... | collective-permute-start | bytes 1572872 | tf_op jit(solution)/shard_map/ppermute | solution.py:624
  150.7 9.0 %collective-permute-start.15 = (f32[16,1024]{1,0:T(8,128)}, f32[16,1024]{1,0:T(8,128)S(1)}, u32[]{:S(2)}, u32[]{:S(2)}) collective-permute-start(f32[16,1024]{1,0:T(8,128)} %get-tuple-element.202), channel_id=1, source_target_pairs={{0,1},{1,0},{2,3},{3,2},{4,5},{5,4},{6,7},{7,6},{8,9},{9,8},{10,11... | collective-permute-start | bytes 196616 | tf_op jit(solution)/shard_map/ppermute | solution.py:624
  151.4 26.2 %collective-permute-start.19 = (bf16[512,128]{1,0:T(8,128)(2,1)S(1)}, bf16[512,128]{1,0:T(8,128)(2,1)S(1)}, u32[]{:S(2)}, u32[]{:S(2)}) collective-permute-start(bf16[512,128]{1,0:T(8,128)(2,1)S(1)} %get-tuple-element.233), channel_id=1, source_target_pairs={{0,4},{4,0},{1,5},{5,1},{2,6},{6,2},{3,7},{7,3},{8,12},{12,8},{9,1... | collective-permute-start | bytes 393224 | tf_op jit(solution)/shard_map/ppermute | solution.py:627
  151.9 25.6 %collective-permute-start.20 = (bf16[512,256]{1,0:T(8,128)(2,1)S(1)}, bf16[512,256]{1,0:T(8,128)(2,1)S(1)}, u32[]{:S(2)}, u32[]{:S(2)}) collective-permute-start(bf16[512,256]{1,0:T(8,128)(2,1)S(1)} %slice.61), channel_id=1, source_target_pairs={{0,0},{1,8},{2,16},{3,24},{4,4},{5,12},{6,20},{7,28},{8,1},{9,9},{... | collective-permute-start | bytes 786440 | tf_op jit(solution)/shard_map/ppermute | solution.py:1049
  160.0 8.5 %collective-permute-start.18 = (f32[16,1024]{1,0:T(8,128)S(1)}, f32[16,1024]{1,0:T(8,128)S(1)}, u32[]{:S(2)}, u32[]{:S(2)}) collective-permute-start(f32[16,1024]{1,0:T(8,128)S(1)} %add.45), channel_id=1, source_target_pairs={{0,2},{1,3},{2,0},{3,1},{4,6},{5,7},{6,4},{7,5},{8,10},{9,11},{10,... | collective-permute-start | bytes 196616 | tf_op jit(solution)/shard_map/ppermute | solution.py:624
  166.0 11.6 %collective-permute-start.23 = (bf16[512,128]{1,0:T(8,128)(2,1)S(1)}, bf16[512,128]{1,0:T(8,128)(2,1)S(1)}, u32[]{:S(2)}, u32[]{:S(2)}) collective-permute-start(bf16[512,128]{1,0:T(8,128)(2,1)S(1)} %get-tuple-element.229), channel_id=1, source_target_pairs={{0,24},{8,16},{16,8},{24,0},{1,25},{9,17},{17,9},{25,1},{2,26},{10... | collective-permute-start | bytes 393224 | tf_op jit(solution)/shard_map/ppermute | solution.py:630
  167.1 13.9 %collective-permute-start.22 = (bf16[512,128]{1,0:T(8,128)(2,1)S(1)}, bf16[512,128]{1,0:T(8,128)(2,1)S(1)}, u32[]{:S(2)}, u32[]{:S(2)}) collective-permute-start(bf16[512,128]{1,0:T(8,128)(2,1)S(1)} %get-tuple-element.230), channel_id=1, source_target_pairs={{0,16},{8,24},{16,0},{24,8},{1,17},{9,25},{17,1},{25,9},{2,18},{10... | collective-permute-start | bytes 393224 | tf_op jit(solution)/shard_map/ppermute | solution.py:630
  168.5 12.5 %collective-permute-start.21 = (bf16[512,128]{1,0:T(8,128)(2,1)S(1)}, bf16[512,128]{1,0:T(8,128)(2,1)S(1)}, u32[]{:S(2)}, u32[]{:S(2)}) collective-permute-start(bf16[512,128]{1,0:T(8,128)(2,1)S(1)} %get-tuple-element.231), channel_id=1, source_target_pairs={{0,8},{8,0},{16,24},{24,16},{1,9},{9,1},{17,25},{25,17},{2,10},{10... | collective-permute-start | bytes 393224 | tf_op jit(solution)/shard_map/ppermute | solution.py:630
  185.3 7.6 %collective-permute-start.27 = (f32[16,1024]{1,0:T(8,128)S(1)}, f32[16,1024]{1,0:T(8,128)S(1)}, u32[]{:S(2)}, u32[]{:S(2)}) collective-permute-start(f32[16,1024]{1,0:T(8,128)S(1)} %add.47), channel_id=1, source_target_pairs={{0,24},{8,16},{16,8},{24,0},{1,25},{9,17},{17,9},{25,1},{2,26},{10... | collective-permute-start | bytes 196616 | tf_op jit(solution)/shard_map/ppermute | solution.py:630
  185.7 7.3 %collective-permute-start.26 = (f32[16,1024]{1,0:T(8,128)S(1)}, f32[16,1024]{1,0:T(8,128)S(1)}, u32[]{:S(2)}, u32[]{:S(2)}) collective-permute-start(f32[16,1024]{1,0:T(8,128)S(1)} %add.47), channel_id=1, source_target_pairs={{0,16},{8,24},{16,0},{24,8},{1,17},{9,25},{17,1},{25,9},{2,18},{10... | collective-permute-start | bytes 196616 | tf_op jit(solution)/shard_map/ppermute | solution.py:630
  185.7 7.3 %collective-permute-start.25 = (f32[16,1024]{1,0:T(8,128)S(1)}, f32[16,1024]{1,0:T(8,128)S(1)}, u32[]{:S(2)}, u32[]{:S(2)}) collective-permute-start(f32[16,1024]{1,0:T(8,128)S(1)} %add.47), channel_id=1, source_target_pairs={{0,8},{8,0},{16,24},{24,16},{1,9},{9,1},{17,25},{25,17},{2,10},{10... | collective-permute-start | bytes 196616 | tf_op jit(solution)/shard_map/ppermute | solution.py:630
  (29 other events, 206.6 us)
Sparse Core Ops, SparseCore 0:
  11.3 36.2 all-gather.2
  54.8 26.8 all-gather.4
  90.1 44.0 reduce-scatter.1

commit v4 on v3

--- a/solution.py
+++ b/solution.py
@@ -109,7 +109,7 @@
     return lax.optimization_barrier(values)
 
 
-def latent_kernel(_, lat, gain, bias, cot, wq, rows_o, q_o):
+def latent_kernel(lat, gain, bias, cot, wq, rows_o, q_o):
     dim = lat.shape[1]
     low = norm(lat[...], gain[...], bias[...]).astype(bf16)
     rows_o[:, :dim] = low
@@ -205,9 +205,7 @@
     return total
 
 
-def join_kernel(n_keys, _, latents, gain, bias, wo, *refs):
-    slots = refs[:n_keys]
-    att_o, low_o, mid_o, ff_o, lse_o = refs[n_keys:]
+def join(latents, gain, bias, wo, slots, att_o, low_o, mid_o, ff_o, lse_o):
     inner = att_o.shape[1]
     heads = inner // HEAD
     levels = [sum_runs(r[:, inner:].astype(f32), heads, 0) for r in slots]
@@ -219,7 +217,7 @@
     col = lax.broadcasted_iota(jnp.int32, (LANES, inner), 1)
     select = jnp.where(lane == col // HEAD, 1.0, 0.0)
     attended = None
-    for s in range(n_keys):
+    for s in range(len(slots)):
         wide = mul(weights[s] * inverse, select, NN, lax.Precision.HIGHEST)
         term = wide * slots[s][:, :inner].astype(f32)
         attended = term if attended is None else attended + term
@@ -236,32 +234,26 @@
     n_keys,
     aligned,
     scalars,
-    attended,
-    att_low,
-    middle,
-    ff_low,
-    lse,
+    latents,
     cot,
     out_low,
     gain,
+    bias,
     wo,
     up,
     down,
-    res_o,
-    mid_grad_o,
-    pack_o,
-    small_o,
-    wo_grad_o,
-    res_acc,
-    in_acc,
-    wo_acc,
+    *refs,
 ):
+    slots = refs[:n_keys]
+    res_o, mid_grad_o, pack_o, small_o, wo_grad_o, ff_low = refs[n_keys : n_keys + 6]
+    res_acc, in_acc, wo_acc, attended, att_low, middle, lse = refs[n_keys + 6 :]
     step = pl.program_id(0)
 
     @pl.when(step == 0)
     def _():
         res_acc[...] = jnp.zeros_like(res_acc)
         in_acc[...] = jnp.zeros_like(in_acc)
+        join(latents, gain, bias, wo, slots, attended, att_low, middle, ff_low, lse)
 
     hidden = mul(ff_low[...], up[...])
     act_grad = mul(out_low[...], down[...], NT)
@@ -314,21 +306,38 @@
                 ].astype(bf16)
 
 
-def ff_grad_kernel(aligned, scalars, ff_all, out_all, up, down, grad_o):
+def ff_grad_kernel(n_keys, aligned, scalars, ff_all, out_all, up, down, *refs):
+    own_ups, grad_o = refs[:-1], refs[-1]
     units, dim = down.shape
+    step = pl.program_id(0)
     hidden = mul(ff_all[...], up[...])
     act_grad = mul(out_all[...], down[...], NT)
-    cdf, slope = gelu_parts(hidden)
-    grad_o[units:, :] = mul((hidden * cdf).astype(bf16), out_all[...], TN).astype(bf16)
+    _, slope = gelu_parts(hidden)
     up_grad = mul((act_grad * slope).astype(bf16), ff_all[...], TN).astype(bf16)
-    if aligned:
-        for j in range(dim // LANES):
-            place = ((j // PAIR) * PAIR + (scalars[1] ^ (j % PAIR))) * LANES
-            grad_o[:units, pl.ds(pl.multiple_of(place, LANES), LANES)] = up_grad[
-                :, j * LANES : (j + 1) * LANES
+    rows = pl.ds(pl.multiple_of(step * units, 8), units)
+    if not aligned:
+        grad_o[0] = up_grad
+        hidden = mul(ff_all[...], own_ups[0][...])
+        cdf, _ = gelu_parts(hidden)
+        grad_o[1] = mul((hidden * cdf).astype(bf16), out_all[...], TN).astype(bf16)
+        return
+    for j in range(dim // LANES):
+        place = ((j // PAIR) * PAIR + (scalars[1] ^ (j % PAIR))) * LANES
+        grad_o[0, rows, pl.ds(pl.multiple_of(place, LANES), LANES)] = up_grad[
+            :, j * LANES : (j + 1) * LANES
+        ]
+    each = own_ups[0].shape[1]
+    cols = dim // n_keys
+    hidden = mul(ff_all[...], jnp.concatenate([r[...] for r in own_ups], 1))
+    cdf, _ = gelu_parts(hidden)
+    down_grad = mul((hidden * cdf).astype(bf16), out_all[...], TN).astype(bf16)
+    for n in range(len(own_ups)):
+        lanes = pl.ds(pl.multiple_of((step * len(own_ups) + n) * cols, LANES), cols)
+        for k in range(n_keys):
+            place = pl.ds(pl.multiple_of((scalars[0] ^ k) * each, each), each)
+            grad_o[1, place, lanes] = down_grad[
+                n * each : (n + 1) * each, k * cols : (k + 1) * cols
             ]
-    else:
-        grad_o[:units, :] = up_grad
 
 
 def attend_back_kernel(n_keys, frames, turn, heads, width, aligned, scalars, counts, *refs):
@@ -496,7 +505,7 @@
     half = piece.shape[1] // PAIR
     if aligned:
         for m in range(piece.shape[1] // LANES):
-            place = pl.ds(pl.multiple_of((scalars[2] ^ (m // PAIR)) * LANES, LANES), LANES)
+            place = slice((m // PAIR) * LANES, (m // PAIR + 1) * LANES)
             out[slot, scalars[1] ^ (m % PAIR), rows, place] = piece[:, m * LANES : (m + 1) * LANES]
     else:
         for n in range(PAIR):
@@ -548,10 +557,13 @@
     small_o[n_frames + 4 : n_frames + 6, :] = ff_small[...]
 
 
-def finish_kernel(width, scalars, up_keep, up_got, down, *refs):
-    parts = refs[:-6]
+def finish_kernel(n_keys, width, scalars, up_keep, up_got, *refs):
+    downs, parts = refs[:n_keys], refs[n_keys]
     q_o, k_o, v_o, out_o, up_o, down_o = refs[-6:]
-    total = functools.reduce(jnp.add, [r[...].astype(f32) for r in parts])
+    high = 3 * width + out_o.shape[0] * out_o.shape[1] // LANES
+    total = parts[:high].astype(f32)
+    for s in range(1, parts.shape[0] // high):
+        total = total + parts[s * high : (s + 1) * high].astype(f32)
     for i, ref in enumerate((q_o, k_o, v_o)):
         ref[...] = total[i * width : (i + 1) * width].T
     r = out_o.shape[0]
@@ -563,7 +575,9 @@
     other = pl.ds(pl.multiple_of((1 - near) * units, LANES), units)
     up_o[:, own] = up_keep[...].astype(f32).T
     up_o[:, other] = up_got[...].astype(f32).T
-    down_o[...] = down[...].astype(f32)
+    share = downs[0].shape[0]
+    for s, ref in enumerate(downs):
+        down_o[pl.ds(pl.multiple_of((scalars[0] ^ s) * share, share), share), :] = ref[...].astype(f32)
 
 
 def whole(shape):
@@ -688,7 +702,8 @@
         [whole((rows, 2 * dim)), whole((rows, inner))],
         (struct((rows, 2 * dim), bf16), struct((rows, inner), bf16)),
         cost(2 * rows * dim * inner, 2 * dim * inner + 14 * rows * dim),
-    )(scalars, lat, row(latent_gain), row(latent_bias), cot, query_weight)
+        prefetch=0,
+    )(lat, row(latent_gain), row(latent_bias), cot, query_weight)
     q_all = exchange_keys([q_own] * n_keys)
     rows_all = lax.all_gather(own_rows, ("near", "keys"), axis=0, tiled=True)
 
@@ -746,57 +761,31 @@
     shares = out[8:]
     joined = exchange_keys(shares)
 
-    attended, att_low, middle, ff_low, lse = call(
-        functools.partial(join_kernel, n_keys),
-        "join",
-        (1,),
-        [whole((rows, dim)), whole((1, dim)), whole((1, dim)), whole((inner, dim))]
-        + [whole((rows, packed))] * n_keys,
-        [
-            whole((rows, inner)),
-            whole((rows, inner)),
-            whole((rows, dim)),
-            whole((rows, dim)),
-            whole((rows, LANES)),
-        ],
-        (
-            struct((rows, inner), f32),
-            struct((rows, inner), bf16),
-            struct((rows, dim), f32),
-            struct((rows, dim), bf16),
-            struct((rows, LANES), f32),
-        ),
-        cost(2 * rows * inner * dim, 2 * inner * dim + 16 * rows * dim),
-    )(scalars, lat, row(ff_gain), row(ff_bias), out_weight, *joined)
-    ff_low, rows_all = tie(ff_low, rows_all)
-    ff_all = lax.all_gather(ff_low, ("near", "keys"), axis=0, tiled=True)
-
     chunk = min(1024, hidden)
     wo_rows = inner * dim // n_keys // dim
     wo_shape = (n_keys, wo_rows, dim) if aligned else (inner, dim)
-    resampled, mid_grad, pack, ff_small, out_slots = call(
+    resampled, mid_grad, pack, ff_small, out_slots, ff_low = call(
         functools.partial(forward_kernel, n_keys, aligned),
         "feed_forward",
         (hidden // chunk,),
         [
-            whole((rows, inner)),
-            whole((rows, inner)),
             whole((rows, dim)),
             whole((rows, dim)),
-            whole((rows, LANES)),
-            whole((rows, dim)),
             pl.BlockSpec((rows, dim), lambda i, *_: (0, 1)),
+            whole((1, dim)),
             whole((1, dim)),
             whole((inner, dim)),
             pl.BlockSpec((dim, chunk), lambda i, *_: (0, i)),
             pl.BlockSpec((chunk, dim), lambda i, *_: (i, 0)),
-        ],
+        ]
+        + [whole((rows, packed))] * n_keys,
         [
             whole((rows, dim)),
             whole((rows, dim)),
             whole((rows, packed)),
             whole((2, dim)),
             whole(wo_shape),
+            whole((rows, dim)),
         ],
         (
             struct((rows, dim), f32),
@@ -804,27 +793,32 @@
             struct((rows, packed), bf16),
             struct((2, dim), f32),
             struct(wo_shape, bf16),
+            struct((rows, dim), bf16),
         ),
         cost(8 * rows * dim * hidden, 4 * dim * hidden + 24 * rows * dim),
         scratch_shapes=[
             pltpu.VMEM((rows, dim), f32),
             pltpu.VMEM((rows, dim), f32),
             pltpu.VMEM((inner, dim) if aligned else (8, LANES), f32),
+            pltpu.VMEM((rows, inner), f32),
+            pltpu.VMEM((rows, inner), bf16),
+            pltpu.VMEM((rows, dim), f32),
+            pltpu.VMEM((rows, LANES), f32),
         ],
     )(
         scalars,
-        attended,
-        att_low,
-        middle,
-        ff_low,
-        lse,
+        lat,
         cot,
         own_rows,
         row(ff_gain),
+        row(ff_bias),
         out_weight,
         up_weight,
         down_weight,
+        *joined,
     )
+    ff_low, rows_all = tie(ff_low, rows_all)
+    ff_all = lax.all_gather(ff_low, ("near", "keys"), axis=0, tiled=True)
     if not aligned:
         c = dim // n_keys
         out_slots = out_slots.reshape(n_media, inner // n_media, n_keys, c // each, each)
@@ -935,41 +929,64 @@
         return out[:4], chains, out[6], out[7:]
 
     group_rows = PAIR * n_keys * rows
-    ff_all, *packs = tie(ff_all, *packs)
+    (kv_a, stat_a, kl_a, vl_a), (given_a, kept_a), media_small, q_a = attend_back(0, packs, [], [])
+    far_core = over_keys(given_a, 1)
+    ff_all, kept_a = tie(ff_all, kept_a)
 
     units = hidden // (n_keys * PAIR)
+    share = hidden // (n_media * n_keys)
+    runs, per_run = (2, n_far // 2) if aligned else (1, 1)
+    if aligned:
+        own_up = [
+            pl.BlockSpec(
+                (dim, share),
+                lambda i, s, n=n: (0, ((i * per_run + n) * PAIR + s[1]) * n_keys + s[0]),
+            )
+            for n in range(per_run)
+        ]
+        own_weights = [up_weight] * per_run
+    else:
+        shares = up_weight.reshape(dim, n_far, PAIR, n_keys, share)
+        shares = lax.dynamic_index_in_dim(shares, key, 3, False)
+        own_weights = [lax.dynamic_index_in_dim(shares, near, 2, False).reshape(dim, units)]
+        own_up = [whole((dim, units))]
     ff_partial = call(
-        functools.partial(ff_grad_kernel, aligned),
+        functools.partial(ff_grad_kernel, n_keys, aligned),
         "feed_forward_weights",
-        (1,),
+        (runs,),
         [
             whole((group_rows, dim)),
             pl.BlockSpec((group_rows, dim), lambda i, s: (0, 1)),
-            pl.BlockSpec((dim, units), lambda i, s: (0, s[4])),
-            pl.BlockSpec((units, dim), lambda i, s: (s[4], 0)),
-        ],
-        whole((2 * units, dim)),
-        struct((2 * units, dim), bf16),
-        cost(8 * group_rows * dim * units, 8 * dim * units + 4 * group_rows * dim),
-    )(scalars, ff_all, rows_all, up_weight, down_weight)
+            pl.BlockSpec((dim, units // runs), lambda i, s: (0, s[4] * runs + i)),
+            pl.BlockSpec((units // runs, dim), lambda i, s: (s[4] * runs + i, 0)),
+        ]
+        + own_up,
+        whole((2, units, dim)),
+        struct((2, units, dim), bf16),
+        cost(12 * group_rows * dim * units, 12 * dim * units + 4 * group_rows * dim),
+    )(scalars, ff_all, rows_all, up_weight, down_weight, *own_weights)
     blocks = n_far // n_keys
+    cols = dim // n_keys
     if not aligned:
-        pieces = ff_partial[units:].reshape(blocks, units // blocks, n_keys, dim // n_keys)
-        pieces = pieces.transpose(0, 2, 1, 3).reshape(n_far, units, dim // n_far)
-        pieces = pieces.transpose(1, 0, 2).reshape(units, dim)
-        ups = ff_partial[:units].reshape(units, n_far, PAIR, each)
-        ups = jnp.where(near == 0, ups, ups[:, :, ::-1]).reshape(units, dim)
-        ff_partial = jnp.concatenate([ups, pieces], 0)
-    ff_partial, packs[0] = tie(ff_partial, packs[0])
+        downs = ff_partial[1].reshape(n_far, share, n_keys, blocks, cols // blocks)
+        downs = downs.transpose(2, 1, 3, 0, 4).reshape(n_keys, units // n_keys * dim)
+        downs = jnp.stack(
+            [lax.dynamic_index_in_dim(downs, key ^ s, 0, False) for s in range(n_keys)]
+        )
+        ups = ff_partial[0].reshape(units, n_far, PAIR, each)
+        ups = jnp.where(near == 0, ups, ups[:, :, ::-1])
+        ff_partial = jnp.stack([ups.reshape(units, dim), downs.reshape(units, dim)])
+    ff_partial = ff_partial.reshape(2 * units, dim)
+    far_core, ff_partial = tie(far_core, ff_partial)
     ff_sum = lax.psum_scatter(ff_partial, "far", scatter_dimension=1, tiled=True)
-
-    (kv_a, stat_a, kl_a, vl_a), (given_a, kept_a), media_small, q_a = attend_back(0, packs, [], [])
-    far_core = over_keys(given_a, 1)
+    far_sum = add(kept_a, far_core)
+    far_sum, packs[0] = tie(far_sum, packs[0])
+    far_near = over_near(far_sum[:, 1])
     (kv_b, stat_b, kl_b, vl_b), (given_b, kept_b), media_small, q_b = attend_back(
         1, packs, q_a, [media_small]
     )
-    far_core, given_b, *q_b = tie(far_core, given_b, *q_b)
-    far_sum = add(kept_a, far_core)
+    far_near, given_b, *q_b = tie(far_near, given_b, *q_b)
+    far_half = add(far_sum[:, 0], far_near)
 
     col = lambda turn: pl.BlockSpec((dim, GROUP), lambda i, s: (0, s[5] ^ (1 - turn)))
     both = lambda value: [value, value]
@@ -1026,27 +1043,18 @@
         return tree_sum([value] + [over_far(value, s) for s in range(1, n_far)])
 
     gain = row(media_gain)
-    far_sum, gain, given_b, *q_b = tie(far_sum, gain, given_b, *q_b)
-    far_near = over_near(far_sum[:, 1])
+    far_half, gain, given_b, *q_b = tie(far_half, gain, given_b, *q_b)
+    far_got = [over_keys(far_half[j], half_keys + 2 * j) for j in range(n_keys // 4)]
     near_core = over_keys(given_b, 1)
     q_slots = exchange_keys(q_b)
     patches_grad = patch_back(0, gain, None)
-    patches_grad, far_near, near_core, *q_slots = tie(patches_grad, far_near, near_core, *q_slots)
-    far_half = add(far_sum[:, 0], far_near)
+    patches_grad, near_core, *q_slots = tie(patches_grad, near_core, *q_slots)
     near_sum = add(kept_b, near_core)
-    near_sum, far_half, lat, ff_sum = tie(near_sum, far_half, lat, ff_sum)
-    far_got = [over_keys(far_half[j], half_keys + 2 * j) for j in range(n_keys // 4)]
+    near_sum, lat = tie(near_sum, lat)
     total = near_sum[0]
     for j in range(1, n_keys // 4):
         total = add(total, over_keys(near_sum[j], 2 * j))
     near_got = over_near(total[1])
-    route = []
-    for m in range(n_media):
-        for k in range(n_keys):
-            block, owner = divmod(m // PAIR, n_keys)
-            target = (k * PAIR + m % PAIR) * blocks + block
-            route.append((m * n_keys + k, target * n_keys + owner))
-    down_grad = lax.ppermute(ff_sum[units:], ("far", "near", "keys"), route)
     small_rows = -(-(n_frames + 6) // 8) * 8
     latents_grad, small = call(
         functools.partial(latent_back_kernel, n_keys, frames, n_frames),
@@ -1079,41 +1087,32 @@
         *q_slots,
     )
 
-    gain, small, ff_sum = tie(gain, small, ff_sum)
-    small_got = over_keys(small, 1)
-    up_keep = ff_sum[:units, :each]
-    up_got = over_near(ff_sum[:units, each:])
+    gain, small = tie(gain, small)
+    small = tree_sum([small] + [over_keys(small, s) for s in range(1, n_keys)])
     patches_grad = patch_back(1, gain, patches_grad)
-    patches_grad, small_got, near_got, *far_got = tie(patches_grad, small_got, near_got, *far_got)
-    small = small + small_got
+    patches_grad, small, near_got, *far_got = tie(patches_grad, small, near_got, *far_got)
     total = total[0]
     for value in far_got:
         total = add(total, value)
     total = add(total, near_got)
-    if not aligned:
-        total = total.reshape(-1, n_far, each)
-        total = jnp.concatenate(
-            [lax.dynamic_index_in_dim(total, far ^ s, 1, False) for s in range(n_far)], 1
-        )
-    total, small, gain = tie(total, small, gain)
-    parts = [over_far(total[:, s * each : (s + 1) * each], s) for s in range(1, n_far)]
-    small = tree_sum([small] + [over_keys(small, s) for s in range(2, n_keys, 2)])
+    total, small, gain, ff_sum = tie(total, small, gain, ff_sum)
+    parts = lax.all_to_all(total, "far", split_axis=1, concat_axis=0, tiled=True)
+    small = small + over_near(small)
+    up_keep = ff_sum[:units, :each]
+    up_got = over_near(ff_sum[:units, each:])
+    downs = ff_sum[units:].reshape(n_keys, share, cols)
+    downs = exchange_keys([downs[s] for s in range(n_keys)])
     patches_grad = patch_back(2, gain, patches_grad)
-    patches_grad, small, up_got, down_grad, *parts = tie(
-        patches_grad, small, up_got, down_grad, *parts
-    )
-    small = small + over_near(small)
-    small, up_got = tie(small, up_got)
+    patches_grad, small, up_got, parts, *downs = tie(patches_grad, small, up_got, parts, *downs)
     small = sum_far(small)
-    parts = [total[:, :each]] + parts
     if aligned:
         q_grad, k_grad, v_grad, out_grad, up_grad, down_grad = call(
-            functools.partial(finish_kernel, width),
+            functools.partial(finish_kernel, n_keys, width),
             "finish_weights",
             (1,),
             [whole((units, each))] * 2
-            + [whole((units, dim // n_keys))]
-            + [whole(p.shape) for p in parts],
+            + [whole((share, cols))] * n_keys
+            + [whole(parts.shape)],
             [whole((each, width))] * 3
             + [
                 whole((inner // n_media, dim // n_keys)),
@@ -1127,9 +1126,9 @@
                 struct((units, dim // n_keys), f32),
             ],
             cost(0, 16 * width * each + 12 * units * each),
-        )(scalars, up_keep, up_got, down_grad, *parts)
+        )(scalars, up_keep, up_got, *downs, parts)
     else:
-        total = functools.reduce(jnp.add, [p.astype(f32) for p in parts])
+        total = jnp.sum(parts.reshape(n_far, -1, each).astype(f32), 0)
         q_grad, k_grad, v_grad = (total[i * width : (i + 1) * width].T for i in range(3))
         out_grad = total[3 * width :].reshape(-1, inner // n_media, each)
         out_grad = out_grad.transpose(1, 0, 2).reshape(inner // n_media, dim // n_keys)
@@ -1138,7 +1137,11 @@
             jnp.concatenate([up_keep, up_got], 0),
             jnp.concatenate([up_got, up_keep], 0),
         ).T.astype(f32)
-        down_grad = down_grad.reshape(units // blocks, dim // n_keys).astype(f32)
+        down_grad = jnp.zeros((units // blocks, cols), f32)
+        for s in range(n_keys):
+            down_grad = lax.dynamic_update_slice_in_dim(
+                down_grad, downs[s].astype(f32), (key ^ s) * share, 0
+            )
 
     return (
         resampled.reshape(latents.shape),

time: 201 us -> 188 us (0.935)
  waiting for transfers between devices: 34.3 us -> 21.6 us
    ppermute x4, waiting for transfers between devices: 6.54 us -> 0.01 us  [over_near(): return lax.ppermute(value, 'near', [(0, 1), (1, 0)])]
    all_to_all x0 -> x1, starting transfers between devices: none -> 4.25 us  [shards(): lax.all_to_all(total, 'far', split_axis=1, concat_axis=0, tiled=True)]
    ppermute x6 -> x3, starting transfers between devices: 8.22 us -> 4.39 us  [over_far(): return lax.ppermute(value, 'far', [(i, i ^ shift) for i in range(n_far)])]
    ppermute x17 -> x21, waiting for transfers between devices: 21.8 us -> 19.1 us  [over_keys(): return lax.ppermute(value, 'keys', [(i, i ^ shift) for i in range(n_keys)])]
    ppermute x6 -> x3, waiting for transfers between devices: 3.43 us -> 1.13 us  [over_far(): return lax.ppermute(value, 'far', [(i, i ^ shift) for i in range(n_far)])]
    ppermute x17 -> x21, starting transfers between devices: 14.4 us -> 13.3 us  [over_keys(): return lax.ppermute(value, 'keys', [(i, i ^ shift) for i in range(n_keys)])]
    pallas_call x12 -> x11, Pallas kernels: 116 us -> 115 us  [pinned(): return run(*args)]
  transfers between devices with their start and end apart: 31 -> 32, of which waited for: 11 -> 9; matrix products, arithmetic and copies ran while one was open for 2% -> 3% of each run, Pallas kernels for 52% -> 60%
where the time goes in v4:
time: 188 us
  Pallas kernels  115 us (61%)
  starting transfers between devices  27.4 us (15%)
  waiting for transfers between devices  21.6 us (11%)
  between operations  14.1 us (8%)
  local copies, waits for them, and re-layouts  8.04 us (4%)
  other arithmetic  2 us (1%)
    pallas_call x11, Pallas kernels, pinned(): return run(*args)  115 us
    ppermute x21, waiting for transfers between devices, over_keys(): return lax.ppermute(value, 'keys', [(i, i ^ shift) for i in range(n_keys)])  19.1 us
    ppermute x21, starting transfers between devices, over_keys(): return lax.ppermute(value, 'keys', [(i, i ^ shift) for i in range(n_keys)])  13.3 us
    ppermute x4, starting transfers between devices, over_near(): return lax.ppermute(value, 'near', [(0, 1), (1, 0)])  5.39 us
    ppermute x3, starting transfers between devices, over_far(): return lax.ppermute(value, 'far', [(i, i ^ shift) for i in range(n_far)])  4.39 us
    all_to_all x1, starting transfers between devices, shards(): lax.all_to_all(total, 'far', split_axis=1, concat_axis=0, tiled=True)  4.25 us
  transfers between devices with their start and end apart: 32, of which 9 were waited for; matrix products, arithmetic and copies ran while one was open for 3% of the time, Pallas kernels for 60%

profile of v4, /device:TPU:0, one launch (start us, length us, event | category | flops | bytes accessed | tf_op | source)
XLA Modules:
  0.0 188.0 jit_solution(11843850647199537587)
XLA Ops:
  7.2 2.6 %latent_project.1 = (bf16[96,2048]{1,0:T(8,128)(2,1)}, bf16[96,512]{1,0:T(8,128)(2,1)}) custom-call(f32[96,1024]{1,0:T(8,128)} %bitcast.42, f32[1,1024]{1,0:T(1,128)} %bitcast.59, f32[1,1024]{1,0:T(1,128)} %bitcast.61, f32[96,1024]{1,0:T(8,128)} %bitcast.46, bf16[1024,512]{1,0:T(8,128)(2,1)} %refs_8_.1), custom_call_target="tpu_custom_call" | custom-call | flops 100663296 | bytes 2424832 | tf_op jit(solution)/shard_map/latent_project/pallas_call | solution.py:693
  9.9 2.5 %collective-permute-start.2 = (bf16[96,512]{1,0:T(8,128)(2,1)}, bf16[96,512]{1,0:T(8,128)(2,1)S(1)}, u32[]{:S(2)}, u32[]{:S(2)}) collective-permute-start(bf16[96,512]{1,0:T(8,128)(2,1)} %get-tuple-element.114.refs_0_), channel_id=1, source_target_pairs={{0,3},{1,2},{2,1},{3,0},{4,7},{5,6},{6,5},{7,4},{8,11},{9,10},{10,... | collective-permute-start | bytes 294920 | tf_op jit(solution)/shard_map/ppermute | solution.py:638
  13.7 2.2 %collective-permute-done.2.refs_3_ = bf16[96,512]{1,0:T(8,128)(2,1)S(1)} collective-permute-done((bf16[96,512]{1,0:T(8,128)(2,1)}, bf16[96,512]{1,0:T(8,128)(2,1)S(1)}, u32[]{:S(2)}, u32[]{:S(2)}) %collective-permute-start.2) | collective-permute-done | bytes 98336 | tf_op jit(solution)/shard_map/ppermute | solution.py:638
  15.9 2.2 %collective-permute-done.1.refs_2_ = bf16[96,512]{1,0:T(8,128)(2,1)S(1)} collective-permute-done((bf16[96,512]{1,0:T(8,128)(2,1)}, bf16[96,512]{1,0:T(8,128)(2,1)S(1)}, u32[]{:S(2)}, u32[]{:S(2)}) %collective-permute-start.1) | collective-permute-done | bytes 98336 | tf_op jit(solution)/shard_map/ppermute | solution.py:638
  18.8 19.7 %project_attend.1 = (bf16[6,512,1024]{2,1,0:T(8,128)(2,1)}, bf16[6,512,512]{2,1,0:T(8,128)(2,1)}, bf16[6,512,512]{2,1,0:T(8,128)(2,1)}, bf16[96,512]{1,0:T(8,128...) custom-call(s32[7]{0:T(128)} %stack.24.scalars, ...), custom_call_target="tpu_custom_call" | custom-call | flops 8103395328 | bytes 37748736 | tf_op jit(solution)/shard_map/project_attend/pallas_call | solution.py:693
  38.5 2.4 %collective-permute-start.4 = (bf16[96,640]{1,0:T(8,128)(2,1)}, bf16[96,640]{1,0:T(8,128)(2,1)S(1)}, u32[]{:S(2)}, u32[]{:S(2)}) collective-permute-start(bf16[96,640]{1,0:T(8,128)(2,1)} %get-tuple-element.117), channel_id=1, source_target_pairs={{0,2},{1,3},{2,0},{3,1},{4,6},{5,7},{6,4},{7,5},{8,10},{9,11},{10,... | collective-permute-start | bytes 368648 | tf_op jit(solution)/shard_map/ppermute | solution.py:638
  41.0 5.6 %collective-permute-done.4.refs_2_ = bf16[96,640]{1,0:T(8,128)(2,1)S(1)} collective-permute-done((bf16[96,640]{1,0:T(8,128)(2,1)}, bf16[96,640]{1,0:T(8,128)(2,1)S(1)}, u32[]{:S(2)}, u32[]{:S(2)}) %collective-permute-start.4) | collective-permute-done | bytes 122912 | tf_op jit(solution)/shard_map/ppermute | solution.py:638
  46.6 2.4 %collective-permute-done.5.refs_3_ = bf16[96,640]{1,0:T(8,128)(2,1)S(1)} collective-permute-done((bf16[96,640]{1,0:T(8,128)(2,1)}, bf16[96,640]{1,0:T(8,128)(2,1)S(1)}, u32[]{:S(2)}, u32[]{:S(2)}) %collective-permute-start.5) | collective-permute-done | bytes 122912 | tf_op jit(solution)/shard_map/ppermute | solution.py:638
  49.7 16.6 %feed_forward.1 = (f32[96,1024]{1,0:T(8,128)}, f32[96,1024]{1,0:T(8,128)}, bf16[96,640]{1,0:T(8,128)(2,1)}, f32[2,1024]{1,0:T(2,128)}, bf16[4,128,1024]{2,1,0:T(8,128)(2,1)}, /*index=5*/bf16[96,1024]{1,0:T(8,128)(2,1)}) custom-call(s32[7]{0:T(128)} %stack.24.scalars, f32[96,1024]{1,0:T(8,128)} %bitcast.43, f32[96,1024]{1,0:T(8,128)} %bitcast.47, ...), custom_call_target="tpu_custom_call" | custom-call | flops 3221225472 | bytes 19136512 | tf_op jit(solution)/shard_map/feed_forward/pallas_call | solution.py:693
  66.7 5.4 %collective-permute-done.7.refs_6_.refs_10_ = bf16[96,640]{1,0:T(8,128)(2,1)S(1)} collective-permute-done((bf16[96,640]{1,0:T(8,128)(2,1)}, bf16[96,640]{1,0:T(8,128)(2,1)S(1)}, u32[]{:S(2)}, u32[]{:S(2)}) %collective-permute-start.7) | collective-permute-done | bytes 122912 | tf_op jit(solution)/shard_map/ppermute | solution.py:638
  74.0 17.4 %attend_back.2 = (bf16[2,256,3072]{2,1,0:T(8,128)(2,1)}, f32[8,3072]{1,0:T(8,128)}, bf16[96,256]{1,0:T(8,128)(2,1)}, bf16[96,256]{1,0:T(8,128)(2,1)}, bf16[1,2,5...) custom-call(s32[7]{0:T(128)} %stack.24.scalars, ...), custom_call_target="tpu_custom_call" | custom-call | flops 5297405952 | bytes 18874368 | tf_op jit(solution)/shard_map/attend_back/pallas_call | solution.py:693
  92.1 11.5 %feed_forward_weights.1 = bf16[2,512,1024]{2,1,0:T(8,128)(2,1)} custom-call(s32[7]{0:T(128)} %stack.24.scalars, bf16[768,1024]{1,0:T(8,128)(2,1)} %all-gather.5.cloned.1.call-done.ff_all, bf16[768,2048]{1,0:T(8,128)(2,1)} %all-gather.3.cloned.1.call-done.refs_24_.out_all, bf16[1024,4096]{1,0:T(8,128)(2,1)} %refs_1_.2, bf16[4096,1024]{1,0:T(8,128)(2,1)} %down.3, ...), custom_call_target="tpu_custom_call" | custom-call | flops 4831838208 | bytes 9437184 | tf_op jit(solution)/shard_map/feed_forward_weights/pallas_call | solution.py:693
  105.5 17.4 %attend_back.3 = (bf16[2,256,3072]{2,1,0:T(8,128)(2,1)}, f32[8,3072]{1,0:T(8,128)}, bf16[96,256]{1,0:T(8,128)(2,1)}, bf16[96,256]{1,0:T(8,128)(2,1)}, bf16[1,2,5...) custom-call(s32[7]{0:T(128)} %stack.24.scalars, ...), custom_call_target="tpu_custom_call" | custom-call | flops 5297405952 | bytes 18874368 | tf_op jit(solution)/shard_map/attend_back/pallas_call | solution.py:693
  126.3 7.3 %patch_back.3._ = bf16[6,512,1024]{2,1,0:T(8,128)(2,1)} custom-call(s32[7]{0:T(128)} %stack.24.scalars, bf16[2,256,3072]{2,1,0:T(8,128)(2,1)} %get-tuple-element.132.kv_a, bf16[2,256,3072]{2,1,0:T(8,128)(2,1)} %get-tuple-element.145.kv_b, f32[8,3072]{1,0:T(8,128)} %get-tuple-element.146.stat_a, f32[8,3072]{1,0:T(8,128)} %get-tuple-element.147.stat_b, ...), custom_call_target="tpu_custom_call" | custom-call | flops 2147483648 | bytes 8388608 | tf_op jit(solution)/shard_map/patch_back/pallas_call | solution.py:693
  134.0 1.8 collective-permute-start.18
  135.9 5.0 %latent_back.1 = (f32[96,1024]{1,0:T(8,128)}, f32[16,1024]{1,0:T(8,128)}) custom-call(s32[7]{0:T(128)} %stack.24.scalars, f32[96,1024]{1,0:T(8,128)} %bitcast.44, f32[1,1024]{1,0:T(1,128)} %bitcast.60, f32[96,1024]{1,0:T(8,128)} %get-tuple-element.170.mid_grad, f32[8,1024]{1,0:T(8,128)} %get-tuple-element.171.media_small, ...), custom_call_target="tpu_custom_call" | custom-call | flops 301989888 | bytes 5111808 | tf_op jit(solution)/shard_map/latent_back/pallas_call | solution.py:693
  140.9 1.7 collective-permute-start.16
  142.8 7.1 %patch_back.4._ = bf16[6,512,1024]{2,1,0:T(8,128)(2,1)} custom-call(s32[7]{0:T(128)} %stack.24.scalars, bf16[2,256,3072]{2,1,0:T(8,128)(2,1)} %get-tuple-element.132.kv_a, bf16[2,256,3072]{2,1,0:T(8,128)(2,1)} %get-tuple-element.145.kv_b, f32[8,3072]{1,0:T(8,128)} %get-tuple-element.146.stat_a, ...), custom_call_target="tpu_custom_call", output_to_operand_aliasing={{}: (13, {})} | custom-call | flops 2147483648 | bytes 8388608 | tf_op jit(solution)/shard_map/patch_back/pallas_call | solution.py:693
  152.1 4.3 %all-to-all-start = ((bf16[512,4,128]{2,0,1:T(8,128)(2,1)}), bf16[512,4,128]{2,0,1:T(8,128)(2,1)S(1)}, u32[]{:S(2)}, u32[]{:S(2)}) async-start(bf16[512,4,128]{2,0,1:T(8,128)(2,1)} %copy_bitcast_fusion), calls=%async_computation.1 | async-start | bytes 1048576 | tf_op jit(solution)/shard_map/all_to_all | solution.py:1099
  160.2 1.6 fusion.2
  161.9 1.6 collective-permute-start.21
  163.5 7.1 %patch_back.5 = bf16[6,512,1024]{2,1,0:T(8,128)(2,1)} custom-call(s32[7]{0:T(128)} %stack.24.scalars, bf16[2,256,3072]{2,1,0:T(8,128)(2,1)} %get-tuple-element.132.kv_a, bf16[2,256,3072]{2,1,0:T(8,128)(2,1)} %get-tuple-element.145.kv_b, f32[8,3072]{1,0:T(8,128)} %get-tuple-element.146.stat_a, ...), custom_call_target="tpu_custom_call", output_to_operand_aliasing={{}: (13, {})} | custom-call | flops 2147483648 | bytes 8388608 | tf_op jit(solution)/shard_map/patch_back/pallas_call | solution.py:693
  171.5 3.1 %collective-permute-start.27 = (f32[16,1024]{1,0:T(8,128)S(1)}, f32[16,1024]{1,0:T(8,128)S(1)}, u32[]{:S(2)}, u32[]{:S(2)}) collective-permute-start(f32[16,1024]{1,0:T(8,128)S(1)} %add.51), channel_id=1, source_target_pairs={{0,24},{8,16},{16,8},{24,0},{1,25},{9,17},{17,9},{25,1},{2,26},{10... | collective-permute-start | bytes 196616 | tf_op jit(solution)/shard_map/ppermute | solution.py:644
  175.9 3.2 %finish_weights.1 = (f32[128,128]{1,0:T(8,128)}, f32[128,128]{1,0:T(8,128)}, f32[128,128]{1,0:T(8,128)}, f32[64,256]{1,0:T(8,128)}, f32[128,1024]{1,0:T(8,128)}, /*index=5*/f32[512,256]{1,0:T(8,128)}) custom-call(s32[7]{0:T(128)} %stack.24.scalars, bf16[512,128]{1,0:T(8,128)(2,1)} %get-tuple-element.210.up_keep, bf16[512,128]{1,0:T(8,128)(2,1)} %copy-done.9, ...), custom_call_target="tpu_custom_call" | custom-call | bytes 1048576 | tf_op jit(solution)/shard_map/finish_weights/pallas_call | solution.py:693
  (109 shorter events, 22.3 us)
Async XLA Ops:
  7.2 59.1 %all-gather.3.cloned.1.call-start = ((), (), s32[]{:S(2)}) async-start(), calls=%async_computation.2 | async-start | bytes 3538944 | tf_op jit(solution)/shard_map/all_gather | solution.py:708
  9.9 82.2 %all-gather.5.cloned.1.call-start = ((), (), s32[]{:S(2)}) async-start(), calls=%async_computation.3 | async-start | bytes 1769472 | tf_op jit(solution)/shard_map/all_gather | solution.py:821
  9.9 6.0 %collective-permute-start.2 = (bf16[96,512]{1,0:T(8,128)(2,1)}, bf16[96,512]{1,0:T(8,128)(2,1)S(1)}, u32[]{:S(2)}, u32[]{:S(2)}) collective-permute-start(bf16[96,512]{1,0:T(8,128)(2,1)} %get-tuple-element.114.refs_0_), channel_id=1, source_target_pairs={{0,3},{1,2},{2,1},{3,0},{4,7},{5,6},{6,5},{7,4},{8,11},{9,10},{10,... | collective-permute-start | bytes 294920 | tf_op jit(solution)/shard_map/ppermute | solution.py:638
  38.5 8.0 %collective-permute-start.4 = (bf16[96,640]{1,0:T(8,128)(2,1)}, bf16[96,640]{1,0:T(8,128)(2,1)S(1)}, u32[]{:S(2)}, u32[]{:S(2)}) collective-permute-start(bf16[96,640]{1,0:T(8,128)(2,1)} %get-tuple-element.117), channel_id=1, source_target_pairs={{0,2},{1,3},{2,0},{3,1},{4,6},{5,7},{6,4},{7,5},{8,10},{9,11},{10,... | collective-permute-start | bytes 368648 | tf_op jit(solution)/shard_map/ppermute | solution.py:638
  40.9 8.1 %collective-permute-start.5 = (bf16[96,640]{1,0:T(8,128)(2,1)}, bf16[96,640]{1,0:T(8,128)(2,1)S(1)}, u32[]{:S(2)}, u32[]{:S(2)}) collective-permute-start(bf16[96,640]{1,0:T(8,128)(2,1)} %get-tuple-element.118), channel_id=1, source_target_pairs={{0,3},{1,2},{2,1},{3,0},{4,7},{5,6},{6,5},{7,4},{8,11},{9,10},{10,... | collective-permute-start | bytes 368648 | tf_op jit(solution)/shard_map/ppermute | solution.py:638
  66.3 84.9 %reduce-scatter.2.cloned.1.call-start = ((), (), s32[]{:S(2)}) async-start(), calls=%async_computation.4 | async-start | bytes 2621440 | tf_op jit(solution)/shard_map/reduce_scatter | solution.py:981
  91.4 12.2 %collective-permute-start.9 = (bf16[1,2,512,512]{3,2,1,0:T(8,128)(2,1)}, bf16[1,2,512,512]{3,2,1,0:T(8,128)(2,1)S(1)}, u32[]{:S(2)}, u32[]{:S(2)}) collective-permute-start(bf16[1,2,512,512]{3,2,1,0:T(8,128)(2,1)} %get-tuple-element.136), channel_id=1, source_target_pairs={{0,1},{1,0},{2,3},{3,2},{4,5},{5,4},{6,7},{7,6},{8,9},{9,8},{10,11... | collective-permute-start | bytes 3145736 | tf_op jit(solution)/shard_map/ppermute | solution.py:638
  104.0 18.9 %collective-permute-start.10 = (bf16[1,512,512]{2,1,0:T(8,128)(2,1)S(1)}, bf16[1,512,512]{2,1,0:T(8,128)(2,1)S(1)}, u32[]{:S(2)}, u32[]{:S(2)}) collective-permute-start(bf16[1,512,512]{2,1,0:T(8,128)(2,1)S(1)} %slice_bitcast_fusion.1), channel_id=1, source_target_pairs={{0,4},{4,0},{1,5},{5,1},{2,6},{6,2},{3,7},{7,3},{8,12},{12,8},{9,1... | collective-permute-start | bytes 1572872 | tf_op jit(solution)/shard_map/ppermute | solution.py:641
  123.0 10.6 %collective-permute-start.11 = (bf16[1,2,512,512]{3,2,1,0:T(8,128)(2,1)}, bf16[1,2,512,512]{3,2,1,0:T(8,128)(2,1)S(1)}, u32[]{:S(2)}, u32[]{:S(2)}) collective-permute-start(bf16[1,2,512,512]{3,2,1,0:T(8,128)(2,1)} %get-tuple-element.162), channel_id=1, source_target_pairs={{0,1},{1,0},{2,3},{3,2},{4,5},{5,4},{6,7},{7,6},{8,9},{9,8},{10,11... | collective-permute-start | bytes 3145736 | tf_op jit(solution)/shard_map/ppermute | solution.py:638
  123.1 10.5 %collective-permute-start.12 = (bf16[96,512]{1,0:T(8,128)(2,1)}, bf16[96,512]{1,0:T(8,128)(2,1)S(1)}, u32[]{:S(2)}, u32[]{:S(2)}) collective-permute-start(bf16[96,512]{1,0:T(8,128)(2,1)} %get-tuple-element.164), channel_id=1, source_target_pairs={{0,1},{1,0},{2,3},{3,2},{4,5},{5,4},{6,7},{7,6},{8,9},{9,8},{10,11... | collective-permute-start | bytes 294920 | tf_op jit(solution)/shard_map/ppermute | solution.py:638
  123.6 10.0 %collective-permute-start.13 = (bf16[96,512]{1,0:T(8,128)(2,1)}, bf16[96,512]{1,0:T(8,128)(2,1)S(1)}, u32[]{:S(2)}, u32[]{:S(2)}) collective-permute-start(bf16[96,512]{1,0:T(8,128)(2,1)} %get-tuple-element.165), channel_id=1, source_target_pairs={{0,2},{1,3},{2,0},{3,1},{4,6},{5,7},{6,4},{7,5},{8,10},{9,11},{10,... | collective-permute-start | bytes 294920 | tf_op jit(solution)/shard_map/ppermute | solution.py:638
  124.7 9.0 %collective-permute-start.14 = (bf16[96,512]{1,0:T(8,128)(2,1)}, bf16[96,512]{1,0:T(8,128)(2,1)S(1)}, u32[]{:S(2)}, u32[]{:S(2)}) collective-permute-start(bf16[96,512]{1,0:T(8,128)(2,1)} %get-tuple-element.166), channel_id=1, source_target_pairs={{0,3},{1,2},{2,1},{3,0},{4,7},{5,6},{6,5},{7,4},{8,11},{9,10},{10,... | collective-permute-start | bytes 294920 | tf_op jit(solution)/shard_map/ppermute | solution.py:638
  125.0 24.9 %collective-permute-start.19 = (bf16[512,512]{1,0:T(8,128)(2,1)S(1)}, bf16[512,512]{1,0:T(8,128)(2,1)}, u32[]{:S(2)}, u32[]{:S(2)}) collective-permute-start(bf16[512,512]{1,0:T(8,128)(2,1)S(1)} %bitcast.48), channel_id=1, source_target_pairs={{0,2},{1,3},{2,0},{3,1},{4,6},{5,7},{6,4},{7,5},{8,10},{9,11},{10,... | collective-permute-start | bytes 1572872 | tf_op jit(solution)/shard_map/ppermute | solution.py:638
  134.0 16.0 %collective-permute-start.18 = (bf16[512,512]{1,0:T(8,128)(2,1)S(1)}, bf16[512,512]{1,0:T(8,128)(2,1)S(1)}, u32[]{:S(2)}, u32[]{:S(2)}) collective-permute-start(bf16[512,512]{1,0:T(8,128)(2,1)S(1)} %slice_bitcast_fusion), channel_id=1, source_target_pairs={{0,4},{4,0},{1,5},{5,1},{2,6},{6,2},{3,7},{7,3},{8,12},{12,8},{9,1... | collective-permute-start | bytes 1572872 | tf_op jit(solution)/shard_map/ppermute | solution.py:641
  140.8 9.1 %collective-permute-start.17 = (f32[16,1024]{1,0:T(8,128)}, f32[16,1024]{1,0:T(8,128)S(1)}, u32[]{:S(2)}, u32[]{:S(2)}) collective-permute-start(f32[16,1024]{1,0:T(8,128)} %get-tuple-element.184), channel_id=1, source_target_pairs={{0,3},{1,2},{2,1},{3,0},{4,7},{5,6},{6,5},{7,4},{8,11},{9,10},{10,... | collective-permute-start | bytes 196616 | tf_op jit(solution)/shard_map/ppermute | solution.py:638
  140.9 9.0 %collective-permute-start.16 = (f32[16,1024]{1,0:T(8,128)}, f32[16,1024]{1,0:T(8,128)S(1)}, u32[]{:S(2)}, u32[]{:S(2)}) collective-permute-start(f32[16,1024]{1,0:T(8,128)} %get-tuple-element.184), channel_id=1, source_target_pairs={{0,2},{1,3},{2,0},{3,1},{4,6},{5,7},{6,4},{7,5},{8,10},{9,11},{10,... | collective-permute-start | bytes 196616 | tf_op jit(solution)/shard_map/ppermute | solution.py:638
  142.6 7.3 %collective-permute-start.15 = (f32[16,1024]{1,0:T(8,128)}, f32[16,1024]{1,0:T(8,128)S(1)}, u32[]{:S(2)}, u32[]{:S(2)}) collective-permute-start(f32[16,1024]{1,0:T(8,128)} %get-tuple-element.184), channel_id=1, source_target_pairs={{0,1},{1,0},{2,3},{3,2},{4,5},{5,4},{6,7},{7,6},{8,9},{9,8},{10,11... | collective-permute-start | bytes 196616 | tf_op jit(solution)/shard_map/ppermute | solution.py:638
  152.1 19.3 %all-to-all-start = ((bf16[512,4,128]{2,0,1:T(8,128)(2,1)}), bf16[512,4,128]{2,0,1:T(8,128)(2,1)S(1)}, u32[]{:S(2)}, u32[]{:S(2)}) async-start(bf16[512,4,128]{2,0,1:T(8,128)(2,1)} %copy_bitcast_fusion), calls=%async_computation.1 | async-start | bytes 1048576 | tf_op jit(solution)/shard_map/all_to_all | solution.py:1099
  156.4 14.2 %collective-permute-start.20 = (f32[16,1024]{1,0:T(8,128)S(1)}, f32[16,1024]{1,0:T(8,128)S(1)}, u32[]{:S(2)}, u32[]{:S(2)}) collective-permute-start(f32[16,1024]{1,0:T(8,128)S(1)} %add_add_fusion.1), channel_id=1, source_target_pairs={{0,4},{4,0},{1,5},{5,1},{2,6},{6,2},{3,7},{7,3},{8,12},{12,8},{9,1... | collective-permute-start | bytes 196616 | tf_op jit(solution)/shard_map/ppermute | solution.py:641
  158.4 12.3 %collective-permute-start.24 = (bf16[128,256]{1,0:T(8,128)(2,1)S(1)}, bf16[128,256]{1,0:T(8,128)(2,1)S(1)}, u32[]{:S(2)}, u32[]{:S(2)}) collective-permute-start(bf16[128,256]{1,0:T(8,128)(2,1)S(1)} %get-tuple-element.212), channel_id=1, source_target_pairs={{0,3},{1,2},{2,1},{3,0},{4,7},{5,6},{6,5},{7,4},{8,11},{9,10},{10,... | collective-permute-start | bytes 196616 | tf_op jit(solution)/shard_map/ppermute | solution.py:638
  158.8 11.9 %collective-permute-start.23 = (bf16[128,256]{1,0:T(8,128)(2,1)S(1)}, bf16[128,256]{1,0:T(8,128)(2,1)S(1)}, u32[]{:S(2)}, u32[]{:S(2)}) collective-permute-start(bf16[128,256]{1,0:T(8,128)(2,1)S(1)} %get-tuple-element.213), channel_id=1, source_target_pairs={{0,2},{1,3},{2,0},{3,1},{4,6},{5,7},{6,4},{7,5},{8,10},{9,11},{10,... | collective-permute-start | bytes 196616 | tf_op jit(solution)/shard_map/ppermute | solution.py:638
  160.0 10.7 %collective-permute-start.22 = (bf16[128,256]{1,0:T(8,128)(2,1)S(1)}, bf16[128,256]{1,0:T(8,128)(2,1)S(1)}, u32[]{:S(2)}, u32[]{:S(2)}) collective-permute-start(bf16[128,256]{1,0:T(8,128)(2,1)S(1)} %get-tuple-element.214), channel_id=1, source_target_pairs={{0,1},{1,0},{2,3},{3,2},{4,5},{5,4},{6,7},{7,6},{8,9},{9,8},{10,11... | collective-permute-start | bytes 196616 | tf_op jit(solution)/shard_map/ppermute | solution.py:638
  161.9 8.8 %collective-permute-start.21 = (bf16[512,128]{1,0:T(8,128)(2,1)S(1)}, bf16[512,128]{1,0:T(8,128)(2,1)S(1)}, u32[]{:S(2)}, u32[]{:S(2)}) collective-permute-start(bf16[512,128]{1,0:T(8,128)(2,1)S(1)} %get-tuple-element.211), channel_id=1, source_target_pairs={{0,4},{4,0},{1,5},{5,1},{2,6},{6,2},{3,7},{7,3},{8,12},{12,8},{9,1... | collective-permute-start | bytes 393224 | tf_op jit(solution)/shard_map/ppermute | solution.py:641
  171.5 7.6 %collective-permute-start.27 = (f32[16,1024]{1,0:T(8,128)S(1)}, f32[16,1024]{1,0:T(8,128)S(1)}, u32[]{:S(2)}, u32[]{:S(2)}) collective-permute-start(f32[16,1024]{1,0:T(8,128)S(1)} %add.51), channel_id=1, source_target_pairs={{0,24},{8,16},{16,8},{24,0},{1,25},{9,17},{17,9},{25,1},{2,26},{10... | collective-permute-start | bytes 196616 | tf_op jit(solution)/shard_map/ppermute | solution.py:644
  (28 other events, 114.8 us)
Sparse Core Ops, SparseCore 0:
  10.5 36.5 all-gather.2
  66.5 25.6 all-gather.4
  103.7 44.5 reduce-scatter.1

commit v5 on v4

--- a/solution.py
+++ b/solution.py
@@ -12,10 +12,11 @@
 GROUP = 256
 LANES = 128
 
-VMEM_LIMIT = 60 << 20
+VMEM_LIMIT = 44 << 20
 
 EPS = 1e-05
 NEG = -1e30
+SIDE = 2
 PAIR = 2
 
 f32 = jnp.float32
@@ -351,12 +352,13 @@
     kv_t_o, stat_o, kl_o, vl_o, given, kept, small = take(7)
     q_o = take(n_keys)
     grad_acc, sums, scalar_sums, q_acc, rows_all, wo_g, wk, wv, sems = refs
+    n = kp.shape[0]
+    each = range(n)
     rows = kl_o.shape[0]
-    own = rows // pl.num_programs(0)
+    own = rows // (pl.num_programs(0) * n)
     dim = low.shape[2]
     per = GROUP // HEAD
     step = pl.program_id(0)
-    count = counts[step]
     first_frame = scalars[0] * frames
     group = scalars[5] ^ (1 - turn)
     owners = GROUP // width
@@ -377,77 +379,92 @@
         sums[...] = jnp.zeros_like(sums)
         scalar_sums[...] = jnp.zeros_like(scalar_sums)
 
-    here = pl.ds(pl.multiple_of(step * own, own), own)
-    query = jnp.concatenate([r[here, :] for r in q], 0)
-    grad = jnp.concatenate([r[here, :] for r in grads], 0)
-    stats = jnp.concatenate([r[here, :] for r in stat], 0).astype(f32)
-    n_query = query.shape[0]
+    here = [pl.ds(pl.multiple_of((step * n + m) * own, own), own) for m in each]
+    n_patch = kp.shape[1]
+    n_query = n_keys * own
     row, lane = head_mask(n_query, LANES, per)
-    tiled = jnp.concatenate([stats] * per, 0)
     mine = lane % heads == row + group * per
-    level = jnp.sum(jnp.where(mine & (lane < 3 * heads), tiled, 0.0), -1, keepdims=True)
-    delta = jnp.sum(
-        jnp.where(mine & (lane >= 3 * heads) & (lane < 6 * heads), tiled, 0.0), -1, keepdims=True
+    levels = mine & (lane < 3 * heads)
+    deltas = mine & (lane >= 3 * heads) & (lane < 6 * heads)
+    wide, wide_grad, keys, values, level, delta = [], [], [], [], [], []
+    for m in each:
+        wide.append(
+            spread_heads(jnp.concatenate([r[here[m], :] for r in q], 0) * bf16(HEAD**-0.5))
+        )
+        wide_grad.append(spread_heads(jnp.concatenate([r[here[m], :] for r in grads], 0)))
+        keys.append(jnp.concatenate([kp[m], kl[here[m], :]], 0))
+        values.append(jnp.concatenate([vp[m], vl[here[m], :]], 0))
+    scores = [
+        masked_scores(wide[m], keys[m], frames, first_frame, counts[step * n + m]) for m in each
+    ]
+    prob_grad = [mul(wide_grad[m], values[m], NT) for m in each]
+    for m in each:
+        stats = jnp.concatenate([r[here[m], :] for r in stat], 0).astype(f32)
+        tiled = jnp.concatenate([stats] * per, 0)
+        level.append(jnp.sum(jnp.where(levels, tiled, 0.0), -1, keepdims=True))
+        delta.append(jnp.sum(jnp.where(deltas, tiled, 0.0), -1, keepdims=True))
+    probs = [jnp.exp(scores[m] - level[m]) for m in each]
+    score_grad = [probs[m] * (prob_grad[m] - delta[m]) for m in each]
+    along = [
+        jnp.sum(score_grad[m] * scores[m] + probs[m] * prob_grad[m], 0, keepdims=True) for m in each
+    ]
+    score_grad = [v.astype(bf16) for v in score_grad]
+    probs = [v.astype(bf16) for v in probs]
+    beside = lambda value, vec: jnp.concatenate(
+        [value, mul(value, vec[...].astype(bf16), NT).astype(bf16)], 1
     )
-    wide = spread_heads(query * bf16(HEAD**-0.5))
-    wide_grad = spread_heads(grad)
-    keys = jnp.concatenate([kp[0], kl[here, :]], 0)
-    values = jnp.concatenate([vp[0], vl[here, :]], 0)
-    n_patch = kp.shape[1]
-    scores = masked_scores(wide, keys, frames, first_frame, count)
-    probs = jnp.exp(scores - level)
-    prob_grad = mul(wide_grad, values, NT)
-    score_grad = probs * (prob_grad - delta)
-    along = jnp.sum(score_grad * scores + probs * prob_grad, 0, keepdims=True)
-    score_grad = score_grad.astype(bf16)
-    key_side = jnp.concatenate([wide, mul(wide, k_vec[...].astype(bf16), NT).astype(bf16)], 1)
-    value_side = jnp.concatenate(
-        [wide_grad, mul(wide_grad, v_vec[...].astype(bf16), NT).astype(bf16)], 1
-    )
-    key_t = mul(key_side, score_grad, TN)
-    value_t = mul(value_side, probs.astype(bf16), TN)
-    kl_o[here, :] = key_t[:GROUP, n_patch:].T.astype(bf16)
-    vl_o[here, :] = value_t[:GROUP, n_patch:].T.astype(bf16)
-    kv = jnp.concatenate([key_t[:GROUP, :n_patch], value_t[:GROUP, :n_patch]], 0).astype(bf16)
-    kv_t_o[0] = kv[:GROUP]
-    kv_t_o[1] = kv[GROUP:]
-    ends = key_t[GROUP:, :n_patch] + value_t[GROUP:, :n_patch]
-    line = lax.broadcasted_iota(jnp.int32, ends.shape, 0)
-    stat_rows = jnp.where(line == 1, along[:, :n_patch] - ends, ends)
-    span = pl.ds(pl.multiple_of(step * n_patch, n_patch), n_patch)
-    stat_o[:, span] = stat_rows
-
-    scale = norm_stat[1:2, span] * (1.0 / dim)
-    first = stat_rows[0:1, :] * scale
-    second = stat_rows[1:2, :] * scale
+    key_side = [beside(v, k_vec) for v in wide]
+    value_side = [beside(v, v_vec) for v in wide_grad]
+    key_t = [mul(key_side[m], score_grad[m], TN) for m in each]
+    value_t = [mul(value_side[m], probs[m], TN) for m in each]
+    query_grad = [mul(score_grad[m], keys[m]) for m in each]
     frame = lax.broadcasted_iota(jnp.int32, (16, n_patch), 1) // PATCH
     row16 = lax.broadcasted_iota(jnp.int32, (16, n_patch), 0)
-    high = second.astype(bf16).astype(f32)
     same = frame == row16 % frames
-    ends = jnp.where(same & (row16 < frames), high, 0.0)
-    ends = jnp.where(same & (row16 >= frames) & (row16 < 2 * frames), second - high, ends)
-    grad_acc[...] += mul(jnp.concatenate([kv, ends.astype(bf16)], 0), low[0])
-    sums[...] += mul(kv, once[0])
-    line = lax.broadcasted_iota(jnp.int32, scalar_sums.shape, 0)
+    sides, kvs = [], []
+    line8 = lax.broadcasted_iota(jnp.int32, scalar_sums.shape, 0)
     adds = jnp.zeros(scalar_sums.shape, f32)
-    for f in range(frames):
-        span = slice(f * PATCH, (f + 1) * PATCH)
-        adds = jnp.where(line == f, jnp.sum(first[:, span], -1, keepdims=True), adds)
-        adds = jnp.where(line == frames + f, jnp.sum(second[:, span], -1, keepdims=True), adds)
+    for m in each:
+        kl_o[here[m], :] = key_t[m][:GROUP, n_patch:].T.astype(bf16)
+        vl_o[here[m], :] = value_t[m][:GROUP, n_patch:].T.astype(bf16)
+        kv = jnp.concatenate([key_t[m][:GROUP, :n_patch], value_t[m][:GROUP, :n_patch]], 0)
+        kv = kv.astype(bf16)
+        kv_t_o[0, :, m * n_patch : (m + 1) * n_patch] = kv[:GROUP]
+        kv_t_o[1, :, m * n_patch : (m + 1) * n_patch] = kv[GROUP:]
+        ends = key_t[m][GROUP:, :n_patch] + value_t[m][GROUP:, :n_patch]
+        line = lax.broadcasted_iota(jnp.int32, ends.shape, 0)
+        stat_rows = jnp.where(line == 1, along[m][:, :n_patch] - ends, ends)
+        span = pl.ds(pl.multiple_of((step * n + m) * n_patch, n_patch), n_patch)
+        stat_o[:, span] = stat_rows
+        scale = norm_stat[1:2, span] * (1.0 / dim)
+        first = stat_rows[0:1, :] * scale
+        second = stat_rows[1:2, :] * scale
+        high = second.astype(bf16).astype(f32)
+        ends = jnp.where(same & (row16 < frames), high, 0.0)
+        ends = jnp.where(same & (row16 >= frames) & (row16 < 2 * frames), second - high, ends)
+        kvs.append(kv)
+        sides.append(jnp.concatenate([kv, ends.astype(bf16)], 0))
+        for f in range(frames):
+            cut = slice(f * PATCH, (f + 1) * PATCH)
+            one = jnp.sum(first[:, cut], -1, keepdims=True)
+            two = jnp.sum(second[:, cut], -1, keepdims=True)
+            adds = adds + jnp.where(line8 == f, one, jnp.where(line8 == frames + f, two, 0.0))
     scalar_sums[...] += adds
-
-    query_grad = mul(score_grad, keys)
-    query_grad = (fold_heads(query_grad) * HEAD**-0.5).astype(bf16)
-    for s in range(n_keys):
-        part = query_grad[s * own : (s + 1) * own]
-        place = pl.multiple_of((scalars[0] ^ s) * rows + step * own, own)
-        q_acc[pl.ds(place, own), :] = part
-        if turn == 0:
-            q_o[s][here, :] = part
-        else:
-            other = pl.ds(pl.multiple_of((1 - group) * GROUP, GROUP), GROUP)
-            q_o[s][here, group_cols] = part
-            q_o[s][here, other] = q_before[s][here, :]
+    grad_acc[...] += mul(jnp.concatenate(sides, 1), low[...].reshape(n * n_patch, dim))
+    sums[...] += mul(jnp.concatenate(kvs, 1), once[...].reshape(n * n_patch, LANES))
+
+    for m in each:
+        part = (fold_heads(query_grad[m]) * HEAD**-0.5).astype(bf16)
+        for s in range(n_keys):
+            piece = part[s * own : (s + 1) * own]
+            place = pl.multiple_of((scalars[0] ^ s) * rows + (step * n + m) * own, own)
+            q_acc[pl.ds(place, own), :] = piece
+            if turn == 0:
+                q_o[s][here[m], :] = piece
+            else:
+                other = pl.ds(pl.multiple_of((1 - group) * GROUP, GROUP), GROUP)
+                q_o[s][here[m], group_cols] = piece
+                q_o[s][here[m], other] = q_before[s][here[m], :]
 
     @pl.when(step == pl.num_programs(0) - 1)
     def _():
@@ -585,7 +602,7 @@
 
 
 def struct(shape, dtype):
-    return jax.ShapeDtypeStruct(shape, dtype)
+    return pltpu.HBM(shape, dtype)
 
 
 def tree_sum(parts):
@@ -668,7 +685,7 @@
     patch_flops = 4 * all_rows * dim * inner
     att_flops = 4 * media * n_keys * own * (key_rows + own) * inner * (GROUP // HEAD)
 
-    def call(kernel, name, grid, in_specs, out_specs, out_shape, price, prefetch=1, **more):
+    def call(kernel, name, grid, in_specs, out_specs, out_shape, price, prefetch=1, free=(), **more):
         run = pl.pallas_call(
             kernel,
             name=name,
@@ -688,7 +705,7 @@
         def pinned(*args):
             args = list(args)
             for i in range(prefetch, len(args)):
-                if in_specs[i - prefetch].memory_space is None:
+                if i - prefetch not in free:
                     args[i] = pltpu.with_memory_space_constraint(args[i], pltpu.HBM)
             return run(*args)
 
@@ -745,6 +762,7 @@
         + [struct((rows, packed), bf16)] * n_keys,
         cost(patch_flops + att_flops, 12 * all_rows * dim),
         prefetch=2,
+        free=range(8, 7 + n_keys),
     )(
         scalars,
         frame_counts,
@@ -796,6 +814,7 @@
             struct((rows, dim), bf16),
         ),
         cost(8 * rows * dim * hidden, 4 * dim * hidden + 24 * rows * dim),
+        free=range(9, 8 + n_keys),
         scratch_shapes=[
             pltpu.VMEM((rows, dim), f32),
             pltpu.VMEM((rows, dim), f32),
@@ -841,7 +860,8 @@
         g = pick(turn)
         own_cols = pl.BlockSpec((rows, GROUP), lambda i, s, *_: (0, g(s)))
         stat_cols = pl.BlockSpec((rows, LANES), lambda i, *_: (0, inner // LANES))
-        key_cols = pl.BlockSpec((1, key_rows, GROUP), lambda i, s, *_: (i, 0, g(s)))
+        n = SIDE if media % SIDE == 0 else 1
+        key_cols = pl.BlockSpec((n, key_rows, GROUP), lambda i, s, *_: (i, 0, g(s)))
         far_spec = pl.BlockSpec(memory_space=pl.ANY)
         q_width = GROUP if turn == 0 else inner
         chain = (n_keys // 4, PAIR, high, dim // PAIR)
@@ -850,15 +870,15 @@
                 attend_back_kernel, n_keys, frames, turn, inner // HEAD, width, aligned
             ),
             "attend_back",
-            (media,),
+            (media // n,),
             [own_cols] * (2 * n_keys)
             + [stat_cols] * n_keys
             + [key_cols, key_cols, own_cols, own_cols]
             + [
                 pl.BlockSpec((8, GROUP), lambda i, s, *_: (0, g(s))),
                 pl.BlockSpec((8, GROUP), lambda i, s, *_: (0, inner // GROUP + g(s))),
-                patch_block,
-                pl.BlockSpec((1, key_rows, LANES), lambda i, *_: (i, 0, 0)),
+                pl.BlockSpec((n, key_rows, dim), lambda i, *_: (i, 0, 0)),
+                pl.BlockSpec((n, key_rows, LANES), lambda i, *_: (i, 0, 0)),
                 whole((8, all_rows)),
                 pl.BlockSpec((rows, dim), lambda i, *_: (0, 0)),
                 whole((1, dim)),
@@ -868,7 +888,7 @@
             + [whole((rows, GROUP))] * len(q_before)
             + [whole((8, dim))] * len(small_before),
             [
-                pl.BlockSpec((2, GROUP, key_rows), lambda i, *_: (0, 0, i)),
+                pl.BlockSpec((2, GROUP, n * key_rows), lambda i, *_: (0, 0, i)),
                 whole((8, all_rows)),
                 whole((rows, GROUP)),
                 whole((rows, GROUP)),
@@ -889,6 +909,7 @@
             + [struct((rows, q_width), bf16)] * n_keys,
             cost(5 * att_flops // 4 + patch_flops // 2, 4 * all_rows * (inner + dim)),
             prefetch=2,
+            free=tuple(j * n_keys + s for j in range(3) for s in range(1, n_keys)),
             scratch_shapes=[
                 pltpu.VMEM((2 * GROUP + 16, dim), f32),
                 pltpu.VMEM((2 * GROUP, LANES), f32),
@@ -1068,6 +1089,7 @@
         [whole((rows, dim)), whole((small_rows, dim))],
         (struct((rows, dim), f32), struct((small_rows, dim), f32)),
         cost(6 * rows * dim * inner, 6 * dim * inner + 20 * rows * dim),
+        free=range(15, 14 + n_keys),
     )(
         scalars,
         lat,
@@ -1126,6 +1148,7 @@
                 struct((units, dim // n_keys), f32),
             ],
             cost(0, 16 * width * each + 12 * units * each),
+            free=(1,) + tuple(range(3, 3 + n_keys)),
         )(scalars, up_keep, up_got, *downs, parts)
     else:
         total = jnp.sum(parts.reshape(n_far, -1, each).astype(f32), 0)

time: 188 us -> 184 us (0.979)
  Pallas kernels: 115 us -> 110 us
  waiting for transfers between devices: 21.6 us -> 26 us
  local copies, waits for them, and re-layouts: 8.04 us -> 6.15 us
    pallas_call x11, Pallas kernels: 115 us -> 110 us  [pinned(): return run(*args)]
    all_gather x1, waiting for transfers between devices: 0.51 us -> 2.82 us  [shards(): ff_all = lax.all_gather(ff_low, ('near', 'keys'), axis=0, tiled=True)]
  transfers between devices with their start and end apart: 32 -> 32, of which waited for: 9 -> 10; matrix products, arithmetic and copies ran while one was open for 3% -> 2% of each run, Pallas kernels for 60% -> 59%
where the time goes in v5:
time: 184 us; the launch traced here: 183 us
  Pallas kernels  110 us (60%)
  waiting for transfers between devices  26 us (14%)
  starting transfers between devices  25.9 us (14%)
  between operations  14 us (8%)
  local copies, waits for them, and re-layouts  6.15 us (3%)
    pallas_call x11, Pallas kernels, pinned(): return run(*args)  110 us
    ppermute x21, waiting for transfers between devices, over_keys(): return lax.ppermute(value, 'keys', [(i, i ^ shift) for i in range(n_keys)])  20 us
    ppermute x21, starting transfers between devices, over_keys(): return lax.ppermute(value, 'keys', [(i, i ^ shift) for i in range(n_keys)])  12.6 us
    ppermute x4, starting transfers between devices, over_near(): return lax.ppermute(value, 'near', [(0, 1), (1, 0)])  4.58 us
    ppermute x3, starting transfers between devices, over_far(): return lax.ppermute(value, 'far', [(i, i ^ shift) for i in range(n_far)])  4.39 us
    all_to_all x1, starting transfers between devices, shards(): lax.all_to_all(total, 'far', split_axis=1, concat_axis=0, tiled=True)  4.05 us
  transfers between devices with their start and end apart: 32, of which 10 were waited for; matrix products, arithmetic and copies ran while one was open for 2% of the time, Pallas kernels for 59%

profile of v5, /device:TPU:0, one launch (start us, length us, event | category | flops | bytes accessed | tf_op | source)
XLA Modules:
  0.0 183.3 jit_solution(17624401389827463627)
XLA Ops:
  7.2 2.6 %latent_project.1 = (bf16[96,2048]{1,0:T(8,128)(2,1)}, bf16[96,512]{1,0:T(8,128)(2,1)}) custom-call(f32[96,1024]{1,0:T(8,128)} %bitcast.43, f32[1,1024]{1,0:T(1,128)} %bitcast.59, f32[1,1024]{1,0:T(1,128)} %bitcast.61, f32[96,1024]{1,0:T(8,128)} %bitcast.46, bf16[1024,512]{1,0:T(8,128)(2,1)} %refs_8_.1), custom_call_target="tpu_custom_call" | custom-call | flops 100663296 | bytes 2424832 | tf_op jit(solution)/shard_map/latent_project/pallas_call | solution.py:710
  9.9 2.5 %collective-permute-start.2 = (bf16[96,512]{1,0:T(8,128)(2,1)}, bf16[96,512]{1,0:T(8,128)(2,1)S(1)}, u32[]{:S(2)}, u32[]{:S(2)}) collective-permute-start(bf16[96,512]{1,0:T(8,128)(2,1)} %get-tuple-element.114.refs_0_), channel_id=1, source_target_pairs={{0,3},{1,2},{2,1},{3,0},{4,7},{5,6},{6,5},{7,4},{8,11},{9,10},{10,... | collective-permute-start | bytes 294920 | tf_op jit(solution)/shard_map/ppermute | solution.py:655
  13.2 2.7 %collective-permute-done.2.refs_3_ = bf16[96,512]{1,0:T(8,128)(2,1)S(1)} collective-permute-done((bf16[96,512]{1,0:T(8,128)(2,1)}, bf16[96,512]{1,0:T(8,128)(2,1)S(1)}, u32[]{:S(2)}, u32[]{:S(2)}) %collective-permute-start.2) | collective-permute-done | bytes 98336 | tf_op jit(solution)/shard_map/ppermute | solution.py:655
  15.9 2.2 %collective-permute-done.1.refs_2_ = bf16[96,512]{1,0:T(8,128)(2,1)S(1)} collective-permute-done((bf16[96,512]{1,0:T(8,128)(2,1)}, bf16[96,512]{1,0:T(8,128)(2,1)S(1)}, u32[]{:S(2)}, u32[]{:S(2)}) %collective-permute-start.1) | collective-permute-done | bytes 98336 | tf_op jit(solution)/shard_map/ppermute | solution.py:655
  18.7 19.4 %project_attend.1 = (bf16[6,512,1024]{2,1,0:T(8,128)(2,1)}, bf16[6,512,512]{2,1,0:T(8,128)(2,1)}, bf16[6,512,512]{2,1,0:T(8,128)(2,1)}, bf16[96,512]{1,0:T(8,128...) custom-call(s32[7]{0:T(128)S(1)} %stack.24.scalars, ...), custom_call_target="tpu_custom_call" | custom-call | flops 8103395328 | bytes 37748736 | tf_op jit(solution)/shard_map/project_attend/pallas_call | solution.py:710
  38.3 2.3 %collective-permute-start.4 = (bf16[96,640]{1,0:T(8,128)(2,1)}, bf16[96,640]{1,0:T(8,128)(2,1)S(1)}, u32[]{:S(2)}, u32[]{:S(2)}) collective-permute-start(bf16[96,640]{1,0:T(8,128)(2,1)} %get-tuple-element.117), channel_id=1, source_target_pairs={{0,2},{1,3},{2,0},{3,1},{4,6},{5,7},{6,4},{7,5},{8,10},{9,11},{10,... | collective-permute-start | bytes 368648 | tf_op jit(solution)/shard_map/ppermute | solution.py:655
  40.7 5.9 %collective-permute-done.4.refs_2_ = bf16[96,640]{1,0:T(8,128)(2,1)S(1)} collective-permute-done((bf16[96,640]{1,0:T(8,128)(2,1)}, bf16[96,640]{1,0:T(8,128)(2,1)S(1)}, u32[]{:S(2)}, u32[]{:S(2)}) %collective-permute-start.4) | collective-permute-done | bytes 122912 | tf_op jit(solution)/shard_map/ppermute | solution.py:655
  46.6 2.5 %collective-permute-done.5.refs_3_ = bf16[96,640]{1,0:T(8,128)(2,1)S(1)} collective-permute-done((bf16[96,640]{1,0:T(8,128)(2,1)}, bf16[96,640]{1,0:T(8,128)(2,1)S(1)}, u32[]{:S(2)}, u32[]{:S(2)}) %collective-permute-start.5) | collective-permute-done | bytes 122912 | tf_op jit(solution)/shard_map/ppermute | solution.py:655
  49.0 16.4 %feed_forward.1 = (f32[96,1024]{1,0:T(8,128)}, f32[96,1024]{1,0:T(8,128)}, bf16[96,640]{1,0:T(8,128)(2,1)}, f32[2,1024]{1,0:T(2,128)}, bf16[4,128,1024]{2,1,0:T(8,128)(2,1)}, /*index=5*/bf16[96,1024]{1,0:T(8,128)(2,1)}) custom-call(s32[7]{0:T(128)S(1)} %stack.24.scalars, f32[96,1024]{1,0:T(8,128)} %bitcast.44, f32[96,1024]{1,0:T(8,128)} %bitcast.47, ...), custom_call_target="tpu_custom_call" | custom-call | flops 3221225472 | bytes 19136512 | tf_op jit(solution)/shard_map/feed_forward/pallas_call | solution.py:710
  65.9 5.4 %collective-permute-done.7.refs_6_.refs_10_ = bf16[96,640]{1,0:T(8,128)(2,1)S(1)} collective-permute-done((bf16[96,640]{1,0:T(8,128)(2,1)}, bf16[96,640]{1,0:T(8,128)(2,1)S(1)}, u32[]{:S(2)}, u32[]{:S(2)}) %collective-permute-start.7) | collective-permute-done | bytes 122912 | tf_op jit(solution)/shard_map/ppermute | solution.py:655
  72.6 15.9 %attend_back.2 = (bf16[2,256,3072]{2,1,0:T(8,128)(2,1)}, f32[8,3072]{1,0:T(8,128)}, bf16[96,256]{1,0:T(8,128)(2,1)}, bf16[96,256]{1,0:T(8,128)(2,1)}, bf16[1,2,5...) custom-call(s32[7]{0:T(128)S(1)} %stack.24.scalars, ...), custom_call_target="tpu_custom_call" | custom-call | flops 5297405952 | bytes 18874368 | tf_op jit(solution)/shard_map/attend_back/pallas_call | solution.py:710
  88.8 2.8 %all-gather.5.cloned.1.call-done.ff_all = bf16[768,1024]{1,0:T(8,128)(2,1)} async-done(((bf16[96,1024]{1,0:T(8,128)(2,1)}), bf16[768,1024]{1,0:T(8,128)(2,1)}) %all-gather.5.cloned.1.call-update) | async-done | bytes 1572880 | tf_op jit(solution)/shard_map/all_gather | solution.py:840
  91.6 11.2 %feed_forward_weights.1 = bf16[2,512,1024]{2,1,0:T(8,128)(2,1)} custom-call(s32[7]{0:T(128)S(1)} %stack.24.scalars, bf16[768,1024]{1,0:T(8,128)(2,1)} %all-gather.5.cloned.1.call-done.ff_all, bf16[768,2048]{1,0:T(8,128)(2,1)} %all-gather.3.cloned.1.call-done.refs_24_.out_all, bf16[1024,4096]{1,0:T(8,128)(2,1)} %refs_1_.2, bf16[4096,1024]{1,0:T(8,128)(2,1)} %down.3, ...), custom_call_target="tpu_custom_call" | custom-call | flops 4831838208 | bytes 9437184 | tf_op jit(solution)/shard_map/feed_forward_weights/pallas_call | solution.py:710
  104.7 16.3 %attend_back.3 = (bf16[2,256,3072]{2,1,0:T(8,128)(2,1)}, f32[8,3072]{1,0:T(8,128)}, bf16[96,256]{1,0:T(8,128)(2,1)}, bf16[96,256]{1,0:T(8,128)(2,1)}, bf16[1,2,5...) custom-call(s32[7]{0:T(128)S(1)} %stack.24.scalars, ...), custom_call_target="tpu_custom_call" | custom-call | flops 5297405952 | bytes 18874368 | tf_op jit(solution)/shard_map/attend_back/pallas_call | solution.py:710
  123.9 7.0 %patch_back.3._ = bf16[6,512,1024]{2,1,0:T(8,128)(2,1)} custom-call(s32[7]{0:T(128)S(1)} %stack.24.scalars, bf16[2,256,3072]{2,1,0:T(8,128)(2,1)} %get-tuple-element.132.kv_a, bf16[2,256,3072]{2,1,0:T(8,128)(2,1)} %get-tuple-element.145.kv_b, f32[8,3072]{1,0:T(8,128)} %get-tuple-element.146.stat_a, f32[8,3072]{1,0:T(8,128)} %get-tuple-element.147.stat_b, ...), custom_call_target="tpu_custom_call" | custom-call | flops 2147483648 | bytes 8388608 | tf_op jit(solution)/shard_map/patch_back/pallas_call | solution.py:710
  132.3 4.8 %latent_back.1 = (f32[96,1024]{1,0:T(8,128)}, f32[16,1024]{1,0:T(8,128)}) custom-call(s32[7]{0:T(128)S(1)} %stack.24.scalars, f32[96,1024]{1,0:T(8,128)} %bitcast.45, f32[1,1024]{1,0:T(1,128)} %bitcast.60, f32[96,1024]{1,0:T(8,128)} %get-tuple-element.170.mid_grad, f32[8,1024]{1,0:T(8,128)} %get-tuple-element.171.media_small, ...), custom_call_target="tpu_custom_call" | custom-call | flops 301989888 | bytes 5111808 | tf_op jit(solution)/shard_map/latent_back/pallas_call | solution.py:710
  139.0 7.0 %patch_back.4._ = bf16[6,512,1024]{2,1,0:T(8,128)(2,1)} custom-call(s32[7]{0:T(128)S(1)} %stack.24.scalars, bf16[2,256,3072]{2,1,0:T(8,128)(2,1)} %get-tuple-element.132.kv_a, bf16[2,256,3072]{2,1,0:T(8,128)(2,1)} %get-tuple-element.145.kv_b, f32[8,3072]{1,0:T(8,128)} %get-tuple-element.146.stat_a, ...), custom_call_target="tpu_custom_call", output_to_operand_aliasing={{}: (13, {})} | custom-call | flops 2147483648 | bytes 8388608 | tf_op jit(solution)/shard_map/patch_back/pallas_call | solution.py:710
  147.7 4.0 %all-to-all-start = ((bf16[512,4,128]{2,0,1:T(8,128)(2,1)}), bf16[512,4,128]{2,0,1:T(8,128)(2,1)S(1)}, u32[]{:S(2)}, u32[]{:S(2)}) async-start(bf16[512,4,128]{2,0,1:T(8,128)(2,1)} %copy_bitcast_fusion), calls=%async_computation.1 | async-start | bytes 1048576 | tf_op jit(solution)/shard_map/all_to_all | solution.py:1121
  153.0 1.6 fusion.3
  156.5 1.6 fusion.2
  158.9 7.0 %patch_back.5 = bf16[6,512,1024]{2,1,0:T(8,128)(2,1)} custom-call(s32[7]{0:T(128)S(1)} %stack.24.scalars, bf16[2,256,3072]{2,1,0:T(8,128)(2,1)} %get-tuple-element.132.kv_a, bf16[2,256,3072]{2,1,0:T(8,128)(2,1)} %get-tuple-element.145.kv_b, f32[8,3072]{1,0:T(8,128)} %get-tuple-element.146.stat_a, ...), custom_call_target="tpu_custom_call", output_to_operand_aliasing={{}: (13, {})} | custom-call | flops 2147483648 | bytes 8388608 | tf_op jit(solution)/shard_map/patch_back/pallas_call | solution.py:710
  166.9 2.9 %collective-permute-start.27 = (f32[16,1024]{1,0:T(8,128)S(1)}, f32[16,1024]{1,0:T(8,128)S(1)}, u32[]{:S(2)}, u32[]{:S(2)}) collective-permute-start(f32[16,1024]{1,0:T(8,128)S(1)} %add.51), channel_id=1, source_target_pairs={{0,24},{8,16},{16,8},{24,0},{1,25},{9,17},{17,9},{25,1},{2,26},{10... | collective-permute-start | bytes 196616 | tf_op jit(solution)/shard_map/ppermute | solution.py:661
  171.3 2.6 %finish_weights.1 = (f32[128,128]{1,0:T(8,128)}, f32[128,128]{1,0:T(8,128)}, f32[128,128]{1,0:T(8,128)}, f32[64,256]{1,0:T(8,128)}, f32[128,1024]{1,0:T(8,128)}, /*index=5*/f32[512,256]{1,0:T(8,128)}) custom-call(s32[7]{0:T(128)S(1)} %stack.24.scalars, bf16[512,128]{1,0:T(8,128)(2,1)} %get-tuple-element.210.up_keep, ...), custom_call_target="tpu_custom_call" | custom-call | bytes 1048576 | tf_op jit(solution)/shard_map/finish_weights/pallas_call | solution.py:710
  173.9 1.6 collective-permute-done.26
  (77 shorter events, 21.0 us)
Async XLA Ops:
  7.2 58.2 %all-gather.3.cloned.1.call-start = ((), (), s32[]{:S(2)}) async-start(), calls=%async_computation.2 | async-start | bytes 3538944 | tf_op jit(solution)/shard_map/all_gather | solution.py:725
  9.9 81.7 %all-gather.5.cloned.1.call-start = ((), (), s32[]{:S(2)}) async-start(), calls=%async_computation.3 | async-start | bytes 1769472 | tf_op jit(solution)/shard_map/all_gather | solution.py:840
  9.9 6.0 %collective-permute-start.2 = (bf16[96,512]{1,0:T(8,128)(2,1)}, bf16[96,512]{1,0:T(8,128)(2,1)S(1)}, u32[]{:S(2)}, u32[]{:S(2)}) collective-permute-start(bf16[96,512]{1,0:T(8,128)(2,1)} %get-tuple-element.114.refs_0_), channel_id=1, source_target_pairs={{0,3},{1,2},{2,1},{3,0},{4,7},{5,6},{6,5},{7,4},{8,11},{9,10},{10,... | collective-permute-start | bytes 294920 | tf_op jit(solution)/shard_map/ppermute | solution.py:655
  38.3 8.3 %collective-permute-start.4 = (bf16[96,640]{1,0:T(8,128)(2,1)}, bf16[96,640]{1,0:T(8,128)(2,1)S(1)}, u32[]{:S(2)}, u32[]{:S(2)}) collective-permute-start(bf16[96,640]{1,0:T(8,128)(2,1)} %get-tuple-element.117), channel_id=1, source_target_pairs={{0,2},{1,3},{2,0},{3,1},{4,6},{5,7},{6,4},{7,5},{8,10},{9,11},{10,... | collective-permute-start | bytes 368648 | tf_op jit(solution)/shard_map/ppermute | solution.py:655
  40.6 8.4 %collective-permute-start.5 = (bf16[96,640]{1,0:T(8,128)(2,1)}, bf16[96,640]{1,0:T(8,128)(2,1)S(1)}, u32[]{:S(2)}, u32[]{:S(2)}) collective-permute-start(bf16[96,640]{1,0:T(8,128)(2,1)} %get-tuple-element.118), channel_id=1, source_target_pairs={{0,3},{1,2},{2,1},{3,0},{4,7},{5,6},{6,5},{7,4},{8,11},{9,10},{10,... | collective-permute-start | bytes 368648 | tf_op jit(solution)/shard_map/ppermute | solution.py:655
  65.4 81.4 %reduce-scatter.2.cloned.1.call-start = ((), (), s32[]{:S(2)}) async-start(), calls=%async_computation.4 | async-start | bytes 2621440 | tf_op jit(solution)/shard_map/reduce_scatter | solution.py:1002
  88.6 14.3 %collective-permute-start.9 = (bf16[1,2,512,512]{3,2,1,0:T(8,128)(2,1)}, bf16[1,2,512,512]{3,2,1,0:T(8,128)(2,1)S(1)}, u32[]{:S(2)}, u32[]{:S(2)}) collective-permute-start(bf16[1,2,512,512]{3,2,1,0:T(8,128)(2,1)} %get-tuple-element.136), channel_id=1, source_target_pairs={{0,1},{1,0},{2,3},{3,2},{4,5},{5,4},{6,7},{7,6},{8,9},{9,8},{10,11... | collective-permute-start | bytes 3145736 | tf_op jit(solution)/shard_map/ppermute | solution.py:655
  103.2 17.8 %collective-permute-start.10 = (bf16[1,512,512]{2,1,0:T(8,128)(2,1)S(1)}, bf16[1,512,512]{2,1,0:T(8,128)(2,1)S(1)}, u32[]{:S(2)}, u32[]{:S(2)}) collective-permute-start(bf16[1,512,512]{2,1,0:T(8,128)(2,1)S(1)} %slice_bitcast_fusion.1), channel_id=1, source_target_pairs={{0,4},{4,0},{1,5},{5,1},{2,6},{6,2},{3,7},{7,3},{8,12},{12,8},{9,1... | collective-permute-start | bytes 1572872 | tf_op jit(solution)/shard_map/ppermute | solution.py:658
  121.2 9.7 %collective-permute-start.11 = (bf16[1,2,512,512]{3,2,1,0:T(8,128)(2,1)}, bf16[1,2,512,512]{3,2,1,0:T(8,128)(2,1)S(1)}, u32[]{:S(2)}, u32[]{:S(2)}) collective-permute-start(bf16[1,2,512,512]{3,2,1,0:T(8,128)(2,1)} %get-tuple-element.162), channel_id=1, source_target_pairs={{0,1},{1,0},{2,3},{3,2},{4,5},{5,4},{6,7},{7,6},{8,9},{9,8},{10,11... | collective-permute-start | bytes 3145736 | tf_op jit(solution)/shard_map/ppermute | solution.py:655
  121.3 9.5 %collective-permute-start.12 = (bf16[96,512]{1,0:T(8,128)(2,1)}, bf16[96,512]{1,0:T(8,128)(2,1)S(1)}, u32[]{:S(2)}, u32[]{:S(2)}) collective-permute-start(bf16[96,512]{1,0:T(8,128)(2,1)} %get-tuple-element.164), channel_id=1, source_target_pairs={{0,1},{1,0},{2,3},{3,2},{4,5},{5,4},{6,7},{7,6},{8,9},{9,8},{10,11... | collective-permute-start | bytes 294920 | tf_op jit(solution)/shard_map/ppermute | solution.py:655
  121.8 9.1 %collective-permute-start.13 = (bf16[96,512]{1,0:T(8,128)(2,1)}, bf16[96,512]{1,0:T(8,128)(2,1)S(1)}, u32[]{:S(2)}, u32[]{:S(2)}) collective-permute-start(bf16[96,512]{1,0:T(8,128)(2,1)} %get-tuple-element.165), channel_id=1, source_target_pairs={{0,2},{1,3},{2,0},{3,1},{4,6},{5,7},{6,4},{7,5},{8,10},{9,11},{10,... | collective-permute-start | bytes 294920 | tf_op jit(solution)/shard_map/ppermute | solution.py:655
  122.4 8.4 %collective-permute-start.14 = (bf16[96,512]{1,0:T(8,128)(2,1)}, bf16[96,512]{1,0:T(8,128)(2,1)S(1)}, u32[]{:S(2)}, u32[]{:S(2)}) collective-permute-start(bf16[96,512]{1,0:T(8,128)(2,1)} %get-tuple-element.166), channel_id=1, source_target_pairs={{0,3},{1,2},{2,1},{3,0},{4,7},{5,6},{6,5},{7,4},{8,11},{9,10},{10,... | collective-permute-start | bytes 294920 | tf_op jit(solution)/shard_map/ppermute | solution.py:655
  123.2 22.9 %collective-permute-start.19 = (bf16[512,512]{1,0:T(8,128)(2,1)S(1)}, bf16[512,512]{1,0:T(8,128)(2,1)S(1)}, u32[]{:S(2)}, u32[]{:S(2)}) collective-permute-start(bf16[512,512]{1,0:T(8,128)(2,1)S(1)} %bitcast.48), channel_id=1, source_target_pairs={{0,2},{1,3},{2,0},{3,1},{4,6},{5,7},{6,4},{7,5},{8,10},{9,11},{10,... | collective-permute-start | bytes 1572872 | tf_op jit(solution)/shard_map/ppermute | solution.py:655
  131.2 14.9 %collective-permute-start.18 = (bf16[512,512]{1,0:T(8,128)(2,1)S(1)}, bf16[512,512]{1,0:T(8,128)(2,1)S(1)}, u32[]{:S(2)}, u32[]{:S(2)}) collective-permute-start(bf16[512,512]{1,0:T(8,128)(2,1)S(1)} %slice_bitcast_fusion), channel_id=1, source_target_pairs={{0,4},{4,0},{1,5},{5,1},{2,6},{6,2},{3,7},{7,3},{8,12},{12,8},{9,1... | collective-permute-start | bytes 1572872 | tf_op jit(solution)/shard_map/ppermute | solution.py:658
  137.1 8.9 %collective-permute-start.17 = (f32[16,1024]{1,0:T(8,128)}, f32[16,1024]{1,0:T(8,128)S(1)}, u32[]{:S(2)}, u32[]{:S(2)}) collective-permute-start(f32[16,1024]{1,0:T(8,128)} %get-tuple-element.184), channel_id=1, source_target_pairs={{0,3},{1,2},{2,1},{3,0},{4,7},{5,6},{6,5},{7,4},{8,11},{9,10},{10,... | collective-permute-start | bytes 196616 | tf_op jit(solution)/shard_map/ppermute | solution.py:655
  137.9 8.1 %collective-permute-start.16 = (f32[16,1024]{1,0:T(8,128)}, f32[16,1024]{1,0:T(8,128)S(1)}, u32[]{:S(2)}, u32[]{:S(2)}) collective-permute-start(f32[16,1024]{1,0:T(8,128)} %get-tuple-element.184), channel_id=1, source_target_pairs={{0,2},{1,3},{2,0},{3,1},{4,6},{5,7},{6,4},{7,5},{8,10},{9,11},{10,... | collective-permute-start | bytes 196616 | tf_op jit(solution)/shard_map/ppermute | solution.py:655
  138.9 7.1 %collective-permute-start.15 = (f32[16,1024]{1,0:T(8,128)}, f32[16,1024]{1,0:T(8,128)S(1)}, u32[]{:S(2)}, u32[]{:S(2)}) collective-permute-start(f32[16,1024]{1,0:T(8,128)} %get-tuple-element.184), channel_id=1, source_target_pairs={{0,1},{1,0},{2,3},{3,2},{4,5},{5,4},{6,7},{7,6},{8,9},{9,8},{10,11... | collective-permute-start | bytes 196616 | tf_op jit(solution)/shard_map/ppermute | solution.py:655
  147.7 19.2 %all-to-all-start = ((bf16[512,4,128]{2,0,1:T(8,128)(2,1)}), bf16[512,4,128]{2,0,1:T(8,128)(2,1)S(1)}, u32[]{:S(2)}, u32[]{:S(2)}) async-start(bf16[512,4,128]{2,0,1:T(8,128)(2,1)} %copy_bitcast_fusion), calls=%async_computation.1 | async-start | bytes 1048576 | tf_op jit(solution)/shard_map/all_to_all | solution.py:1121
  151.8 14.1 %collective-permute-start.20 = (f32[16,1024]{1,0:T(8,128)S(1)}, f32[16,1024]{1,0:T(8,128)S(1)}, u32[]{:S(2)}, u32[]{:S(2)}) collective-permute-start(f32[16,1024]{1,0:T(8,128)S(1)} %add_add_fusion.1), channel_id=1, source_target_pairs={{0,4},{4,0},{1,5},{5,1},{2,6},{6,2},{3,7},{7,3},{8,12},{12,8},{9,1... | collective-permute-start | bytes 196616 | tf_op jit(solution)/shard_map/ppermute | solution.py:658
  154.6 11.3 %collective-permute-start.24 = (bf16[128,256]{1,0:T(8,128)(2,1)S(1)}, bf16[128,256]{1,0:T(8,128)(2,1)S(1)}, u32[]{:S(2)}, u32[]{:S(2)}) collective-permute-start(bf16[128,256]{1,0:T(8,128)(2,1)S(1)} %get-tuple-element.212), channel_id=1, source_target_pairs={{0,3},{1,2},{2,1},{3,0},{4,7},{5,6},{6,5},{7,4},{8,11},{9,10},{10,... | collective-permute-start | bytes 196616 | tf_op jit(solution)/shard_map/ppermute | solution.py:655
  155.3 10.6 %collective-permute-start.23 = (bf16[128,256]{1,0:T(8,128)(2,1)S(1)}, bf16[128,256]{1,0:T(8,128)(2,1)S(1)}, u32[]{:S(2)}, u32[]{:S(2)}) collective-permute-start(bf16[128,256]{1,0:T(8,128)(2,1)S(1)} %get-tuple-element.213), channel_id=1, source_target_pairs={{0,2},{1,3},{2,0},{3,1},{4,6},{5,7},{6,4},{7,5},{8,10},{9,11},{10,... | collective-permute-start | bytes 196616 | tf_op jit(solution)/shard_map/ppermute | solution.py:655
  156.1 9.8 %collective-permute-start.22 = (bf16[128,256]{1,0:T(8,128)(2,1)S(1)}, bf16[128,256]{1,0:T(8,128)(2,1)S(1)}, u32[]{:S(2)}, u32[]{:S(2)}) collective-permute-start(bf16[128,256]{1,0:T(8,128)(2,1)S(1)} %get-tuple-element.214), channel_id=1, source_target_pairs={{0,1},{1,0},{2,3},{3,2},{4,5},{5,4},{6,7},{7,6},{8,9},{9,8},{10,11... | collective-permute-start | bytes 196616 | tf_op jit(solution)/shard_map/ppermute | solution.py:655
  158.1 7.8 %collective-permute-start.21 = (bf16[512,128]{1,0:T(8,128)(2,1)S(1)}, bf16[512,128]{1,0:T(8,128)(2,1)S(1)}, u32[]{:S(2)}, u32[]{:S(2)}) collective-permute-start(bf16[512,128]{1,0:T(8,128)(2,1)S(1)} %get-tuple-element.211), channel_id=1, source_target_pairs={{0,4},{4,0},{1,5},{5,1},{2,6},{6,2},{3,7},{7,3},{8,12},{12,8},{9,1... | collective-permute-start | bytes 393224 | tf_op jit(solution)/shard_map/ppermute | solution.py:658
  166.9 7.0 %collective-permute-start.27 = (f32[16,1024]{1,0:T(8,128)S(1)}, f32[16,1024]{1,0:T(8,128)S(1)}, u32[]{:S(2)}, u32[]{:S(2)}) collective-permute-start(f32[16,1024]{1,0:T(8,128)S(1)} %add.51), channel_id=1, source_target_pairs={{0,24},{8,16},{16,8},{24,0},{1,25},{9,17},{17,9},{25,1},{2,26},{10... | collective-permute-start | bytes 196616 | tf_op jit(solution)/shard_map/ppermute | solution.py:661
  (12 other events, 64.9 us)
Sparse Core Ops, SparseCore 0:
  10.5 36.9 all-gather.2
  65.6 26.0 all-gather.4
  103.0 43.8 reduce-scatter.1

commit v6 on v5

--- a/solution.py
+++ b/solution.py
@@ -1133,7 +1133,8 @@
             "finish_weights",
             (1,),
             [whole((units, each))] * 2
-            + [whole((share, cols))] * n_keys
+            + [pl.BlockSpec((share, cols), lambda i, *_: (units // share, 0))]
+            + [whole((share, cols))] * (n_keys - 1)
             + [whole(parts.shape)],
             [whole((each, width))] * 3
             + [
@@ -1149,7 +1150,7 @@
             ],
             cost(0, 16 * width * each + 12 * units * each),
             free=(1,) + tuple(range(3, 3 + n_keys)),
-        )(scalars, up_keep, up_got, *downs, parts)
+        )(scalars, ff_sum, up_got, ff_sum, *downs[1:], parts)
     else:
         total = jnp.sum(parts.reshape(n_far, -1, each).astype(f32), 0)
         q_grad, k_grad, v_grad = (total[i * width : (i + 1) * width].T for i in range(3))

time: 184 us -> 183 us (level)
  no operation moved by 1% of the time
where the time goes in v6:
time: 183 us
  Pallas kernels  110 us (60%)
  waiting for transfers between devices  26.6 us (15%)
  starting transfers between devices  26 us (14%)
  between operations  14 us (8%)
  local copies, waits for them, and re-layouts  4.77 us (3%)
    pallas_call x11, Pallas kernels, pinned(): return run(*args)  110 us
    ppermute x21, waiting for transfers between devices, over_keys(): return lax.ppermute(value, 'keys', [(i, i ^ shift) for i in range(n_keys)])  20 us
    ppermute x21, starting transfers between devices, over_keys(): return lax.ppermute(value, 'keys', [(i, i ^ shift) for i in range(n_keys)])  12.6 us
    ppermute x4, starting transfers between devices, over_near(): return lax.ppermute(value, 'near', [(0, 1), (1, 0)])  4.64 us
    ppermute x3, starting transfers between devices, over_far(): return lax.ppermute(value, 'far', [(i, i ^ shift) for i in range(n_far)])  4.39 us
    all_to_all x1, starting transfers between devices, shards(): lax.all_to_all(total, 'far', split_axis=1, concat_axis=0, tiled=True)  4.04 us
  transfers between devices with their start and end apart: 32, of which 10 were waited for; matrix products, arithmetic and copies ran while one was open for 2% of the time, Pallas kernels for 59%

profile of v6, /device:TPU:0, one launch (start us, length us, event | category | flops | bytes accessed | tf_op | source)
XLA Modules:
  0.0 182.6 jit_solution(4402020804138212405)
XLA Ops:
  7.2 2.6 %latent_project.1 = (bf16[96,2048]{1,0:T(8,128)(2,1)}, bf16[96,512]{1,0:T(8,128)(2,1)}) custom-call(f32[96,1024]{1,0:T(8,128)} %bitcast.43, f32[1,1024]{1,0:T(1,128)} %bitcast.59, f32[1,1024]{1,0:T(1,128)} %bitcast.61, f32[96,1024]{1,0:T(8,128)} %bitcast.46, bf16[1024,512]{1,0:T(8,128)(2,1)} %refs_8_.1), custom_call_target="tpu_custom_call" | custom-call | flops 100663296 | bytes 2424832 | tf_op jit(solution)/shard_map/latent_project/pallas_call | solution.py:710
  9.9 2.5 %collective-permute-start.2 = (bf16[96,512]{1,0:T(8,128)(2,1)}, bf16[96,512]{1,0:T(8,128)(2,1)S(1)}, u32[]{:S(2)}, u32[]{:S(2)}) collective-permute-start(bf16[96,512]{1,0:T(8,128)(2,1)} %get-tuple-element.113.refs_0_), channel_id=1, source_target_pairs={{0,3},{1,2},{2,1},{3,0},{4,7},{5,6},{6,5},{7,4},{8,11},{9,10},{10,... | collective-permute-start | bytes 294920 | tf_op jit(solution)/shard_map/ppermute | solution.py:655
  13.2 2.7 %collective-permute-done.2.refs_3_ = bf16[96,512]{1,0:T(8,128)(2,1)S(1)} collective-permute-done((bf16[96,512]{1,0:T(8,128)(2,1)}, bf16[96,512]{1,0:T(8,128)(2,1)S(1)}, u32[]{:S(2)}, u32[]{:S(2)}) %collective-permute-start.2) | collective-permute-done | bytes 98336 | tf_op jit(solution)/shard_map/ppermute | solution.py:655
  15.9 2.2 %collective-permute-done.1.refs_2_ = bf16[96,512]{1,0:T(8,128)(2,1)S(1)} collective-permute-done((bf16[96,512]{1,0:T(8,128)(2,1)}, bf16[96,512]{1,0:T(8,128)(2,1)S(1)}, u32[]{:S(2)}, u32[]{:S(2)}) %collective-permute-start.1) | collective-permute-done | bytes 98336 | tf_op jit(solution)/shard_map/ppermute | solution.py:655
  18.7 19.4 %project_attend.1 = (bf16[6,512,1024]{2,1,0:T(8,128)(2,1)}, bf16[6,512,512]{2,1,0:T(8,128)(2,1)}, bf16[6,512,512]{2,1,0:T(8,128)(2,1)}, bf16[96,512]{1,0:T(8,128...) custom-call(s32[7]{0:T(128)S(1)} %stack.24.scalars, ...), custom_call_target="tpu_custom_call" | custom-call | flops 8103395328 | bytes 37748736 | tf_op jit(solution)/shard_map/project_attend/pallas_call | solution.py:710
  38.3 2.3 %collective-permute-start.4 = (bf16[96,640]{1,0:T(8,128)(2,1)}, bf16[96,640]{1,0:T(8,128)(2,1)S(1)}, u32[]{:S(2)}, u32[]{:S(2)}) collective-permute-start(bf16[96,640]{1,0:T(8,128)(2,1)} %get-tuple-element.116), channel_id=1, source_target_pairs={{0,2},{1,3},{2,0},{3,1},{4,6},{5,7},{6,4},{7,5},{8,10},{9,11},{10,... | collective-permute-start | bytes 368648 | tf_op jit(solution)/shard_map/ppermute | solution.py:655
  40.7 5.9 %collective-permute-done.4.refs_2_ = bf16[96,640]{1,0:T(8,128)(2,1)S(1)} collective-permute-done((bf16[96,640]{1,0:T(8,128)(2,1)}, bf16[96,640]{1,0:T(8,128)(2,1)S(1)}, u32[]{:S(2)}, u32[]{:S(2)}) %collective-permute-start.4) | collective-permute-done | bytes 122912 | tf_op jit(solution)/shard_map/ppermute | solution.py:655
  46.6 2.5 %collective-permute-done.5.refs_3_ = bf16[96,640]{1,0:T(8,128)(2,1)S(1)} collective-permute-done((bf16[96,640]{1,0:T(8,128)(2,1)}, bf16[96,640]{1,0:T(8,128)(2,1)S(1)}, u32[]{:S(2)}, u32[]{:S(2)}) %collective-permute-start.5) | collective-permute-done | bytes 122912 | tf_op jit(solution)/shard_map/ppermute | solution.py:655
  49.0 16.4 %feed_forward.1 = (f32[96,1024]{1,0:T(8,128)}, f32[96,1024]{1,0:T(8,128)}, bf16[96,640]{1,0:T(8,128)(2,1)}, f32[2,1024]{1,0:T(2,128)}, bf16[4,128,1024]{2,1,0:T(8,128)(2,1)}, /*index=5*/bf16[96,1024]{1,0:T(8,128)(2,1)}) custom-call(s32[7]{0:T(128)S(1)} %stack.24.scalars, f32[96,1024]{1,0:T(8,128)} %bitcast.44, f32[96,1024]{1,0:T(8,128)} %bitcast.47, ...), custom_call_target="tpu_custom_call" | custom-call | flops 3221225472 | bytes 19136512 | tf_op jit(solution)/shard_map/feed_forward/pallas_call | solution.py:710
  65.9 5.4 %collective-permute-done.7.refs_6_.refs_10_ = bf16[96,640]{1,0:T(8,128)(2,1)S(1)} collective-permute-done((bf16[96,640]{1,0:T(8,128)(2,1)}, bf16[96,640]{1,0:T(8,128)(2,1)S(1)}, u32[]{:S(2)}, u32[]{:S(2)}) %collective-permute-start.7) | collective-permute-done | bytes 122912 | tf_op jit(solution)/shard_map/ppermute | solution.py:655
  72.6 15.9 %attend_back.2 = (bf16[2,256,3072]{2,1,0:T(8,128)(2,1)}, f32[8,3072]{1,0:T(8,128)}, bf16[96,256]{1,0:T(8,128)(2,1)}, bf16[96,256]{1,0:T(8,128)(2,1)}, bf16[1,2,5...) custom-call(s32[7]{0:T(128)S(1)} %stack.24.scalars, ...), custom_call_target="tpu_custom_call" | custom-call | flops 5297405952 | bytes 18874368 | tf_op jit(solution)/shard_map/attend_back/pallas_call | solution.py:710
  88.8 2.8 %all-gather.5.cloned.1.call-done.ff_all = bf16[768,1024]{1,0:T(8,128)(2,1)} async-done(((bf16[96,1024]{1,0:T(8,128)(2,1)}), bf16[768,1024]{1,0:T(8,128)(2,1)}) %all-gather.5.cloned.1.call-update) | async-done | bytes 1572880 | tf_op jit(solution)/shard_map/all_gather | solution.py:840
  91.6 11.2 %feed_forward_weights.1 = bf16[2,512,1024]{2,1,0:T(8,128)(2,1)} custom-call(s32[7]{0:T(128)S(1)} %stack.24.scalars, bf16[768,1024]{1,0:T(8,128)(2,1)} %all-gather.5.cloned.1.call-done.ff_all, bf16[768,2048]{1,0:T(8,128)(2,1)} %all-gather.3.cloned.1.call-done.refs_24_.out_all, bf16[1024,4096]{1,0:T(8,128)(2,1)} %refs_1_.2, bf16[4096,1024]{1,0:T(8,128)(2,1)} %down.3, ...), custom_call_target="tpu_custom_call" | custom-call | flops 4831838208 | bytes 9437184 | tf_op jit(solution)/shard_map/feed_forward_weights/pallas_call | solution.py:710
  103.2 1.5 collective-permute-start.10
  104.7 16.3 %attend_back.3 = (bf16[2,256,3072]{2,1,0:T(8,128)(2,1)}, f32[8,3072]{1,0:T(8,128)}, bf16[96,256]{1,0:T(8,128)(2,1)}, bf16[96,256]{1,0:T(8,128)(2,1)}, bf16[1,2,5...) custom-call(s32[7]{0:T(128)S(1)} %stack.24.scalars, ...), custom_call_target="tpu_custom_call" | custom-call | flops 5297405952 | bytes 18874368 | tf_op jit(solution)/shard_map/attend_back/pallas_call | solution.py:710
  123.9 7.0 %patch_back.3._ = bf16[6,512,1024]{2,1,0:T(8,128)(2,1)} custom-call(s32[7]{0:T(128)S(1)} %stack.24.scalars, bf16[2,256,3072]{2,1,0:T(8,128)(2,1)} %get-tuple-element.131.kv_a, bf16[2,256,3072]{2,1,0:T(8,128)(2,1)} %get-tuple-element.144.kv_b, f32[8,3072]{1,0:T(8,128)} %get-tuple-element.145.stat_a, f32[8,3072]{1,0:T(8,128)} %get-tuple-element.146.stat_b, ...), custom_call_target="tpu_custom_call" | custom-call | flops 2147483648 | bytes 8388608 | tf_op jit(solution)/shard_map/patch_back/pallas_call | solution.py:710
  132.3 4.8 %latent_back.1 = (f32[96,1024]{1,0:T(8,128)}, f32[16,1024]{1,0:T(8,128)}) custom-call(s32[7]{0:T(128)S(1)} %stack.24.scalars, f32[96,1024]{1,0:T(8,128)} %bitcast.45, f32[1,1024]{1,0:T(1,128)} %bitcast.60, f32[96,1024]{1,0:T(8,128)} %get-tuple-element.169.mid_grad, f32[8,1024]{1,0:T(8,128)} %get-tuple-element.170.media_small, ...), custom_call_target="tpu_custom_call" | custom-call | flops 301989888 | bytes 5111808 | tf_op jit(solution)/shard_map/latent_back/pallas_call | solution.py:710
  139.0 7.0 %patch_back.4._ = bf16[6,512,1024]{2,1,0:T(8,128)(2,1)} custom-call(s32[7]{0:T(128)S(1)} %stack.24.scalars, bf16[2,256,3072]{2,1,0:T(8,128)(2,1)} %get-tuple-element.131.kv_a, bf16[2,256,3072]{2,1,0:T(8,128)(2,1)} %get-tuple-element.144.kv_b, f32[8,3072]{1,0:T(8,128)} %get-tuple-element.145.stat_a, ...), custom_call_target="tpu_custom_call", output_to_operand_aliasing={{}: (13, {})} | custom-call | flops 2147483648 | bytes 8388608 | tf_op jit(solution)/shard_map/patch_back/pallas_call | solution.py:710
  147.7 4.0 %all-to-all-start = ((bf16[512,4,128]{2,0,1:T(8,128)(2,1)}), bf16[512,4,128]{2,0,1:T(8,128)(2,1)S(1)}, u32[]{:S(2)}, u32[]{:S(2)}) async-start(bf16[512,4,128]{2,0,1:T(8,128)(2,1)} %copy_bitcast_fusion), calls=%async_computation.1 | async-start | bytes 1048576 | tf_op jit(solution)/shard_map/all_to_all | solution.py:1121
  157.6 7.0 %patch_back.5 = bf16[6,512,1024]{2,1,0:T(8,128)(2,1)} custom-call(s32[7]{0:T(128)S(1)} %stack.24.scalars, bf16[2,256,3072]{2,1,0:T(8,128)(2,1)} %get-tuple-element.131.kv_a, bf16[2,256,3072]{2,1,0:T(8,128)(2,1)} %get-tuple-element.144.kv_b, f32[8,3072]{1,0:T(8,128)} %get-tuple-element.145.stat_a, ...), custom_call_target="tpu_custom_call", output_to_operand_aliasing={{}: (13, {})} | custom-call | flops 2147483648 | bytes 8388608 | tf_op jit(solution)/shard_map/patch_back/pallas_call | solution.py:710
  164.7 2.2 %all-to-all-done = bf16[512,4,128]{2,0,1:T(8,128)(2,1)S(1)} async-done(((bf16[512,4,128]{2,0,1:T(8,128)(2,1)}), bf16[512,4,128]{2,0,1:T(8,128)(2,1)S(1)}, u32[]{:S(2)}, u32[]{:S(2)}) %all-to-all-start) | async-done | bytes 524320 | tf_op jit(solution)/shard_map/all_to_all | solution.py:1121
  166.9 1.7 collective-permute-start.27
  168.6 2.7 %collective-permute-start.25 = (f32[16,1024]{1,0:T(8,128)S(1)}, f32[16,1024]{1,0:T(8,128)S(1)}, u32[]{:S(2)}, u32[]{:S(2)}) collective-permute-start(f32[16,1024]{1,0:T(8,128)S(1)} %add.51), channel_id=1, source_target_pairs={{0,8},{8,0},{16,24},{24,16},{1,9},{9,1},{17,25},{25,17},{2,10},{10... | collective-permute-start | bytes 196616 | tf_op jit(solution)/shard_map/ppermute | solution.py:661
  171.3 2.6 %finish_weights.1 = (f32[128,128]{1,0:T(8,128)}, f32[128,128]{1,0:T(8,128)}, f32[128,128]{1,0:T(8,128)}, f32[64,256]{1,0:T(8,128)}, f32[128,1024]{1,0:T(8,128)}, /*index=5*/f32[512,256]{1,0:T(8,128)}) custom-call(s32[7]{0:T(128)S(1)} %stack.24.scalars, bf16[1024,256]{1,0:T(8,128)(2,1)} %reduce-scatter.2.cloned.1.call-done.up_keep.refs_0_, ...), custom_call_target="tpu_custom_call" | custom-call | bytes 1048576 | tf_op jit(solution)/shard_map/finish_weights/pallas_call | solution.py:710
  (77 shorter events, 20.0 us)
Async XLA Ops:
  7.2 58.2 %all-gather.3.cloned.1.call-start = ((), (), s32[]{:S(2)}) async-start(), calls=%async_computation.2 | async-start | bytes 3538944 | tf_op jit(solution)/shard_map/all_gather | solution.py:725
  9.9 81.7 %all-gather.5.cloned.1.call-start = ((), (), s32[]{:S(2)}) async-start(), calls=%async_computation.3 | async-start | bytes 1769472 | tf_op jit(solution)/shard_map/all_gather | solution.py:840
  38.3 8.3 %collective-permute-start.4 = (bf16[96,640]{1,0:T(8,128)(2,1)}, bf16[96,640]{1,0:T(8,128)(2,1)S(1)}, u32[]{:S(2)}, u32[]{:S(2)}) collective-permute-start(bf16[96,640]{1,0:T(8,128)(2,1)} %get-tuple-element.116), channel_id=1, source_target_pairs={{0,2},{1,3},{2,0},{3,1},{4,6},{5,7},{6,4},{7,5},{8,10},{9,11},{10,... | collective-permute-start | bytes 368648 | tf_op jit(solution)/shard_map/ppermute | solution.py:655
  40.6 8.4 %collective-permute-start.5 = (bf16[96,640]{1,0:T(8,128)(2,1)}, bf16[96,640]{1,0:T(8,128)(2,1)S(1)}, u32[]{:S(2)}, u32[]{:S(2)}) collective-permute-start(bf16[96,640]{1,0:T(8,128)(2,1)} %get-tuple-element.117), channel_id=1, source_target_pairs={{0,3},{1,2},{2,1},{3,0},{4,7},{5,6},{6,5},{7,4},{8,11},{9,10},{10,... | collective-permute-start | bytes 368648 | tf_op jit(solution)/shard_map/ppermute | solution.py:655
  65.4 81.4 %reduce-scatter.2.cloned.1.call-start = ((), (), s32[]{:S(2)}) async-start(), calls=%async_computation.4 | async-start | bytes 2621440 | tf_op jit(solution)/shard_map/reduce_scatter | solution.py:1002
  88.6 14.3 %collective-permute-start.9 = (bf16[1,2,512,512]{3,2,1,0:T(8,128)(2,1)}, bf16[1,2,512,512]{3,2,1,0:T(8,128)(2,1)S(1)}, u32[]{:S(2)}, u32[]{:S(2)}) collective-permute-start(bf16[1,2,512,512]{3,2,1,0:T(8,128)(2,1)} %get-tuple-element.135), channel_id=1, source_target_pairs={{0,1},{1,0},{2,3},{3,2},{4,5},{5,4},{6,7},{7,6},{8,9},{9,8},{10,11... | collective-permute-start | bytes 3145736 | tf_op jit(solution)/shard_map/ppermute | solution.py:655
  103.2 17.8 %collective-permute-start.10 = (bf16[1,512,512]{2,1,0:T(8,128)(2,1)S(1)}, bf16[1,512,512]{2,1,0:T(8,128)(2,1)S(1)}, u32[]{:S(2)}, u32[]{:S(2)}) collective-permute-start(bf16[1,512,512]{2,1,0:T(8,128)(2,1)S(1)} %slice_bitcast_fusion.1), channel_id=1, source_target_pairs={{0,4},{4,0},{1,5},{5,1},{2,6},{6,2},{3,7},{7,3},{8,12},{12,8},{9,1... | collective-permute-start | bytes 1572872 | tf_op jit(solution)/shard_map/ppermute | solution.py:658
  121.2 9.7 %collective-permute-start.11 = (bf16[1,2,512,512]{3,2,1,0:T(8,128)(2,1)}, bf16[1,2,512,512]{3,2,1,0:T(8,128)(2,1)S(1)}, u32[]{:S(2)}, u32[]{:S(2)}) collective-permute-start(bf16[1,2,512,512]{3,2,1,0:T(8,128)(2,1)} %get-tuple-element.161), channel_id=1, source_target_pairs={{0,1},{1,0},{2,3},{3,2},{4,5},{5,4},{6,7},{7,6},{8,9},{9,8},{10,11... | collective-permute-start | bytes 3145736 | tf_op jit(solution)/shard_map/ppermute | solution.py:655
  121.3 9.6 %collective-permute-start.12 = (bf16[96,512]{1,0:T(8,128)(2,1)}, bf16[96,512]{1,0:T(8,128)(2,1)S(1)}, u32[]{:S(2)}, u32[]{:S(2)}) collective-permute-start(bf16[96,512]{1,0:T(8,128)(2,1)} %get-tuple-element.163), channel_id=1, source_target_pairs={{0,1},{1,0},{2,3},{3,2},{4,5},{5,4},{6,7},{7,6},{8,9},{9,8},{10,11... | collective-permute-start | bytes 294920 | tf_op jit(solution)/shard_map/ppermute | solution.py:655
  121.8 9.1 %collective-permute-start.13 = (bf16[96,512]{1,0:T(8,128)(2,1)}, bf16[96,512]{1,0:T(8,128)(2,1)S(1)}, u32[]{:S(2)}, u32[]{:S(2)}) collective-permute-start(bf16[96,512]{1,0:T(8,128)(2,1)} %get-tuple-element.164), channel_id=1, source_target_pairs={{0,2},{1,3},{2,0},{3,1},{4,6},{5,7},{6,4},{7,5},{8,10},{9,11},{10,... | collective-permute-start | bytes 294920 | tf_op jit(solution)/shard_map/ppermute | solution.py:655
  122.4 8.5 %collective-permute-start.14 = (bf16[96,512]{1,0:T(8,128)(2,1)}, bf16[96,512]{1,0:T(8,128)(2,1)S(1)}, u32[]{:S(2)}, u32[]{:S(2)}) collective-permute-start(bf16[96,512]{1,0:T(8,128)(2,1)} %get-tuple-element.165), channel_id=1, source_target_pairs={{0,3},{1,2},{2,1},{3,0},{4,7},{5,6},{6,5},{7,4},{8,11},{9,10},{10,... | collective-permute-start | bytes 294920 | tf_op jit(solution)/shard_map/ppermute | solution.py:655
  123.2 22.9 %collective-permute-start.19 = (bf16[512,512]{1,0:T(8,128)(2,1)S(1)}, bf16[512,512]{1,0:T(8,128)(2,1)S(1)}, u32[]{:S(2)}, u32[]{:S(2)}) collective-permute-start(bf16[512,512]{1,0:T(8,128)(2,1)S(1)} %bitcast.48), channel_id=1, source_target_pairs={{0,2},{1,3},{2,0},{3,1},{4,6},{5,7},{6,4},{7,5},{8,10},{9,11},{10,... | collective-permute-start | bytes 1572872 | tf_op jit(solution)/shard_map/ppermute | solution.py:655
  131.2 14.8 %collective-permute-start.18 = (bf16[512,512]{1,0:T(8,128)(2,1)S(1)}, bf16[512,512]{1,0:T(8,128)(2,1)S(1)}, u32[]{:S(2)}, u32[]{:S(2)}) collective-permute-start(bf16[512,512]{1,0:T(8,128)(2,1)S(1)} %slice_bitcast_fusion), channel_id=1, source_target_pairs={{0,4},{4,0},{1,5},{5,1},{2,6},{6,2},{3,7},{7,3},{8,12},{12,8},{9,1... | collective-permute-start | bytes 1572872 | tf_op jit(solution)/shard_map/ppermute | solution.py:658
  137.1 8.9 %collective-permute-start.17 = (f32[16,1024]{1,0:T(8,128)}, f32[16,1024]{1,0:T(8,128)S(1)}, u32[]{:S(2)}, u32[]{:S(2)}) collective-permute-start(f32[16,1024]{1,0:T(8,128)} %get-tuple-element.183), channel_id=1, source_target_pairs={{0,3},{1,2},{2,1},{3,0},{4,7},{5,6},{6,5},{7,4},{8,11},{9,10},{10,... | collective-permute-start | bytes 196616 | tf_op jit(solution)/shard_map/ppermute | solution.py:655
  137.9 8.1 %collective-permute-start.16 = (f32[16,1024]{1,0:T(8,128)}, f32[16,1024]{1,0:T(8,128)S(1)}, u32[]{:S(2)}, u32[]{:S(2)}) collective-permute-start(f32[16,1024]{1,0:T(8,128)} %get-tuple-element.183), channel_id=1, source_target_pairs={{0,2},{1,3},{2,0},{3,1},{4,6},{5,7},{6,4},{7,5},{8,10},{9,11},{10,... | collective-permute-start | bytes 196616 | tf_op jit(solution)/shard_map/ppermute | solution.py:655
  138.9 7.1 %collective-permute-start.15 = (f32[16,1024]{1,0:T(8,128)}, f32[16,1024]{1,0:T(8,128)S(1)}, u32[]{:S(2)}, u32[]{:S(2)}) collective-permute-start(f32[16,1024]{1,0:T(8,128)} %get-tuple-element.183), channel_id=1, source_target_pairs={{0,1},{1,0},{2,3},{3,2},{4,5},{5,4},{6,7},{7,6},{8,9},{9,8},{10,11... | collective-permute-start | bytes 196616 | tf_op jit(solution)/shard_map/ppermute | solution.py:655
  147.7 19.1 %all-to-all-start = ((bf16[512,4,128]{2,0,1:T(8,128)(2,1)}), bf16[512,4,128]{2,0,1:T(8,128)(2,1)S(1)}, u32[]{:S(2)}, u32[]{:S(2)}) async-start(bf16[512,4,128]{2,0,1:T(8,128)(2,1)} %copy_bitcast_fusion), calls=%async_computation.1 | async-start | bytes 1048576 | tf_op jit(solution)/shard_map/all_to_all | solution.py:1121
  151.8 12.8 %collective-permute-start.20 = (f32[16,1024]{1,0:T(8,128)S(1)}, f32[16,1024]{1,0:T(8,128)S(1)}, u32[]{:S(2)}, u32[]{:S(2)}) collective-permute-start(f32[16,1024]{1,0:T(8,128)S(1)} %add_add_fusion.1), channel_id=1, source_target_pairs={{0,4},{4,0},{1,5},{5,1},{2,6},{6,2},{3,7},{7,3},{8,12},{12,8},{9,1... | collective-permute-start | bytes 196616 | tf_op jit(solution)/shard_map/ppermute | solution.py:658
  153.9 10.7 %collective-permute-start.21 = (bf16[512,128]{1,0:T(8,128)(2,1)S(1)}, bf16[512,128]{1,0:T(8,128)(2,1)S(1)}, u32[]{:S(2)}, u32[]{:S(2)}) collective-permute-start(bf16[512,128]{1,0:T(8,128)(2,1)S(1)} %slice.60), channel_id=1, source_target_pairs={{0,4},{4,0},{1,5},{5,1},{2,6},{6,2},{3,7},{7,3},{8,12},{12,8},{9,1... | collective-permute-start | bytes 393224 | tf_op jit(solution)/shard_map/ppermute | solution.py:658
  155.7 8.9 %collective-permute-start.24 = (bf16[128,256]{1,0:T(8,128)(2,1)S(1)}, bf16[128,256]{1,0:T(8,128)(2,1)S(1)}, u32[]{:S(2)}, u32[]{:S(2)}) collective-permute-start(bf16[128,256]{1,0:T(8,128)(2,1)S(1)} %get-tuple-element.208), channel_id=1, source_target_pairs={{0,3},{1,2},{2,1},{3,0},{4,7},{5,6},{6,5},{7,4},{8,11},{9,10},{10,... | collective-permute-start | bytes 196616 | tf_op jit(solution)/shard_map/ppermute | solution.py:655
  155.9 8.7 %collective-permute-start.23 = (bf16[128,256]{1,0:T(8,128)(2,1)S(1)}, bf16[128,256]{1,0:T(8,128)(2,1)S(1)}, u32[]{:S(2)}, u32[]{:S(2)}) collective-permute-start(bf16[128,256]{1,0:T(8,128)(2,1)S(1)} %get-tuple-element.209), channel_id=1, source_target_pairs={{0,2},{1,3},{2,0},{3,1},{4,6},{5,7},{6,4},{7,5},{8,10},{9,11},{10,... | collective-permute-start | bytes 196616 | tf_op jit(solution)/shard_map/ppermute | solution.py:655
  157.1 7.6 %collective-permute-start.22 = (bf16[128,256]{1,0:T(8,128)(2,1)S(1)}, bf16[128,256]{1,0:T(8,128)(2,1)S(1)}, u32[]{:S(2)}, u32[]{:S(2)}) collective-permute-start(bf16[128,256]{1,0:T(8,128)(2,1)S(1)} %get-tuple-element.210), channel_id=1, source_target_pairs={{0,1},{1,0},{2,3},{3,2},{4,5},{5,4},{6,7},{7,6},{8,9},{9,8},{10,11... | collective-permute-start | bytes 196616 | tf_op jit(solution)/shard_map/ppermute | solution.py:655
  166.9 7.0 %collective-permute-start.27 = (f32[16,1024]{1,0:T(8,128)S(1)}, f32[16,1024]{1,0:T(8,128)S(1)}, u32[]{:S(2)}, u32[]{:S(2)}) collective-permute-start(f32[16,1024]{1,0:T(8,128)S(1)} %add.51), channel_id=1, source_target_pairs={{0,24},{8,16},{16,8},{24,0},{1,25},{9,17},{17,9},{25,1},{2,26},{10... | collective-permute-start | bytes 196616 | tf_op jit(solution)/shard_map/ppermute | solution.py:661
  168.6 6.2 %collective-permute-start.26 = (f32[16,1024]{1,0:T(8,128)S(1)}, f32[16,1024]{1,0:T(8,128)S(1)}, u32[]{:S(2)}, u32[]{:S(2)}) collective-permute-start(f32[16,1024]{1,0:T(8,128)S(1)} %add.51), channel_id=1, source_target_pairs={{0,16},{8,24},{16,0},{24,8},{1,17},{9,25},{17,1},{25,9},{2,18},{10... | collective-permute-start | bytes 196616 | tf_op jit(solution)/shard_map/ppermute | solution.py:661
  (12 other events, 65.7 us)
Sparse Core Ops, SparseCore 0:
  10.5 36.9 all-gather.2
  65.6 26.0 all-gather.4
  103.0 43.8 reduce-scatter.1
